TPU v7x, 32 devices: a whole 2x2x4 slice. The times are simulated.
32 devices in a mesh: harm: 8 (over y, x, core), mode: 4 (over z).
Axes of the slice: x: 2, y: 2, z: 4, core: 2. Of those that a mesh axis runs over, the one named last changes fastest.
Arguments:
- mode_vectors: float32 [49152, 1024], P('harm', 'mode'), may hold values from -0.09375 to 0.09375
- weights: float32 [49152, 1024], P('harm', 'mode'), may hold values from -0.1875 to 0.1875
- cotangent: float32 [49152, 1024], P('harm', 'mode'), may hold values from -6 to 6
- eigenvalues: float32 [1024], replicated, may hold values from 0 to 4
- eigen_cotangent: float32 [1024], replicated, may hold values from -6 to 6
- slab_rows: int32 [4096], replicated, may hold values from 0 to 49151, as said below
Outputs:
- slab: float32 [4096, 49152], P('mode', 'harm')
Inputs may be any that keep to these rules, and one draw needn't show every extreme that they name: `slab_rows`: each block of 6144 consecutive harmonics (0 to 6143, 6144 to 12287 and so on) holds exactly 512 of the slab rows.
All inputs are finite; a program needn't handle non-finite values.
Results may differ from a plain program's by a relative error of at most 0.0001.
Values sent between devices are 32-bit elements; how exact they have to be, the bound alone decides.
A program may use at most 128 MiB of HBM per device.

v0:
```python
import jax
import jax.numpy as jnp
from jax import lax
from jax.sharding import PartitionSpec as P

regular = 0.01
precision = lax.Precision.HIGHEST


def product(left, right, left_dim, right_dim):
    return lax.dot_general(
        left,
        right,
        (((left_dim,), (right_dim,)), ((), ())),
        precision=precision,
        preferred_element_type=jnp.float32,
    )


def weigh_gap(block, row_ids, col_ids, eigenvalues, eigen_cotangent):
    eigen_rows = lax.dynamic_slice_in_dim(eigenvalues, row_ids, block.shape[0])
    eigen_cols = lax.dynamic_slice_in_dim(eigenvalues, col_ids, block.shape[1])
    slope_cols = lax.dynamic_slice_in_dim(eigen_cotangent, col_ids, block.shape[1])
    differ = eigen_cols[None, :] - eigen_rows[:, None]
    factor = differ / (differ * differ + regular)
    rows = row_ids + lax.broadcasted_iota(jnp.int32, block.shape, 0)
    cols = col_ids + lax.broadcasted_iota(jnp.int32, block.shape, 1)
    return factor * block + jnp.where(rows == cols, slope_cols[None, :], 0.0)


def pick_rows(table, slab_rows, harm_index):
    row_count = table.shape[0]
    offset = slab_rows - harm_index * row_count
    inside = (offset >= 0) & (offset < row_count)
    picked = jnp.take(table, jnp.clip(offset, 0, row_count - 1), axis=0)
    return jnp.where(inside[:, None], picked, 0.0)


def gather_weights(weights, slab_rows, harm_index, harm_count, mode_count):
    width = weights.shape[1]
    with jax.named_scope("pick"):
        picked = pick_rows(weights, slab_rows, harm_index)
    piece = slab_rows.shape[0] // (harm_count * mode_count)
    picked = picked.reshape(mode_count, harm_count, piece, width)
    with jax.named_scope("sum_weights"):
        picked = lax.psum_scatter(picked, "harm", scatter_dimension=1, tiled=True)
    picked = picked.reshape(mode_count, piece, width)
    with jax.named_scope("swap"):
        swapped = lax.all_to_all(picked, "mode", split_axis=0, concat_axis=2, tiled=True)
    with jax.named_scope("spread_weights"):
        return lax.all_gather(swapped.reshape(piece, mode_count * width), "harm", axis=0, tiled=True)


def plain(mode_vectors, weights, cotangent, eigenvalues, eigen_cotangent, slab_rows, harm_count, mode_count):
    harm_index = lax.axis_index("harm")
    width = mode_vectors.shape[1]
    modes = width * mode_count
    full = lax.all_gather(mode_vectors, "mode", axis=1, tiled=True)
    owned_weights = gather_weights(weights, slab_rows, harm_index, harm_count, mode_count)
    gram = product(full, cotangent, 0, 0)
    gram = lax.psum_scatter(gram, "harm", scatter_dimension=0, tiled=True)
    weighted = weigh_gap(
        gram,
        harm_index * (modes // harm_count),
        lax.axis_index("mode") * width,
        eigenvalues,
        eigen_cotangent,
    )
    weighted = lax.all_gather(weighted, "mode", axis=1, tiled=True)
    weighted = lax.all_gather(weighted, "harm", axis=0, tiled=True)
    return product(product(owned_weights, weighted, 1, 0), full, 1, 1)


def solution(mesh):
    harm_count = mesh.shape["harm"]
    mode_count = mesh.shape["mode"]
    placed = (P("harm", "mode"), P("harm", "mode"), P("harm", "mode"), P(), P(), P())

    def local(*operands):
        return plain(*operands, harm_count, mode_count)

    return jax.shard_map(
        local, mesh=mesh, in_specs=placed, out_specs=P("mode", "harm"), check_vma=False
    )
```

profile of v0, /device:TPU:0, one launch (start us, length us, event | category | flops | bytes accessed | tf_op | source)
XLA Modules:
  0.0 702.6 jit_solution(5876162007898497041)
XLA Ops:
  7.4 0.7 all-gather.6.cloned.1.call-update
  8.1 0.0 reduce-scatter.3.cloned.1.call-start
  8.2 18.9 %gather_fusion = f32[4096,256]{1,0:T(8,128)} fusion(f32[6144,256]{1,0:T(8,128)} %param.7, s32[4096]{0:T(1024)S(1)} %fusion.3), kind=kCustom, calls=%fused_computation | custom fusion | bytes 8404992 | tf_op jit(solution)/shard_map/pick/jit(_take)/gather | solution.py:35
  27.2 5.6 copy.10
  32.7 5.5 select_select_fusion
  38.3 0.0 reduce-scatter.5.cloned.1.call-start
  38.3 399.3 %all-gather.6.cloned.1.call-done = f32[6144,1024]{1,0:T(8,128)} async-done(((f32[6144,256]{1,0:T(8,128)}), f32[6144,1024]{1,0:T(8,128)}) %all-gather.6.cloned.1.call-update) | async-done | bytes 25165840 | tf_op jit(solution)/shard_map/all_gather | solution.py:58
  437.7 44.0 %fusion.4 = f32[1024,256]{1,0:T(8,128)} fusion(f32[6144,1024]{1,0:T(8,128)} %all-gather.6.cloned.1.call-done, f32[6144,256]{1,0:T(8,128)} %param.8), kind=kOutput, calls=%fused_computation.13 | convolution fusion | flops 19327352832 | bytes 32505856 | tf_op jit(solution)/shard_map/dot_general | solution.py:11
  481.6 0.0 all-gather.4.cloned.1.call-start
  481.7 0.0 reduce-scatter.3.cloned.1.call-done
  481.7 19.2 %all_to_all.15 = f32[4,128,256]{1,2,0:T(8,128)} all-to-all(f32[4,128,256]{1,2,0:T(8,128)} %bitcast.19), channel_id=1, replica_groups=mesh['harm'=8,'mode'=4] {'mode'}, dimensions={0} | all-to-all | bytes 1048576 | tf_op jit(solution)/shard_map/swap/all_to_all | solution.py:49
  500.9 0.0 all-gather.4.cloned.1.call-update
  500.9 0.0 all-gather.8.cloned.1.call-start
  501.0 0.8 dynamic_slice.10
  501.7 0.8 dynamic_slice.9
  502.5 0.8 dynamic_slice.11
  503.2 12.6 %reduce-scatter.5.cloned.1.call-done = f32[128,256]{1,0:T(8,128)} async-done(((f32[1024,256]{1,0:T(8,128)}), f32[128,256]{1,0:T(8,128)}) %reduce-scatter.5.cloned.1.call-update) | async-done | bytes 131088 | tf_op jit(solution)/shard_map/reduce_scatter | solution.py:61
  515.8 1.0 fusion.2
  516.9 15.9 %all_gather.14 = f32[128,1024]{1,0:T(8,128)} all-gather(f32[128,256]{1,0:T(8,128)S(1)} %fusion.2), channel_id=1, replica_groups=mesh['harm'=8,'mode'=4] {'mode'}, dimensions={1}, use_global_device_ids=true | all-gather | bytes 655360 | tf_op jit(solution)/shard_map/all_gather | solution.py:69
  532.8 0.0 all-gather.8.cloned.1.call-update
  532.8 22.0 %all-gather.4.cloned.1.call-done = f32[1024,1024]{0,1:T(8,128)} async-done(((f32[128,1024]{0,1:T(8,128)}), f32[1024,1024]{0,1:T(8,128)}) %all-gather.4.cloned.1.call-update) | async-done | bytes 4194320 | tf_op jit(solution)/shard_map/spread_weights/all_gather | solution.py:51
  554.8 38.4 %all-gather.8.cloned.1.call-done = f32[1024,1024]{1,0:T(8,128)} async-done(((f32[128,1024]{1,0:T(8,128)}), f32[1024,1024]{1,0:T(8,128)}) %all-gather.8.cloned.1.call-update) | async-done | bytes 4194320 | tf_op jit(solution)/shard_map/all_gather | solution.py:70
  593.2 16.6 %fusion.5 = f32[1024,1024]{1,0:T(8,128)S(1)} fusion(f32[1024,1024]{0,1:T(8,128)} %all-gather.4.cloned.1.call-done, f32[1024,1024]{1,0:T(8,128)} %all-gather.8.cloned.1.call-done), kind=kOutput, calls=%fused_computation.14 | convolution fusion | flops 12884901888 | bytes 12582912 | tf_op jit(solution)/shard_map/dot_general | solution.py:11
  609.8 85.2 %fusion.6 = f32[1024,6144]{1,0:T(8,128)} fusion(f32[1024,1024]{1,0:T(8,128)S(1)} %fusion.5, f32[6144,1024]{1,0:T(8,128)} %all-gather.6.cloned.1.call-done), kind=kOutput, calls=%fused_computation.15 | convolution fusion | flops 77309411328 | bytes 54525952 | tf_op jit(solution)/shard_map/dot_general | solution.py:11
  (11 shorter events, 0.1 us)
Async XLA Ops:
  7.4 0.8 copy-start
  7.4 430.3 %all-gather.6.cloned.1.call-start = ((), (), s32[]{:S(2)}) async-start(), calls=%async_computation.5 | async-start | bytes 31457280 | tf_op jit(solution)/shard_map/all_gather | solution.py:58
  8.1 473.6 %reduce-scatter.3.cloned.1.call-start = ((), (), s32[]{:S(2)}) async-start(), calls=%async_computation.3 | async-start | bytes 4718592 | tf_op jit(solution)/shard_map/sum_weights/reduce_scatter | solution.py:46
  38.3 477.6 %reduce-scatter.5.cloned.1.call-start = ((), (), s32[]{:S(2)}) async-start(), calls=%async_computation.6 | async-start | bytes 1179648 | tf_op jit(solution)/shard_map/reduce_scatter | solution.py:61
  481.6 73.2 %all-gather.4.cloned.1.call-start = ((), (), s32[]{:S(2)}) async-start(), calls=%async_computation.4 | async-start | bytes 4718592 | tf_op jit(solution)/shard_map/spread_weights/all_gather | solution.py:51
  500.9 92.3 %all-gather.8.cloned.1.call-start = ((), (), s32[]{:S(2)}) async-start(), calls=%async_computation.7 | async-start | bytes 4718592 | tf_op jit(solution)/shard_map/all_gather | solution.py:70
Sparse Core Ops, SparseCore 0:
  9.7 427.8 all-gather.5
Sparse Core Ops, SparseCore 1:
  38.4 53.7 reduce-scatter.2
  481.7 34.1 reduce-scatter.4
  517.6 37.2 all-gather.3
  556.8 36.4 all-gather.7
where the time goes:
time: 703 us
  waiting for transfers between devices  473 us (67%)
  matrix products  146 us (21%)
  blocking collectives  35.1 us (5%)
  local copies, waits for them, and re-layouts  26.8 us (4%)
  between operations  15.1 us (2%)
    all_gather x1, waiting for transfers between devices, plain(): full = lax.all_gather(mode_vectors, 'mode', axis=1, tiled=True)  399 us
    dot_general x3, matrix products, product(): lax.dot_general(left, right, (((left_dim,), (right_dim,)), ((), ())), pre...  146 us
    all_gather x1, waiting for transfers between devices, plain(): weighted = lax.all_gather(weighted, 'harm', axis=0, tiled=True)  38.4 us
    gather x2, local copies, waits for them, and re-layouts, pick_rows(): picked = jnp.take(table, jnp.clip(offset, 0, row_count - 1), axis=0)  24.5 us
    all_gather x1, waiting for transfers between devices, gather_weights(): lax.all_gather(swapped.reshape(piece, mode_count * width), 'harm', axis=0...  22 us
    all_to_all x1, blocking collectives, gather_weights(): lax.all_to_all(picked, 'mode', split_axis=0, concat_axis=2, tiled=True)  19.2 us
    all_gather x1, blocking collectives, plain(): weighted = lax.all_gather(weighted, 'mode', axis=1, tiled=True)  15.9 us
  transfers between devices with their start and end apart: 5, of which 4 were waited for; matrix products, arithmetic and copies ran while one was open for 11% of the time, Pallas kernels for 0%

commit v1 on v0

--- a/solution.py
+++ b/solution.py
@@ -1,10 +1,16 @@
+import functools
+
 import jax
 import jax.numpy as jnp
 from jax import lax
+from jax.experimental import pallas as pl
+from jax.experimental.pallas import tpu as pltpu
 from jax.sharding import PartitionSpec as P
 
+
 regular = 0.01
-precision = lax.Precision.HIGHEST
+chunks = 4
+tile = 512
 
 
 def product(left, right, left_dim, right_dim):
@@ -12,7 +18,7 @@
         left,
         right,
         (((left_dim,), (right_dim,)), ((), ())),
-        precision=precision,
+        precision=lax.Precision.HIGH,
         preferred_element_type=jnp.float32,
     )
 
@@ -38,17 +44,13 @@
 
 def gather_weights(weights, slab_rows, harm_index, harm_count, mode_count):
     width = weights.shape[1]
-    with jax.named_scope("pick"):
-        picked = pick_rows(weights, slab_rows, harm_index)
+    picked = pick_rows(weights, slab_rows, harm_index)
     piece = slab_rows.shape[0] // (harm_count * mode_count)
     picked = picked.reshape(mode_count, harm_count, piece, width)
-    with jax.named_scope("sum_weights"):
-        picked = lax.psum_scatter(picked, "harm", scatter_dimension=1, tiled=True)
+    picked = lax.psum_scatter(picked, "harm", scatter_dimension=1, tiled=True)
     picked = picked.reshape(mode_count, piece, width)
-    with jax.named_scope("swap"):
-        swapped = lax.all_to_all(picked, "mode", split_axis=0, concat_axis=2, tiled=True)
-    with jax.named_scope("spread_weights"):
-        return lax.all_gather(swapped.reshape(piece, mode_count * width), "harm", axis=0, tiled=True)
+    swapped = lax.all_to_all(picked, "mode", split_axis=0, concat_axis=2, tiled=True)
+    return lax.all_gather(swapped.reshape(piece, mode_count * width), "harm", axis=0, tiled=True)
 
 
 def plain(mode_vectors, weights, cotangent, eigenvalues, eigen_cotangent, slab_rows, harm_count, mode_count):
@@ -71,13 +73,306 @@
     return product(product(owned_weights, weighted, 1, 0), full, 1, 1)
 
 
+def shift(value, pairs):
+    return lax.ppermute(value, "mode", pairs)
+
+
+def split_outside(value):
+    high = lax.reduce_precision(value, 8, 7)
+    return high.astype(jnp.bfloat16), lax.reduce_precision(value - high, 8, 7).astype(jnp.bfloat16)
+
+
+def split(value):
+    high = value.astype(jnp.bfloat16)
+    low = (value - high.astype(jnp.float32)).astype(jnp.bfloat16)
+    return high, low
+
+
+def final_kernel(first_row, pieces, z_ref, own, b1, b2, b3, a1, a2, a3, *rest):
+    out_ref, x_buf, x3, sems = rest[-4:]
+    step = pl.program_id(0)
+    steps = pl.num_programs(0)
+    layer = lax.axis_index("mode")
+    width = own.shape[1]
+    rows = x_buf.shape[1]
+    below = {1: b1, 2: b2, 3: b3}
+    above = {1: a1, 2: a2, 3: a3}
+
+    def fetch(at, slot):
+        for piece in range(pieces):
+            for here in range(pieces):
+
+                @pl.when(layer == here)
+                def _():
+                    delta = piece - here
+                    begin = at * rows
+                    if delta == 0:
+                        source = own
+                        begin = first_row + begin
+                    else:
+                        source = above[delta] if delta > 0 else below[-delta]
+                    pltpu.make_async_copy(
+                        source.at[pl.ds(begin, rows), :],
+                        x_buf.at[slot, :, pl.ds(piece * width, width)],
+                        sems.at[slot, piece],
+                    ).start()
+
+    slot = lax.rem(step, 2)
+
+    @pl.when(step == 0)
+    def _():
+        fetch(0, 0)
+
+    @pl.when(step + 1 < steps)
+    def _():
+        fetch(step + 1, 1 - slot)
+
+    for piece in range(pieces):
+        pltpu.make_async_copy(
+            own.at[pl.ds(0, rows), :],
+            x_buf.at[slot, :, pl.ds(piece * width, width)],
+            sems.at[slot, piece],
+        ).wait()
+    depth = x_buf.shape[2]
+    high, low = split(x_buf[slot])
+    x3[:, :depth] = high
+    x3[:, depth : 2 * depth] = high
+    x3[:, 2 * depth :] = low
+    out_ref[...] = lax.dot_general(
+        z_ref[...], x3[...], (((1,), (1,)), ((), ())), preferred_element_type=jnp.float32
+    )
+
+
+def gram_kernel(lefts, rights, plan, *refs):
+    sides = refs[: lefts + len(rights)]
+    count = len(plan)
+    outs = refs[-2 - count : -2]
+    seeds = refs[lefts + len(rights) : -2 - count]
+    left3, right3 = refs[-2:]
+    rows = sides[0].shape[0]
+    slots = [sum(rights[:i]) for i in range(len(rights))]
+
+    @pl.when(pl.program_id(0) == 0)
+    def _():
+        for index, out in enumerate(outs):
+            out[...] = seeds[index][...] if seeds else jnp.zeros_like(out)
+
+    for index in range(lefts):
+        width = sides[index].shape[1]
+        high, low = split(sides[index][...])
+        at = pl.ds(index * width, width)
+        left3[:rows, at] = high
+        left3[rows : 2 * rows, at] = low
+        left3[2 * rows :, at] = high
+    for index, fresh in enumerate(rights):
+        if not fresh:
+            continue
+        value = sides[lefts + index][...]
+        if index + 1 < len(rights) and not rights[index + 1]:
+            value = value + sides[lefts + index + 1][...]
+        width = value.shape[1]
+        high, low = split(value)
+        at = pl.ds(slots[index] * width, width)
+        right3[:rows, at] = high
+        right3[rows : 2 * rows, at] = high
+        right3[2 * rows :, at] = low
+    for out, (row, col) in zip(outs, plan):
+        high, wide = out.shape
+        out[...] += lax.dot_general(
+            left3[:, row : row + high],
+            right3[:, col : col + wide],
+            (((0,), (0,)), ((), ())),
+            preferred_element_type=jnp.float32,
+        )
+
+
+def gram_chunk(index, height, lefts, rights, fresh, plan, shapes, seeds):
+    width = lefts[0].shape[1]
+    steps = height // tile
+    first = index * steps
+    whole = pl.BlockSpec((tile, width), lambda i: (first + i, 0))
+    part = pl.BlockSpec((tile, width), lambda i: (i, 0))
+    specs = [part if v.shape[0] == height else whole for v in (*lefts, *rights)]
+    fixed = [pl.BlockSpec(s, lambda i: (0, 0)) for s in shapes]
+    work = sum(s[0] * s[1] for s in shapes)
+    operands = [*lefts, *rights]
+    if seeds is not None:
+        operands += seeds
+        specs += fixed
+    return pl.pallas_call(
+        functools.partial(gram_kernel, len(lefts), fresh, plan),
+        grid=(steps,),
+        in_specs=specs,
+        out_specs=fixed,
+        out_shape=[jax.ShapeDtypeStruct(s, jnp.float32) for s in shapes],
+        scratch_shapes=[
+            pltpu.VMEM((3 * tile, len(lefts) * width), jnp.bfloat16),
+            pltpu.VMEM((3 * tile, sum(fresh) * width), jnp.bfloat16),
+        ],
+        compiler_params=pltpu.CompilerParams(vmem_limit_bytes=32 * 2**20),
+        cost_estimate=pl.CostEstimate(
+            flops=6 * work * height,
+            bytes_accessed=4 * len(operands) * height * width,
+            transcendentals=0,
+        ),
+        name="gram_chunk",
+    )(*operands)
+
+
+def final_chunk(index, z3, own, lists, previous, columns):
+    rows = z3.shape[0]
+    width = own.shape[1]
+    pieces = z3.shape[1] // (3 * width)
+    first_row = index * lists[0].shape[0]
+    steps = lists[0].shape[0] // tile
+    anywhere = pl.BlockSpec(memory_space=pl.ANY)
+    operands = [z3, own, *lists]
+    specs = [pl.BlockSpec(z3.shape, lambda i: (0, 0), pipeline_mode=pl.Buffered(1))] + [anywhere] * 7
+    aliases = {}
+    if previous is not None:
+        operands.append(previous)
+        specs.append(anywhere)
+        aliases = {8: 0}
+    first_block = first_row // tile
+    return pl.pallas_call(
+        functools.partial(final_kernel, first_row, pieces),
+        grid=(steps,),
+        in_specs=specs,
+        out_specs=pl.BlockSpec((rows, tile), lambda i: (0, first_block + i)),
+        out_shape=jax.ShapeDtypeStruct((rows, columns), jnp.float32),
+        scratch_shapes=[
+            pltpu.VMEM((2, tile, pieces * width), jnp.float32),
+            pltpu.VMEM((tile, 3 * pieces * width), jnp.bfloat16),
+            pltpu.SemaphoreType.DMA((2, pieces)),
+        ],
+        input_output_aliases=aliases,
+        compiler_params=pltpu.CompilerParams(vmem_limit_bytes=40 * 2**20),
+        cost_estimate=pl.CostEstimate(
+            flops=6 * rows * z3.shape[1] // 3 * steps * tile,
+            bytes_accessed=4 * steps * tile * (rows + pieces * width),
+            transcendentals=0,
+        ),
+        name="final_chunk",
+    )(*operands)
+
+
+def slab_order(slab_rows, row_count, harm_count, harm_index):
+    total = slab_rows.shape[0]
+    share = total // harm_count
+    owner = slab_rows // row_count
+    ids = lax.broadcasted_iota(jnp.int32, (harm_count, total), 0)
+    hit = (owner[None, :] == ids).astype(jnp.int32)
+    running = jnp.cumsum(hit, axis=1)
+    rank = jnp.sum(hit * running, axis=0) - 1
+    position = owner * share + rank
+    slots = lax.broadcasted_iota(jnp.int32, (share, total), 0)
+    mine = (position - harm_index * share)[None, :] == slots
+    offsets = jnp.sum(jnp.where(mine, (slab_rows - harm_index * row_count)[None, :], 0), axis=1)
+    return position, offsets
+
+
+def line_body(mode_vectors, weights, cotangent, eigenvalues, eigen_cotangent, slab_rows, harm_count, mode_count):
+    harm = lax.axis_index("harm")
+    layer = lax.axis_index("mode")
+    height, width = mode_vectors.shape
+    total = slab_rows.shape[0]
+    lower = layer <= 1
+    own = jnp.split(mode_vectors, chunks, 0)
+    slope = jnp.split(cotangent, chunks, 0)
+
+    def hop(values, pairs):
+        results = []
+        for value in values:
+            results.append(shift(value, pairs))
+        return results
+
+    b1 = hop(own, [(0, 1), (1, 2), (2, 3)])
+    a1 = hop(own, [(1, 0), (2, 1), (3, 2)])
+
+    position, offsets = slab_order(slab_rows, height, harm_count, harm)
+    picked = jnp.take(weights, offsets, axis=0, mode="clip")
+    w_b1 = shift(picked, [(0, 1), (1, 2)])
+    w_a1 = shift(picked, [(3, 2), (2, 1)])
+    w_third = shift(w_b1, [(1, 2)]) + shift(w_a1, [(2, 1)])
+    w_all = jnp.concatenate([picked, w_b1, w_a1, w_third], axis=1)
+    w_every = lax.all_gather(w_all, "harm", axis=0, tiled=True)
+    w_slab = jnp.take(w_every, position, axis=0, mode="clip")
+
+    b2 = hop(b1, [(1, 2), (2, 3)])
+    a2 = hop(a1, [(2, 1), (1, 0)])
+    edge = hop(slope, [(0, 1), (3, 2)])
+    b3 = hop(b2, [(2, 3)])
+    a3 = hop(a2, [(1, 0)])
+
+    part = height // chunks
+    near = None
+    for c in range(chunks):
+        near = gram_chunk(
+            c, part, [cotangent], [mode_vectors, b1[c], a1[c]], (1, 1, 1),
+            ((0, 0),), ((width, 3 * width),), near,
+        )
+    far_parts = None
+    for c in range(chunks):
+        side = edge[c]
+        if c == 1:
+            side, w_slab = lax.optimization_barrier((side, w_slab))
+        far_parts = gram_chunk(
+            c, part, [cotangent, side], [mode_vectors, b1[c], a1[c], b2[c], a2[c]], (1, 1, 1, 1, 0),
+            ((0, 3 * width), (width, 0)), ((width, width), (width, 4 * width)), far_parts,
+        )
+    top = jnp.concatenate([near[0], far_parts[0]], axis=1)
+    gram = jnp.concatenate([top, far_parts[1]], axis=0)
+    gram = lax.psum_scatter(gram, "harm", scatter_dimension=0, tiled=True)
+
+    span = 2 * width // harm_count
+    half = harm_count // 2
+    last = mode_count - 1
+    end = jnp.where(lower, 0, last)
+    far = jnp.where(lower, last, 0)
+    first_col = jnp.where(harm < half, layer * width + harm * span, end * width + (harm - half) * span)
+    blocks = [layer, jnp.maximum(layer - 1, 0), jnp.minimum(layer + 1, last), far]
+    row_ids = jnp.concatenate([b * width + jnp.arange(width, dtype=jnp.int32) for b in blocks])
+    eigen_i = jnp.concatenate([lax.dynamic_slice_in_dim(eigenvalues, b * width, width) for b in blocks])
+    eigen_j = lax.dynamic_slice_in_dim(eigenvalues, first_col, span)
+    slope_j = lax.dynamic_slice_in_dim(eigen_cotangent, first_col, span)
+    col_ids = first_col + jnp.arange(span, dtype=jnp.int32)
+    differ = eigen_j[:, None] - eigen_i[None, :]
+    factor = differ / (differ * differ + regular)
+    weighted = factor * gram + jnp.where(col_ids[:, None] == row_ids[None, :], slope_j[:, None], 0.0)
+
+    zt = product(weighted, w_slab, 1, 1).reshape(span, mode_count, total // mode_count)
+    keep = jnp.where(lower, zt[:, :2], zt[:, 2:])
+    give = jnp.where(lower, zt[:, 2:], zt[:, :2])
+    got = shift(give, [(1, 2), (2, 1)])
+    both = jnp.stack([jnp.where(lower, keep, got), jnp.where(lower, got, keep)])
+    outer = shift(jnp.where(lower, both[:, :, 0], both[:, :, 1]), [(1, 0), (2, 3)])
+    inner = jnp.where(lower, both[:, :, 1], both[:, :, 0])
+    mine = jnp.where((layer == 0) | (layer == last), outer, inner)
+    every = lax.all_gather(mine, "harm", axis=0, tiled=False)
+    zt = jnp.concatenate(
+        [every[half:, 0], every[:half, 0], every[:half, 1], every[half:, 1]], axis=0
+    ).reshape(mode_count * width, total // mode_count)
+    high, low = split_outside(zt.T)
+    z3 = jnp.concatenate([high, low, high], axis=1)
+
+    out = None
+    for c in range(chunks):
+        out = final_chunk(c, z3, mode_vectors, [b1[c], b2[c], b3[c], a1[c], a2[c], a3[c]], out, height)
+    return out
+
+
+def line(*operands):
+    return line_body(*operands)
+
+
 def solution(mesh):
     harm_count = mesh.shape["harm"]
     mode_count = mesh.shape["mode"]
     placed = (P("harm", "mode"), P("harm", "mode"), P("harm", "mode"), P(), P(), P())
+    form = line if mode_count == 4 else plain
 
     def local(*operands):
-        return plain(*operands, harm_count, mode_count)
+        return form(*operands, harm_count, mode_count)
 
     return jax.shard_map(
         local, mesh=mesh, in_specs=placed, out_specs=P("mode", "harm"), check_vma=False

time: 703 us -> 682 us (0.970); the launches traced: 703 us -> 674 us
  matrix products: 146 us -> 14.7 us
  waiting for transfers between devices: 473 us -> 356 us
  Pallas kernels: 0 us -> 99.6 us
  starting transfers between devices: 0.18 us -> 91.6 us
  local copies, waits for them, and re-layouts: 26.8 us -> 76.6 us
  blocking collectives: 35.1 us -> 0 us
  other arithmetic: 6.58 us -> 21.1 us
    all_gather x3 -> x2, waiting for transfers between devices: 460 us -> 27.6 us  [the longest x1 27.6 us: line_body(): every = lax.all_gather(mine, 'harm', axis=0, tiled=False)]
    ppermute x0 -> x34, waiting for transfers between devices: none -> 266 us  [shift(): return lax.ppermute(value, 'mode', pairs)]
    dot_general x3 -> x1, matrix products: 146 us -> 14.7 us  [product(): lax.dot_general(left, right, (((left_dim,), (right_dim,)), ((), ())), pre...]
    pallas_call x0 -> x12, Pallas kernels: none -> 99.6 us  [the longest x4 64.1 us: final_chunk(): pl.pallas_call(functools.partial(final_kernel, first_row, pieces), grid=(...]
    ppermute x0 -> x34, starting transfers between devices: none -> 91.4 us  [shift(): return lax.ppermute(value, 'mode', pairs)]
    reduce_scatter x2 -> x1, waiting for transfers between devices: 12.6 us -> 62.6 us  [line_body(): gram = lax.psum_scatter(gram, 'harm', scatter_dimension=0, tiled=True)]
    unnamed x2 -> x62, local copies, waits for them, and re-layouts: 0.01 us -> 21.5 us
    all_to_all x1 -> x0, blocking collectives: 19.2 us -> none  [gather_weights(): lax.all_to_all(picked, 'mode', split_axis=0, concat_axis=2, tiled=True)]
  transfers between devices with their start and end apart: 5 -> 37, of which waited for: 4 -> 14; matrix products, arithmetic and copies ran while one was open for 11% -> 8% of each run, Pallas kernels for 0% -> 11%
where the time goes in v1:
time: 682 us; the launch traced here: 674 us
  waiting for transfers between devices  356 us (52%)
  Pallas kernels  99.6 us (15%)
  starting transfers between devices  91.6 us (13%)
  local copies, waits for them, and re-layouts  76.6 us (11%)
  other arithmetic  21.1 us (3%)
  matrix products  14.7 us (2%)
  between operations  14.2 us (2%)
    ppermute x34, waiting for transfers between devices, shift(): return lax.ppermute(value, 'mode', pairs)  266 us
    ppermute x34, starting transfers between devices, shift(): return lax.ppermute(value, 'mode', pairs)  91.4 us
    pallas_call x4, Pallas kernels, final_chunk(): pl.pallas_call(functools.partial(final_kernel, first_row, pieces), grid=(...  64.1 us
    reduce_scatter x1, waiting for transfers between devices, line_body(): gram = lax.psum_scatter(gram, 'harm', scatter_dimension=0, tiled=True)  62.6 us
    pallas_call x8, Pallas kernels, gram_chunk(): pl.pallas_call(functools.partial(gram_kernel, len(lefts), fresh, plan), g...  35.5 us
    gather x1, local copies, waits for them, and re-layouts, line_body(): w_slab = jnp.take(w_every, position, axis=0, mode='clip')  27.9 us
    all_gather x1, waiting for transfers between devices, line_body(): every = lax.all_gather(mine, 'harm', axis=0, tiled=False)  27.6 us
    unnamed x62, local copies, waits for them, and re-layouts  21.5 us
  transfers between devices with their start and end apart: 37, of which 14 were waited for; matrix products, arithmetic and copies ran while one was open for 8% of the time, Pallas kernels for 11%

profile of v1, /device:TPU:0, one launch (start us, length us, event | category | flops | bytes accessed | tf_op | source)
XLA Modules:
  0.0 674.0 jit_solution(1394430533026110321)
XLA Ops:
  22.2 10.4 %collective-permute-done.15 = f32[512,256]{1,0:T(8,128)S(1)} collective-permute-done((f32[512,256]{1,0:T(8,128)S(1)}, f32[512,256]{1,0:T(8,128)S(1)}, u32[]{:S(2)}, u32[]{:S(2)}) %collective-permute-start.15) | collective-permute-done | bytes 524320 | tf_op jit(solution)/shard_map/ppermute | solution.py:77
  40.2 21.2 %collective-permute-start.14 = (f32[1536,256]{1,0:T(8,128)S(1)}, f32[1536,256]{1,0:T(8,128)S(1)}, u32[]{:S(2)}, u32[]{:S(2)}) collective-permute-start(f32[1536,256]{1,0:T(8,128)S(1)} %get-tuple-element.30), channel_id=1, source_target_pairs={{0,1},{3,2},{4,5},{7,6},{8,9},{11,10},{12,13},{15,14},{16,17},{19,... | collective-permute-start | bytes 4718600 | tf_op jit(solution)/shard_map/ppermute | solution.py:77
  75.1 20.9 %collective-permute-done.14.refs_1_ = f32[1536,256]{1,0:T(8,128)S(1)} collective-permute-done((f32[1536,256]{1,0:T(8,128)S(1)}, f32[1536,256]{1,0:T(8,128)S(1)}, u32[]{:S(2)}, u32[]{:S(2)}) %collective-permute-start.14) | collective-permute-done | bytes 1572896 | tf_op jit(solution)/shard_map/ppermute | solution.py:77
  98.5 31.3 %collective-permute-done.6.refs_2_.refs_3_.b1 = f32[1536,256]{1,0:T(8,128)S(1)} collective-permute-done((f32[1536,256]{1,0:T(8,128)S(1)}, f32[1536,256]{1,0:T(8,128)S(1)}, u32[]{:S(2)}, u32[]{:S(2)}) %collective-permute-start.6) | collective-permute-done | bytes 1572896 | tf_op jit(solution)/shard_map/ppermute | solution.py:77
  136.6 26.9 %collective-permute-done.21.refs_1_ = f32[1536,256]{1,0:T(8,128)S(1)} collective-permute-done((f32[1536,256]{1,0:T(8,128)S(1)}, f32[1536,256]{1,0:T(8,128)S(1)}, u32[]{:S(2)}, u32[]{:S(2)}) %collective-permute-start.21) | collective-permute-done | bytes 1572896 | tf_op jit(solution)/shard_map/ppermute | solution.py:77
  168.0 29.2 %collective-permute-done.4.refs_2_.refs_3_.b1 = f32[1536,256]{1,0:T(8,128)S(1)} collective-permute-done((f32[1536,256]{1,0:T(8,128)S(1)}, f32[1536,256]{1,0:T(8,128)S(1)}, u32[]{:S(2)}, u32[]{:S(2)}) %collective-permute-start.4) | collective-permute-done | bytes 1572896 | tf_op jit(solution)/shard_map/ppermute | solution.py:77
  198.5 6.2 collective-permute-start
  204.7 26.2 %collective-permute-done.2.refs_2_.refs_3_.b1 = f32[1536,256]{1,0:T(8,128)} collective-permute-done((f32[1536,256]{1,0:T(8,128)S(1)}, f32[1536,256]{1,0:T(8,128)}, u32[]{:S(2)}, u32[]{:S(2)}) %collective-permute-start.2) | collective-permute-done | bytes 1572896 | tf_op jit(solution)/shard_map/ppermute | solution.py:77
  233.0 31.6 %collective-permute-done.11.refs_1_ = f32[1536,256]{1,0:T(8,128)S(1)} collective-permute-done((f32[1536,256]{1,0:T(8,128)S(1)}, f32[1536,256]{1,0:T(8,128)S(1)}, u32[]{:S(2)}, u32[]{:S(2)}) %collective-permute-start.11) | collective-permute-done | bytes 1572896 | tf_op jit(solution)/shard_map/ppermute | solution.py:77
  267.9 27.3 %collective-permute-done.refs_2_.refs_3_.b1 = f32[1536,256]{1,0:T(8,128)} collective-permute-done((f32[1536,256]{1,0:T(8,128)S(1)}, f32[1536,256]{1,0:T(8,128)}, u32[]{:S(2)}, u32[]{:S(2)}) %collective-permute-start) | collective-permute-done | bytes 1572896 | tf_op jit(solution)/shard_map/ppermute | solution.py:77
  298.4 8.5 %collective-permute-start.8 = (f32[1536,256]{1,0:T(8,128)}, f32[1536,256]{1,0:T(8,128)}, u32[]{:S(2)}, u32[]{:S(2)}) collective-permute-start(f32[1536,256]{1,0:T(8,128)} %get-tuple-element.32), channel_id=1, source_target_pairs={{0,1},{3,2},{4,5},{7,6},{8,9},{11,10},{12,13},{15,14},{16,17},{19,... | collective-permute-start | bytes 4718600 | tf_op jit(solution)/shard_map/ppermute | solution.py:77
  335.5 27.9 %gather_fusion.1 = f32[4096,1024]{1,0:T(8,128)} fusion(f32[4096,1024]{1,0:T(8,128)} %all-gather.4.cloned.1.call-done, s32[4096]{0:T(1024)S(1)} %get-tuple-element.43), kind=kCustom, calls=%fused_computation.1 | custom fusion | bytes 33570816 | tf_op jit(solution)/shard_map/jit(_take)/gather | solution.py:299
  379.6 6.0 gram_chunk.14
  385.7 6.4 gram_chunk.15
  395.3 62.6 %reduce-scatter.2.cloned.1.call-done = f32[64,1024]{1,0:T(8,128)} async-done(((f32[512,1024]{1,0:T(8,128)}), f32[64,1024]{1,0:T(8,128)}) %reduce-scatter.2.cloned.1.call-update) | async-done | bytes 262160 | tf_op jit(solution)/shard_map/reduce_scatter | solution.py:325
  457.9 14.7 %fusion.6 = f32[64,4096]{1,0:T(8,128)} fusion(f32[4096,1024]{1,0:T(8,128)} %gather_fusion.1, f32[64,1024]{1,0:T(8,128)} %reduce-scatter.2.cloned.1.call-done, f32[64]{0:T(128)S(1)} %dynamic_slice.23, s32[1024]{0:T(1024)S(1)} %pad_add_fusion, f32[1024]{0:T(1024)S(1)} %pad_maximum_fusion.5, f32[64]{0:T(128)S(1)} %dynamic_slice.18, s32[64]{0:T(128)S(1)} %iota_add_fusion.4), kind=kOutput, calls=%fused_computation.31 | convolution fusion | flops 1611137024 | bytes 18096896 | tf_op jit(solution)/shard_map/dot_general | solution.py:17
  481.9 27.3 %collective-permute-done.25 = f32[2,64,1024]{2,1,0:T(8,128)} collective-permute-done((f32[2,64,1024]{2,1,0:T(8,128)}, f32[2,64,1024]{2,1,0:T(8,128)}, u32[]{:S(2)}, u32[]{:S(2)}) %collective-permute-start.25) | collective-permute-done | bytes 524320 | tf_op jit(solution)/shard_map/ppermute | solution.py:77
  519.8 27.6 %all-gather.6.cloned.1.call-done = f32[16,64,1024]{2,1,0:T(8,128)} async-done(((f32[2,64,1024]{2,1,0:T(8,128)}), f32[16,64,1024]{2,1,0:T(8,128)}) %all-gather.6.cloned.1.call-update) | async-done | bytes 4194320 | tf_op jit(solution)/shard_map/all_gather | solution.py:351
  567.0 16.0 %final_chunk.4.rest_0_ = f32[1024,6144]{1,0:T(8,128)} custom-call(bf16[1024,3072]{1,0:T(8,128)(2,1)} %pad_maximum_fusion.z_ref, f32[6144,256]{1,0:T(8,128)} %own.7, f32[1536,256]{1,0:T(8,128)S(1)} %collective-permute-done.6.refs_2_.refs_3_.b1, f32[1536,256]{1,0:T(8,128)S(1)} %copy-done.9, f32[1536,256]{1,0:T(8,128)} %collective-permute-done.32.b3, ...), custom_call_target="tpu_custom_call" | custom-call | flops 9663676416 | bytes 12582912 | tf_op jit(solution)/shard_map/final_chunk/pallas_call | solution.py:237
  586.6 16.0 %final_chunk.5.rest_0_ = f32[1024,6144]{1,0:T(8,128)} custom-call(bf16[1024,3072]{1,0:T(8,128)(2,1)} %pad_maximum_fusion.z_ref, f32[6144,256]{1,0:T(8,128)} %own.7, f32[1536,256]{1,0:T(8,128)S(1)} %copy-done.4, f32[1536,256]{1,0:T(8,128)S(1)} %copy-done.14, f32[1536,256]{1,0:T(8,128)} %collective-permute-done.30.b3, ...), custom_call_target="tpu_custom_call", output_to_operand_aliasing={{}: (8, {})} | custom-call | flops 9663676416 | bytes 12582912 | tf_op jit(solution)/shard_map/final_chunk/pallas_call | solution.py:237
  602.7 17.5 %collective-permute-done.29.a3 = f32[1536,256]{1,0:T(8,128)S(1)} collective-permute-done((f32[1536,256]{1,0:T(8,128)}, f32[1536,256]{1,0:T(8,128)S(1)}, u32[]{:S(2)}, u32[]{:S(2)}) %collective-permute-start.29) | collective-permute-done | bytes 1572896 | tf_op jit(solution)/shard_map/ppermute | solution.py:77
  620.2 16.0 %final_chunk.6.rest_0_ = f32[1024,6144]{1,0:T(8,128)} custom-call(bf16[1024,3072]{1,0:T(8,128)(2,1)} %pad_maximum_fusion.z_ref, f32[6144,256]{1,0:T(8,128)} %own.7, f32[1536,256]{1,0:T(8,128)} %collective-permute-done.2.refs_2_.refs_3_.b1, f32[1536,256]{1,0:T(8,128)} %collective-permute-done.12.refs_5_.b2, ...), custom_call_target="tpu_custom_call", output_to_operand_aliasing={{}: (8, {})} | custom-call | flops 9663676416 | bytes 12582912 | tf_op jit(solution)/shard_map/final_chunk/pallas_call | solution.py:237
  636.2 14.9 %collective-permute-done.27.a3 = f32[1536,256]{1,0:T(8,128)S(1)} collective-permute-done((f32[1536,256]{1,0:T(8,128)}, f32[1536,256]{1,0:T(8,128)S(1)}, u32[]{:S(2)}, u32[]{:S(2)}) %collective-permute-start.27) | collective-permute-done | bytes 1572896 | tf_op jit(solution)/shard_map/ppermute | solution.py:77
  651.2 16.0 %final_chunk.7 = f32[1024,6144]{1,0:T(8,128)} custom-call(bf16[1024,3072]{1,0:T(8,128)(2,1)} %pad_maximum_fusion.z_ref, f32[6144,256]{1,0:T(8,128)} %own.7, f32[1536,256]{1,0:T(8,128)} %collective-permute-done.refs_2_.refs_3_.b1, f32[1536,256]{1,0:T(8,128)} %collective-permute-done.9.refs_5_.b2, ...), custom_call_target="tpu_custom_call", output_to_operand_aliasing={{}: (8, {})} | custom-call | flops 9663676416 | bytes 12582912 | tf_op jit(solution)/shard_map/final_chunk/pallas_call | solution.py:237
  (164 shorter events, 151.0 us)
Async XLA Ops:
  6.5 329.0 %all-gather.4.cloned.1.call-start = ((), (), s32[]{:S(2)}) async-start(), calls=%async_computation.1 | async-start | bytes 18874368 | tf_op jit(solution)/shard_map/all_gather | solution.py:298
  35.7 422.2 %reduce-scatter.2.cloned.1.call-start = ((), (), s32[]{:S(2)}) async-start(), calls=%async_computation.2 | async-start | bytes 2359296 | tf_op jit(solution)/shard_map/reduce_scatter | solution.py:325
  67.8 67.6 %collective-permute-start.7 = (f32[1536,256]{1,0:T(8,128)S(1)}, f32[1536,256]{1,0:T(8,128)S(1)}, u32[]{:S(2)}, u32[]{:S(2)}) collective-permute-start(f32[1536,256]{1,0:T(8,128)S(1)} %get-tuple-element.25), channel_id=1, source_target_pairs={{1,0},{2,1},{3,2},{5,4},{6,5},{7,6},{9,8},{10,9},{11,10},{13,12},{... | collective-permute-start | bytes 4718600 | tf_op jit(solution)/shard_map/ppermute | solution.py:77
  69.1 94.4 %collective-permute-start.21 = (f32[1536,256]{1,0:T(8,128)S(1)}, f32[1536,256]{1,0:T(8,128)S(1)}, u32[]{:S(2)}, u32[]{:S(2)}) collective-permute-start(f32[1536,256]{1,0:T(8,128)S(1)} %get-tuple-element.29), channel_id=1, source_target_pairs={{0,1},{3,2},{4,5},{7,6},{8,9},{11,10},{12,13},{15,14},{16,17},{19,... | collective-permute-start | bytes 4718600 | tf_op jit(solution)/shard_map/ppermute | solution.py:77
  73.7 123.5 %collective-permute-start.4 = (f32[1536,256]{1,0:T(8,128)S(1)}, f32[1536,256]{1,0:T(8,128)S(1)}, u32[]{:S(2)}, u32[]{:S(2)}) collective-permute-start(f32[1536,256]{1,0:T(8,128)S(1)} %get-tuple-element.26), channel_id=1, source_target_pairs={{0,1},{1,2},{2,3},{4,5},{5,6},{6,7},{8,9},{9,10},{10,11},{12,13},{... | collective-permute-start | bytes 4718600 | tf_op jit(solution)/shard_map/ppermute | solution.py:77
  97.2 101.3 %collective-permute-start.5 = (f32[1536,256]{1,0:T(8,128)S(1)}, f32[1536,256]{1,0:T(8,128)S(1)}, u32[]{:S(2)}, u32[]{:S(2)}) collective-permute-start(f32[1536,256]{1,0:T(8,128)S(1)} %get-tuple-element.26), channel_id=1, source_target_pairs={{1,0},{2,1},{3,2},{5,4},{6,5},{7,6},{9,8},{10,9},{11,10},{13,12},{... | collective-permute-start | bytes 4718600 | tf_op jit(solution)/shard_map/ppermute | solution.py:77
  129.8 101.1 %collective-permute-start.2 = (f32[1536,256]{1,0:T(8,128)S(1)}, f32[1536,256]{1,0:T(8,128)}, u32[]{:S(2)}, u32[]{:S(2)}) collective-permute-start(f32[1536,256]{1,0:T(8,128)S(1)} %get-tuple-element.27), channel_id=1, source_target_pairs={{0,1},{1,2},{2,3},{4,5},{5,6},{6,7},{8,9},{9,10},{10,11},{12,13},{... | collective-permute-start | bytes 4718600 | tf_op jit(solution)/shard_map/ppermute | solution.py:77
  135.3 96.3 %collective-permute-start.3 = (f32[1536,256]{1,0:T(8,128)S(1)}, f32[1536,256]{1,0:T(8,128)}, u32[]{:S(2)}, u32[]{:S(2)}) collective-permute-start(f32[1536,256]{1,0:T(8,128)S(1)} %get-tuple-element.27), channel_id=1, source_target_pairs={{1,0},{2,1},{3,2},{5,4},{6,5},{7,6},{9,8},{10,9},{11,10},{13,12},{... | collective-permute-start | bytes 4718600 | tf_op jit(solution)/shard_map/ppermute | solution.py:77
  163.5 101.1 %collective-permute-start.11 = (f32[1536,256]{1,0:T(8,128)S(1)}, f32[1536,256]{1,0:T(8,128)S(1)}, u32[]{:S(2)}, u32[]{:S(2)}) collective-permute-start(f32[1536,256]{1,0:T(8,128)S(1)} %get-tuple-element.31), channel_id=1, source_target_pairs={{0,1},{3,2},{4,5},{7,6},{8,9},{11,10},{12,13},{15,14},{16,17},{19,... | collective-permute-start | bytes 4718600 | tf_op jit(solution)/shard_map/ppermute | solution.py:77
  197.2 69.4 %collective-permute-start.1 = (f32[1536,256]{1,0:T(8,128)S(1)}, f32[1536,256]{1,0:T(8,128)}, u32[]{:S(2)}, u32[]{:S(2)}) collective-permute-start(f32[1536,256]{1,0:T(8,128)S(1)} %get-tuple-element.28), channel_id=1, source_target_pairs={{1,0},{2,1},{3,2},{5,4},{6,5},{7,6},{9,8},{10,9},{11,10},{13,12},{... | collective-permute-start | bytes 4718600 | tf_op jit(solution)/shard_map/ppermute | solution.py:77
  198.5 96.7 %collective-permute-start = (f32[1536,256]{1,0:T(8,128)S(1)}, f32[1536,256]{1,0:T(8,128)}, u32[]{:S(2)}, u32[]{:S(2)}) collective-permute-start(f32[1536,256]{1,0:T(8,128)S(1)} %get-tuple-element.28), channel_id=1, source_target_pairs={{0,1},{1,2},{2,3},{4,5},{5,6},{6,7},{8,9},{9,10},{10,11},{12,13},{... | collective-permute-start | bytes 4718600 | tf_op jit(solution)/shard_map/ppermute | solution.py:77
  230.9 66.2 %collective-permute-start.22 = (f32[1536,256]{1,0:T(8,128)S(1)}, f32[1536,256]{1,0:T(8,128)S(1)}, u32[]{:S(2)}, u32[]{:S(2)}) collective-permute-start(f32[1536,256]{1,0:T(8,128)S(1)} %collective-permute-done.6.refs_2_.refs_3_.b1), channel_id=1, source_target_pairs={{1,2},{2,3},{5,6},{6,7},{9,10},{10,11},{13,14},{14,15},{17,18},{18... | collective-permute-start | bytes 4718600 | tf_op jit(solution)/shard_map/ppermute | solution.py:77
  231.7 66.7 %collective-permute-start.23 = (f32[1536,256]{1,0:T(8,128)S(1)}, f32[1536,256]{1,0:T(8,128)S(1)}, u32[]{:S(2)}, u32[]{:S(2)}) collective-permute-start(f32[1536,256]{1,0:T(8,128)S(1)} %collective-permute-done.7.refs_3_.refs_4_.a1), channel_id=1, source_target_pairs={{2,1},{1,0},{6,5},{5,4},{10,9},{9,8},{14,13},{13,12},{18,17},{17,1... | collective-permute-start | bytes 4718600 | tf_op jit(solution)/shard_map/ppermute | solution.py:77
  295.2 84.4 %collective-permute-start.12 = (f32[1536,256]{1,0:T(8,128)}, f32[1536,256]{1,0:T(8,128)}, u32[]{:S(2)}, u32[]{:S(2)}) collective-permute-start(f32[1536,256]{1,0:T(8,128)} %collective-permute-done.2.refs_2_.refs_3_.b1), channel_id=1, source_target_pairs={{1,2},{2,3},{5,6},{6,7},{9,10},{10,11},{13,14},{14,15},{17,18},{18... | collective-permute-start | bytes 4718600 | tf_op jit(solution)/shard_map/ppermute | solution.py:77
  297.1 82.5 %collective-permute-start.13 = (f32[1536,256]{1,0:T(8,128)}, f32[1536,256]{1,0:T(8,128)}, u32[]{:S(2)}, u32[]{:S(2)}) collective-permute-start(f32[1536,256]{1,0:T(8,128)} %collective-permute-done.3.refs_3_.refs_4_.a1), channel_id=1, source_target_pairs={{2,1},{1,0},{6,5},{5,4},{10,9},{9,8},{14,13},{13,12},{18,17},{17,1... | collective-permute-start | bytes 4718600 | tf_op jit(solution)/shard_map/ppermute | solution.py:77
  298.4 87.2 %collective-permute-start.8 = (f32[1536,256]{1,0:T(8,128)}, f32[1536,256]{1,0:T(8,128)}, u32[]{:S(2)}, u32[]{:S(2)}) collective-permute-start(f32[1536,256]{1,0:T(8,128)} %get-tuple-element.32), channel_id=1, source_target_pairs={{0,1},{3,2},{4,5},{7,6},{8,9},{11,10},{12,13},{15,14},{16,17},{19,... | collective-permute-start | bytes 4718600 | tf_op jit(solution)/shard_map/ppermute | solution.py:77
  308.0 77.6 %collective-permute-start.10 = (f32[1536,256]{1,0:T(8,128)}, f32[1536,256]{1,0:T(8,128)}, u32[]{:S(2)}, u32[]{:S(2)}) collective-permute-start(f32[1536,256]{1,0:T(8,128)} %collective-permute-done.1.refs_3_.refs_4_.a1), channel_id=1, source_target_pairs={{2,1},{1,0},{6,5},{5,4},{10,9},{9,8},{14,13},{13,12},{18,17},{17,1... | collective-permute-start | bytes 4718600 | tf_op jit(solution)/shard_map/ppermute | solution.py:77
  310.5 75.2 %collective-permute-start.9 = (f32[1536,256]{1,0:T(8,128)}, f32[1536,256]{1,0:T(8,128)}, u32[]{:S(2)}, u32[]{:S(2)}) collective-permute-start(f32[1536,256]{1,0:T(8,128)} %collective-permute-done.refs_2_.refs_3_.b1), channel_id=1, source_target_pairs={{1,2},{2,3},{5,6},{6,7},{9,10},{10,11},{13,14},{14,15},{17,18},{18... | collective-permute-start | bytes 4718600 | tf_op jit(solution)/shard_map/ppermute | solution.py:77
  393.7 153.7 %all-gather.6.cloned.1.call-start = ((), (), s32[]{:S(2)}) async-start(), calls=%async_computation.3 | async-start | bytes 4718592 | tf_op jit(solution)/shard_map/all_gather | solution.py:351
  514.7 68.3 %collective-permute-start.30 = (f32[1536,256]{1,0:T(8,128)}, f32[1536,256]{1,0:T(8,128)}, u32[]{:S(2)}, u32[]{:S(2)}) collective-permute-start(f32[1536,256]{1,0:T(8,128)} %copy-done.12), channel_id=1, source_target_pairs={{2,3},{6,7},{10,11},{14,15},{18,19},{22,23},{26,27},{30,31}} | collective-permute-start | bytes 4718600 | tf_op jit(solution)/shard_map/ppermute | solution.py:77
  516.6 70.0 %collective-permute-start.31 = (f32[1536,256]{1,0:T(8,128)}, f32[1536,256]{1,0:T(8,128)}, u32[]{:S(2)}, u32[]{:S(2)}) collective-permute-start(f32[1536,256]{1,0:T(8,128)} %copy-done.15), channel_id=1, source_target_pairs={{1,0},{5,4},{9,8},{13,12},{17,16},{21,20},{25,24},{29,28}} | collective-permute-start | bytes 4718600 | tf_op jit(solution)/shard_map/ppermute | solution.py:77
  517.8 84.8 %collective-permute-start.28 = (f32[1536,256]{1,0:T(8,128)}, f32[1536,256]{1,0:T(8,128)}, u32[]{:S(2)}, u32[]{:S(2)}) collective-permute-start(f32[1536,256]{1,0:T(8,128)} %collective-permute-done.12.refs_5_.b2), channel_id=1, source_target_pairs={{2,3},{6,7},{10,11},{14,15},{18,19},{22,23},{26,27},{30,31}} | collective-permute-start | bytes 4718600 | tf_op jit(solution)/shard_map/ppermute | solution.py:77
  565.9 70.3 %collective-permute-start.26 = (f32[1536,256]{1,0:T(8,128)}, f32[1536,256]{1,0:T(8,128)S(1)}, u32[]{:S(2)}, u32[]{:S(2)}) collective-permute-start(f32[1536,256]{1,0:T(8,128)} %collective-permute-done.9.refs_5_.b2), channel_id=1, source_target_pairs={{2,3},{6,7},{10,11},{14,15},{18,19},{22,23},{26,27},{30,31}} | collective-permute-start | bytes 4718600 | tf_op jit(solution)/shard_map/ppermute | solution.py:77
  583.1 68.1 %collective-permute-start.27 = (f32[1536,256]{1,0:T(8,128)}, f32[1536,256]{1,0:T(8,128)S(1)}, u32[]{:S(2)}, u32[]{:S(2)}) collective-permute-start(f32[1536,256]{1,0:T(8,128)} %collective-permute-done.10.refs_6_.a2), channel_id=1, source_target_pairs={{1,0},{5,4},{9,8},{13,12},{17,16},{21,20},{25,24},{29,28}} | collective-permute-start | bytes 4718600 | tf_op jit(solution)/shard_map/ppermute | solution.py:77
  (44 other events, 1410.2 us)
Sparse Core Ops, SparseCore 0:
  35.8 106.3 all-gather.3
  393.8 64.0 reduce-scatter.1
  511.7 35.6 all-gather.5

commit v2 on v1

--- a/solution.py
+++ b/solution.py
@@ -77,55 +77,50 @@
     return lax.ppermute(value, "mode", pairs)
 
 
-def split_outside(value):
-    high = lax.reduce_precision(value, 8, 7)
-    return high.astype(jnp.bfloat16), lax.reduce_precision(value - high, 8, 7).astype(jnp.bfloat16)
-
-
 def split(value):
     high = value.astype(jnp.bfloat16)
     low = (value - high.astype(jnp.float32)).astype(jnp.bfloat16)
     return high, low
 
 
-def final_kernel(first_row, pieces, z_ref, own, b1, b2, b3, a1, a2, a3, *rest):
+def final_kernel(first_row, pieces, parts, z_ref, own, *rest):
+    lists = [rest[6 * c : 6 * c + 6] for c in range(parts)]
     out_ref, x_buf, x3, sems = rest[-4:]
     step = pl.program_id(0)
     steps = pl.num_programs(0)
+    each = steps // parts
     layer = lax.axis_index("mode")
     width = own.shape[1]
     rows = x_buf.shape[1]
-    below = {1: b1, 2: b2, 3: b3}
-    above = {1: a1, 2: a2, 3: a3}
-
-    def fetch(at, slot):
-        for piece in range(pieces):
-            for here in range(pieces):
-
-                @pl.when(layer == here)
-                def _():
+
+    def fetch(at, slot, chosen):
+        for c in chosen:
+            for piece in range(pieces):
+                for here in range(pieces):
                     delta = piece - here
-                    begin = at * rows
-                    if delta == 0:
-                        source = own
-                        begin = first_row + begin
-                    else:
-                        source = above[delta] if delta > 0 else below[-delta]
-                    pltpu.make_async_copy(
-                        source.at[pl.ds(begin, rows), :],
-                        x_buf.at[slot, :, pl.ds(piece * width, width)],
-                        sems.at[slot, piece],
-                    ).start()
+
+                    @pl.when((layer == here) & (at >= c * each) & (at < (c + 1) * each))
+                    def _():
+                        if delta == 0:
+                            source, begin = own, first_row + at * rows
+                        else:
+                            source = lists[c][2 + delta if delta > 0 else -delta - 1]
+                            begin = (at - c * each) * rows
+                        pltpu.make_async_copy(
+                            source.at[pl.ds(begin, rows), :],
+                            x_buf.at[slot, :, pl.ds(piece * width, width)],
+                            sems.at[slot, piece],
+                        ).start()
 
     slot = lax.rem(step, 2)
 
     @pl.when(step == 0)
     def _():
-        fetch(0, 0)
+        fetch(step, 0, (0,))
 
     @pl.when(step + 1 < steps)
     def _():
-        fetch(step + 1, 1 - slot)
+        fetch(step + 1, 1 - slot, range(parts))
 
     for piece in range(pieces):
         pltpu.make_async_copy(
@@ -219,23 +214,25 @@
     )(*operands)
 
 
-def final_chunk(index, z3, own, lists, previous, columns):
+def final_chunk(index, z3, own, groups, previous, columns):
     rows = z3.shape[0]
     width = own.shape[1]
     pieces = z3.shape[1] // (3 * width)
+    lists = [v for group in groups for v in group]
     first_row = index * lists[0].shape[0]
-    steps = lists[0].shape[0] // tile
+    steps = len(groups) * (lists[0].shape[0] // tile)
     anywhere = pl.BlockSpec(memory_space=pl.ANY)
     operands = [z3, own, *lists]
-    specs = [pl.BlockSpec(z3.shape, lambda i: (0, 0), pipeline_mode=pl.Buffered(1))] + [anywhere] * 7
+    specs = [pl.BlockSpec(z3.shape, lambda i: (0, 0), pipeline_mode=pl.Buffered(1))]
+    specs += [anywhere] * (1 + len(lists))
     aliases = {}
     if previous is not None:
+        aliases = {len(operands): 0}
         operands.append(previous)
         specs.append(anywhere)
-        aliases = {8: 0}
     first_block = first_row // tile
     return pl.pallas_call(
-        functools.partial(final_kernel, first_row, pieces),
+        functools.partial(final_kernel, first_row, pieces, len(groups)),
         grid=(steps,),
         in_specs=specs,
         out_specs=pl.BlockSpec((rows, tile), lambda i: (0, first_block + i)),
@@ -248,12 +245,260 @@
         input_output_aliases=aliases,
         compiler_params=pltpu.CompilerParams(vmem_limit_bytes=40 * 2**20),
         cost_estimate=pl.CostEstimate(
-            flops=6 * rows * z3.shape[1] // 3 * steps * tile,
+            flops=2 * rows * z3.shape[1] * steps * tile,
             bytes_accessed=4 * steps * tile * (rows + pieces * width),
             transcendentals=0,
         ),
         name="final_chunk",
     )(*operands)
+
+
+MESH = pl.DeviceIdType.MESH
+
+
+def send(source, target, send_sem, recv_sem, device):
+    return pltpu.make_async_remote_copy(
+        src_ref=source,
+        dst_ref=target,
+        send_sem=send_sem,
+        recv_sem=recv_sem,
+        device_id=device,
+        device_id_type=MESH,
+    )
+
+
+def greet(device):
+    pl.semaphore_signal(pltpu.get_barrier_semaphore(), inc=1, device_id=device, device_id_type=MESH)
+
+
+def chain_kernel(
+    chips, gram, table, eigen_j, eigen_i, ids_j, ids_i, slope_j, mine,
+    met, total, came, w_tiles, w_high, w_low, zt, got, land,
+    w_sems, met_send, met_recv, came_send, came_recv, z_send, z_recv,
+):
+    me = lax.axis_index("harm")
+    layer = lax.axis_index("mode")
+    core = lax.rem(me, 2)
+    chip = lax.div(me, 2)
+    partner = me + 1 - 2 * core
+    middle = (layer == 1) | (layer == 2)
+    span = met.shape[1]
+    tiles, rows = w_tiles.shape[:2]
+    peer = 3 - layer
+    end = jnp.where(layer == 1, 0, 3)
+    keep = jnp.where(layer == 1, 0, 2)
+    slot = jnp.where(layer == 1, 0, 1)
+
+    @pl.when(middle)
+    def _():
+        greet({"harm": partner})
+        for d in range(1, chips):
+            greet({"harm": lax.rem(chip + d, chips) * 2 + core})
+        greet({"mode": layer - 1})
+        greet({"mode": layer + 1})
+        pl.semaphore_wait(pltpu.get_barrier_semaphore(), chips + 2)
+        first = [
+            send(
+                gram.at[pl.ds((2 * q + 1 - core) * span, span), :],
+                met.at[q],
+                met_send.at[q],
+                met_recv.at[q],
+                {"harm": partner},
+            )
+            for q in range(chips)
+        ]
+        for copy in first:
+            copy.start()
+        loads = [
+            pltpu.make_async_copy(table.at[pl.ds(t * rows, rows), :], w_tiles.at[t], w_sems.at[t])
+            for t in range(tiles)
+        ]
+        for load in loads:
+            load.start()
+        for q in range(chips):
+            first[q].wait()
+            total[q] = gram[pl.ds((2 * q + core) * span, span), :] + met[q]
+        second = []
+        for d in range(1, chips):
+            q = lax.rem(chip + d, chips)
+            second.append(
+                send(
+                    total.at[q],
+                    came.at[d - 1],
+                    came_send.at[d - 1],
+                    came_recv.at[d - 1],
+                    {"harm": q * 2 + core},
+                )
+            )
+            second[-1].start()
+        for load in loads:
+            load.wait()
+
+        def cut(t, carry):
+            high, low = split(w_tiles[t])
+            w_high[t] = high
+            w_low[t] = low
+            return carry
+
+        lax.fori_loop(0, tiles, cut, 0)
+        for copy in second:
+            copy.wait()
+        value = total[chip]
+        for d in range(1, chips):
+            value = value + came[d - 1]
+        differ = eigen_j[...] - eigen_i[...]
+        value = value * (differ / (differ * differ + regular))
+        value = value + jnp.where(ids_j[...] == ids_i[...], slope_j[...], 0.0)
+        high, low = split(value)
+        both = jnp.concatenate([high, low], axis=0)
+        per = zt.shape[2] // rows
+        nt = (((1,), (1,)), ((), ()))
+
+        def mix(t, carry):
+            part = lax.dot_general(both, w_high[t], nt, preferred_element_type=jnp.float32)
+            rest = lax.dot_general(high, w_low[t], nt, preferred_element_type=jnp.float32)
+            zt[t // per, :, pl.ds(pl.multiple_of(lax.rem(t, per) * rows, rows), rows)] = (
+                part[:span] + part[span:] + rest
+            )
+            return carry
+
+        lax.fori_loop(0, tiles, mix, 0)
+        swap = send(zt.at[pl.ds(2 - keep, 2)], got, z_send.at[0], z_recv.at[0], {"mode": peer})
+        swap.start()
+        out = send(zt.at[end], land.at[slot], z_send.at[1], z_recv.at[1], {"mode": end})
+        out.start()
+        mine[slot] = zt[layer]
+        swap.wait()
+        pass_on = send(
+            got.at[end - keep], land.at[1 - slot], z_send.at[2], z_recv.at[2], {"mode": end}
+        )
+        pass_on.start()
+        mine[1 - slot] = got[layer - keep]
+        out.wait_send()
+        pass_on.wait_send()
+
+    @pl.when(jnp.logical_not(middle))
+    def _():
+        inward = jnp.where(layer == 0, 1, 2)
+        side = jnp.where(layer == 0, 0, 1)
+        greet({"mode": inward})
+        pl.semaphore_wait(pltpu.get_barrier_semaphore(), 1)
+        send(zt.at[0], land.at[side], z_send.at[1], z_recv.at[1], {"mode": inward}).wait_recv()
+        send(zt.at[0], land.at[1 - side], z_send.at[2], z_recv.at[2], {"mode": inward}).wait_recv()
+        mine[...] = land[...]
+
+
+def chain(gram, table, eigen_j, eigen_i, ids_j, ids_i, slope_j, harm_count, mode_count):
+    chips = harm_count // 2
+    span = gram.shape[0] // harm_count
+    modes = gram.shape[1]
+    rows = table.shape[0] // mode_count
+    cut = 512
+    tiles = table.shape[0] // cut
+    vmem = pl.BlockSpec(memory_space=pltpu.VMEM)
+    return pl.pallas_call(
+        functools.partial(chain_kernel, chips),
+        in_specs=[vmem, pl.BlockSpec(memory_space=pl.ANY)] + [vmem] * 5,
+        out_specs=vmem,
+        out_shape=jax.ShapeDtypeStruct((2, span, rows), jnp.float32),
+        scratch_shapes=[
+            pltpu.VMEM((chips, span, modes), jnp.float32),
+            pltpu.VMEM((chips, span, modes), jnp.float32),
+            pltpu.VMEM((chips - 1, span, modes), jnp.float32),
+            pltpu.VMEM((tiles, cut, modes), jnp.float32),
+            pltpu.VMEM((tiles, cut, modes), jnp.bfloat16),
+            pltpu.VMEM((tiles, cut, modes), jnp.bfloat16),
+            pltpu.VMEM((mode_count, span, rows), jnp.float32),
+            pltpu.VMEM((2, span, rows), jnp.float32),
+            pltpu.VMEM((2, span, rows), jnp.float32),
+            pltpu.SemaphoreType.DMA((tiles,)),
+            pltpu.SemaphoreType.DMA((chips,)),
+            pltpu.SemaphoreType.DMA((chips,)),
+            pltpu.SemaphoreType.DMA((chips - 1,)),
+            pltpu.SemaphoreType.DMA((chips - 1,)),
+            pltpu.SemaphoreType.DMA((3,)),
+            pltpu.SemaphoreType.DMA((3,)),
+        ],
+        compiler_params=pltpu.CompilerParams(
+            collective_id=1, has_side_effects=True, vmem_limit_bytes=52 * 2**20
+        ),
+        name="chain",
+    )(gram, table, eigen_j, eigen_i, ids_j, ids_i, slope_j)
+
+
+def spread_kernel(chips, width, mine, z_ref, land, out_send, out_recv, pair_send, pair_recv):
+    me = lax.axis_index("harm")
+    core = lax.rem(me, 2)
+    chip = lax.div(me, 2)
+    partner = me + 1 - 2 * core
+    greet({"harm": partner})
+    for d in range(1, chips):
+        greet({"harm": lax.rem(chip + d, chips) * 2 + core})
+    pl.semaphore_wait(pltpu.get_barrier_semaphore(), chips)
+    outward = []
+    for d in range(1, chips):
+        outward.append(
+            send(
+                mine,
+                land.at[chip, core],
+                out_send.at[d - 1],
+                out_recv.at[d - 1],
+                {"harm": lax.rem(chip + d, chips) * 2 + core},
+            )
+        )
+        outward[-1].start()
+    paired = [send(mine, land.at[chip, core], pair_send.at[0], pair_recv.at[0], {"harm": partner})]
+    paired[0].start()
+    land[chip, core] = mine[...]
+    for d in range(1, chips):
+        origin = lax.rem(chip + chips - d, chips)
+        outward[d - 1].wait()
+        paired.append(
+            send(
+                land.at[origin, core],
+                land.at[origin, core],
+                pair_send.at[d],
+                pair_recv.at[d],
+                {"harm": partner},
+            )
+        )
+        paired[-1].start()
+    for copy in paired:
+        copy.wait()
+    depth = z_ref.shape[1] // 3
+    half = chips // 2
+    for q in range(chips):
+        for side in range(2):
+            piece = 1 - q // half if side == 0 else 2 + q // half
+            block = jnp.concatenate([land[q, 0, side], land[q, 1, side]], axis=0).T
+            high, low = split(block)
+            at = piece * width + (q % half) * block.shape[1]
+            size = block.shape[1]
+            z_ref[:, at : at + size] = high
+            z_ref[:, depth + at : depth + at + size] = low
+            z_ref[:, 2 * depth + at : 2 * depth + at + size] = high
+
+
+def spread(mine, harm_count, mode_count, width):
+    chips = harm_count // 2
+    vmem = pl.BlockSpec(memory_space=pltpu.VMEM)
+    return pl.pallas_call(
+        functools.partial(spread_kernel, chips, width),
+        in_specs=[vmem],
+        out_specs=vmem,
+        out_shape=jax.ShapeDtypeStruct((mine.shape[2], 3 * mode_count * width), jnp.bfloat16),
+        scratch_shapes=[
+            pltpu.VMEM((chips, 2, *mine.shape), jnp.float32),
+            pltpu.SemaphoreType.DMA((chips - 1,)),
+            pltpu.SemaphoreType.DMA((chips - 1,)),
+            pltpu.SemaphoreType.DMA((chips,)),
+            pltpu.SemaphoreType.DMA((chips,)),
+        ],
+        compiler_params=pltpu.CompilerParams(
+            collective_id=2, has_side_effects=True, vmem_limit_bytes=40 * 2**20
+        ),
+        name="spread",
+    )(mine)
 
 
 def slab_order(slab_rows, row_count, harm_count, harm_index):
@@ -275,7 +520,6 @@
     harm = lax.axis_index("harm")
     layer = lax.axis_index("mode")
     height, width = mode_vectors.shape
-    total = slab_rows.shape[0]
     lower = layer <= 1
     own = jnp.split(mode_vectors, chunks, 0)
     slope = jnp.split(cotangent, chunks, 0)
@@ -322,7 +566,6 @@
         )
     top = jnp.concatenate([near[0], far_parts[0]], axis=1)
     gram = jnp.concatenate([top, far_parts[1]], axis=0)
-    gram = lax.psum_scatter(gram, "harm", scatter_dimension=0, tiled=True)
 
     span = 2 * width // harm_count
     half = harm_count // 2
@@ -336,28 +579,16 @@
     eigen_j = lax.dynamic_slice_in_dim(eigenvalues, first_col, span)
     slope_j = lax.dynamic_slice_in_dim(eigen_cotangent, first_col, span)
     col_ids = first_col + jnp.arange(span, dtype=jnp.int32)
-    differ = eigen_j[:, None] - eigen_i[None, :]
-    factor = differ / (differ * differ + regular)
-    weighted = factor * gram + jnp.where(col_ids[:, None] == row_ids[None, :], slope_j[:, None], 0.0)
-
-    zt = product(weighted, w_slab, 1, 1).reshape(span, mode_count, total // mode_count)
-    keep = jnp.where(lower, zt[:, :2], zt[:, 2:])
-    give = jnp.where(lower, zt[:, 2:], zt[:, :2])
-    got = shift(give, [(1, 2), (2, 1)])
-    both = jnp.stack([jnp.where(lower, keep, got), jnp.where(lower, got, keep)])
-    outer = shift(jnp.where(lower, both[:, :, 0], both[:, :, 1]), [(1, 0), (2, 3)])
-    inner = jnp.where(lower, both[:, :, 1], both[:, :, 0])
-    mine = jnp.where((layer == 0) | (layer == last), outer, inner)
-    every = lax.all_gather(mine, "harm", axis=0, tiled=False)
-    zt = jnp.concatenate(
-        [every[half:, 0], every[:half, 0], every[:half, 1], every[half:, 1]], axis=0
-    ).reshape(mode_count * width, total // mode_count)
-    high, low = split_outside(zt.T)
-    z3 = jnp.concatenate([high, low, high], axis=1)
+    mine = chain(
+        gram, w_slab, eigen_j[:, None], eigen_i[None, :], col_ids[:, None], row_ids[None, :],
+        slope_j[:, None], harm_count, mode_count,
+    )
+    z3 = spread(mine, harm_count, mode_count, width)
 
     out = None
-    for c in range(chunks):
-        out = final_chunk(c, z3, mode_vectors, [b1[c], b2[c], b3[c], a1[c], a2[c], a3[c]], out, height)
+    lists = list(zip(b1, b2, b3, a1, a2, a3))
+    for first, count in ((0, 2), (2, 1), (3, 1)):
+        out = final_chunk(first, z3, mode_vectors, lists[first : first + count], out, height)
     return out
 
 

time: 682 us -> 654 us (0.959)
  Pallas kernels: 99.6 us -> 173 us
  waiting for transfers between devices: 356 us -> 306 us
  matrix products: 14.7 us -> 0 us
  other arithmetic: 21.1 us -> 8.56 us
  local copies, waits for them, and re-layouts: 76.6 us -> 65.4 us
    pallas_call x4 -> x5, Pallas kernels: 64.1 us -> 136 us  [the longest x3 58.7 us: final_chunk(): pl.pallas_call(functools.partial(final_kernel, first_row, pieces, len(gro...]
    reduce_scatter x1 -> x0, waiting for transfers between devices: 62.6 us -> none  [line_body(): gram = lax.psum_scatter(gram, 'harm', scatter_dimension=0, tiled=True)]
    ppermute x34 -> x32, waiting for transfers between devices: 266 us -> 306 us  [shift(): return lax.ppermute(value, 'mode', pairs)]
    all_gather x1 -> x0, waiting for transfers between devices: 27.6 us -> none  [line_body(): every = lax.all_gather(mine, 'harm', axis=0, tiled=False)]
    dot_general x1 -> x0, matrix products: 14.7 us -> none  [product(): lax.dot_general(left, right, (((left_dim,), (right_dim,)), ((), ())), pre...]
    reshape x2 -> x0, local copies, waits for them, and re-layouts: 8.23 us -> none  [the longest x1 5.33 us: line_body(): zt = jnp.concatenate([every[half:, 0], every[:half, 0], every[:half, 1],...]
    ppermute x34 -> x32, starting transfers between devices: 91.4 us -> 84.8 us  [shift(): return lax.ppermute(value, 'mode', pairs)]
    unnamed x62 -> x66, local copies, waits for them, and re-layouts: 21.5 us -> 28 us
  transfers between devices with their start and end apart: 37 -> 33, of which waited for: 14 -> 13; matrix products, arithmetic and copies ran while one was open for 8% -> 5% of each run, Pallas kernels for 11% -> 24%
where the time goes in v2:
time: 654 us; the launch traced here: 652 us
  waiting for transfers between devices  306 us (47%)
  Pallas kernels  173 us (26%)
  starting transfers between devices  84.8 us (13%)
  local copies, waits for them, and re-layouts  65.4 us (10%)
  between operations  14.2 us (2%)
  other arithmetic  8.56 us (1%)
    ppermute x32, waiting for transfers between devices, shift(): return lax.ppermute(value, 'mode', pairs)  306 us
    ppermute x32, starting transfers between devices, shift(): return lax.ppermute(value, 'mode', pairs)  84.8 us
    pallas_call x3, Pallas kernels, final_chunk(): pl.pallas_call(functools.partial(final_kernel, first_row, pieces, len(gro...  58.7 us
    pallas_call x1, Pallas kernels, chain(): pl.pallas_call(functools.partial(chain_kernel, chips), in_specs=[vmem, pl...  47.8 us
    pallas_call x8, Pallas kernels, gram_chunk(): pl.pallas_call(functools.partial(gram_kernel, len(lefts), fresh, plan), g...  37.1 us
    pallas_call x1, Pallas kernels, spread(): pl.pallas_call(functools.partial(spread_kernel, chips, width), in_specs=[...  29.4 us
    unnamed x66, local copies, waits for them, and re-layouts  28 us
    gather x1, local copies, waits for them, and re-layouts, line_body(): w_slab = jnp.take(w_every, position, axis=0, mode='clip')  27.9 us
  transfers between devices with their start and end apart: 33, of which 13 were waited for; matrix products, arithmetic and copies ran while one was open for 5% of the time, Pallas kernels for 24%

profile of v2, /device:TPU:0, one launch (start us, length us, event | category | flops | bytes accessed | tf_op | source)
XLA Modules:
  0.0 652.4 jit_solution(8289895254220235258)
XLA Ops:
  22.2 10.4 %collective-permute-done.15 = f32[512,256]{1,0:T(8,128)S(1)} collective-permute-done((f32[512,256]{1,0:T(8,128)S(1)}, f32[512,256]{1,0:T(8,128)S(1)}, u32[]{:S(2)}, u32[]{:S(2)}) %collective-permute-start.15) | collective-permute-done | bytes 524320 | tf_op jit(solution)/shard_map/ppermute | solution.py:77
  39.2 21.1 %collective-permute-start.14 = (f32[1536,256]{1,0:T(8,128)S(1)}, f32[1536,256]{1,0:T(8,128)S(1)}, u32[]{:S(2)}, u32[]{:S(2)}) collective-permute-start(f32[1536,256]{1,0:T(8,128)S(1)} %get-tuple-element.30), channel_id=1, source_target_pairs={{0,1},{3,2},{4,5},{7,6},{8,9},{11,10},{12,13},{15,14},{16,17},{19,... | collective-permute-start | bytes 4718600 | tf_op jit(solution)/shard_map/ppermute | solution.py:77
  70.6 24.3 %collective-permute-done.14.refs_1_ = f32[1536,256]{1,0:T(8,128)S(1)} collective-permute-done((f32[1536,256]{1,0:T(8,128)S(1)}, f32[1536,256]{1,0:T(8,128)S(1)}, u32[]{:S(2)}, u32[]{:S(2)}) %collective-permute-start.14) | collective-permute-done | bytes 1572896 | tf_op jit(solution)/shard_map/ppermute | solution.py:77
  97.4 31.3 %collective-permute-done.6.refs_2_.refs_3_.rest_0_ = f32[1536,256]{1,0:T(8,128)S(1)} collective-permute-done((f32[1536,256]{1,0:T(8,128)S(1)}, f32[1536,256]{1,0:T(8,128)S(1)}, u32[]{:S(2)}, u32[]{:S(2)}) %collective-permute-start.6) | collective-permute-done | bytes 1572896 | tf_op jit(solution)/shard_map/ppermute | solution.py:77
  134.5 27.9 %collective-permute-done.21.refs_1_ = f32[1536,256]{1,0:T(8,128)S(1)} collective-permute-done((f32[1536,256]{1,0:T(8,128)S(1)}, f32[1536,256]{1,0:T(8,128)S(1)}, u32[]{:S(2)}, u32[]{:S(2)}) %collective-permute-start.21) | collective-permute-done | bytes 1572896 | tf_op jit(solution)/shard_map/ppermute | solution.py:77
  168.1 28.0 %collective-permute-done.4.refs_2_.refs_3_.rest_6_ = f32[1536,256]{1,0:T(8,128)} collective-permute-done((f32[1536,256]{1,0:T(8,128)S(1)}, f32[1536,256]{1,0:T(8,128)}, u32[]{:S(2)}, u32[]{:S(2)}) %collective-permute-start.4) | collective-permute-done | bytes 1572896 | tf_op jit(solution)/shard_map/ppermute | solution.py:77
  197.4 6.3 collective-permute-start
  203.7 26.1 %collective-permute-done.2.refs_2_.refs_3_.rest_0_ = f32[1536,256]{1,0:T(8,128)S(1)} collective-permute-done((f32[1536,256]{1,0:T(8,128)S(1)}, f32[1536,256]{1,0:T(8,128)S(1)}, u32[]{:S(2)}, u32[]{:S(2)}) %collective-permute-start.2) | collective-permute-done | bytes 1572896 | tf_op jit(solution)/shard_map/ppermute | solution.py:77
  237.3 26.2 %collective-permute-done.11.refs_1_ = f32[1536,256]{1,0:T(8,128)S(1)} collective-permute-done((f32[1536,256]{1,0:T(8,128)S(1)}, f32[1536,256]{1,0:T(8,128)S(1)}, u32[]{:S(2)}, u32[]{:S(2)}) %collective-permute-start.11) | collective-permute-done | bytes 1572896 | tf_op jit(solution)/shard_map/ppermute | solution.py:77
  268.9 28.3 %collective-permute-done.refs_2_.refs_3_.rest_0_ = f32[1536,256]{1,0:T(8,128)} collective-permute-done((f32[1536,256]{1,0:T(8,128)S(1)}, f32[1536,256]{1,0:T(8,128)}, u32[]{:S(2)}, u32[]{:S(2)}) %collective-permute-start) | collective-permute-done | bytes 1572896 | tf_op jit(solution)/shard_map/ppermute | solution.py:77
  298.5 29.3 %collective-permute-done.8.refs_1_ = f32[1536,256]{1,0:T(8,128)S(1)} collective-permute-done((f32[1536,256]{1,0:T(8,128)S(1)}, f32[1536,256]{1,0:T(8,128)S(1)}, u32[]{:S(2)}, u32[]{:S(2)}) %collective-permute-start.8) | collective-permute-done | bytes 1572896 | tf_op jit(solution)/shard_map/ppermute | solution.py:77
  354.9 16.4 %collective-permute-done.13.refs_6_.rest_4_ = f32[1536,256]{1,0:T(8,128)} collective-permute-done((f32[1536,256]{1,0:T(8,128)S(1)}, f32[1536,256]{1,0:T(8,128)}, u32[]{:S(2)}, u32[]{:S(2)}) %collective-permute-start.13) | collective-permute-done | bytes 1572896 | tf_op jit(solution)/shard_map/ppermute | solution.py:77
  373.1 31.9 %collective-permute-done.10.refs_6_.rest_4_ = f32[1536,256]{1,0:T(8,128)} collective-permute-done((f32[1536,256]{1,0:T(8,128)}, f32[1536,256]{1,0:T(8,128)}, u32[]{:S(2)}, u32[]{:S(2)}) %collective-permute-start.10) | collective-permute-done | bytes 1572896 | tf_op jit(solution)/shard_map/ppermute | solution.py:77
  421.0 27.9 %gather_fusion.1 = f32[4096,1024]{1,0:T(8,128)} fusion(f32[4096,1024]{1,0:T(8,128)} %all-gather.2.cloned.1.call-done, s32[4096]{0:T(1024)S(1)} %get-tuple-element.33), kind=kCustom, calls=%fused_computation.1 | custom fusion | bytes 33570816 | tf_op jit(solution)/shard_map/jit(_take)/gather | solution.py:543
  454.3 6.1 gram_chunk.13
  460.4 5.5 gram_chunk.14
  466.7 6.1 gram_chunk.15
  474.4 47.8 %chain.1.mine = f32[2,64,1024]{2,1,0:T(8,128)S(1)} custom-call(f32[512,1024]{1,0:T(8,128)} %pad_maximum_fusion.1.gram, f32[4096,1024]{1,0:T(8,128)} %gather_fusion.1, f32[64,1]{1,0:T(8,128)S(1)} %copy.13.eigen_j, f32[1,1024]{1,0:T(1,128)S(1)} %bitcast.21, s32[64,1]{1,0:T(8,128)S(1)} %iota_add_fusion.ids_j, s32[1,1024]{1,0:T(1,128)S(1)} %bitcast.22, ...), custom_call_target="tpu_custom_call" | custom-call | tf_op jit(solution)/shard_map/chain/pallas_call | solution.py:399
  522.3 29.4 %spread.1.z_ref = bf16[1024,3072]{1,0:T(8,128)(2,1)S(1)} custom-call(f32[2,64,1024]{2,1,0:T(8,128)S(1)} %chain.1.mine), custom_call_target="tpu_custom_call" | custom-call | tf_op jit(solution)/shard_map/spread/pallas_call | solution.py:485
  558.0 26.7 %final_chunk.3.rest_6_ = f32[1024,6144]{1,0:T(8,128)} custom-call(bf16[1024,3072]{1,0:T(8,128)(2,1)} %copy-done.3, f32[6144,256]{1,0:T(8,128)} %own.5, f32[1536,256]{1,0:T(8,128)S(1)} %copy-done.7, f32[1536,256]{1,0:T(8,128)} %collective-permute-done.22.refs_5_.rest_1_, f32[1536,256]{1,0:T(8,128)} %collective-permute-done.28.rest_2_, ...), custom_call_target="tpu_custom_call" | custom-call | flops 19327352832 | bytes 25165824 | tf_op jit(solution)/shard_map/final_chunk/pallas_call | solution.py:234
  584.7 9.0 %collective-permute-done.27.rest_5_ = f32[1536,256]{1,0:T(8,128)S(1)} collective-permute-done((f32[1536,256]{1,0:T(8,128)}, f32[1536,256]{1,0:T(8,128)S(1)}, u32[]{:S(2)}, u32[]{:S(2)}) %collective-permute-start.27) | collective-permute-done | bytes 1572896 | tf_op jit(solution)/shard_map/ppermute | solution.py:77
  593.7 16.0 %final_chunk.4.rest_6_ = f32[1024,6144]{1,0:T(8,128)} custom-call(bf16[1024,3072]{1,0:T(8,128)(2,1)} %copy-done.3, f32[6144,256]{1,0:T(8,128)} %own.5, f32[1536,256]{1,0:T(8,128)S(1)} %collective-permute-done.2.refs_2_.refs_3_.rest_0_, f32[1536,256]{1,0:T(8,128)} %collective-permute-done.12.refs_5_.rest_1_, ...), custom_call_target="tpu_custom_call", output_to_operand_aliasing={{}: (8, {})} | custom-call | flops 9663676416 | bytes 12582912 | tf_op jit(solution)/shard_map/final_chunk/pallas_call | solution.py:234
  609.7 17.1 %collective-permute-done.25.rest_5_ = f32[1536,256]{1,0:T(8,128)S(1)} collective-permute-done((f32[1536,256]{1,0:T(8,128)}, f32[1536,256]{1,0:T(8,128)S(1)}, u32[]{:S(2)}, u32[]{:S(2)}) %collective-permute-start.25) | collective-permute-done | bytes 1572896 | tf_op jit(solution)/shard_map/ppermute | solution.py:77
  629.5 16.0 %final_chunk.5 = f32[1024,6144]{1,0:T(8,128)} custom-call(bf16[1024,3072]{1,0:T(8,128)(2,1)} %copy-done.3, f32[6144,256]{1,0:T(8,128)} %own.5, f32[1536,256]{1,0:T(8,128)} %collective-permute-done.refs_2_.refs_3_.rest_0_, f32[1536,256]{1,0:T(8,128)} %collective-permute-done.9.refs_5_.rest_1_, ...), custom_call_target="tpu_custom_call", output_to_operand_aliasing={{}: (8, {})} | custom-call | flops 9663676416 | bytes 12582912 | tf_op jit(solution)/shard_map/final_chunk/pallas_call | solution.py:234
  (150 shorter events, 122.9 us)
Async XLA Ops:
  6.5 414.4 %all-gather.2.cloned.1.call-start = ((), (), s32[]{:S(2)}) async-start(), calls=%async_computation | async-start | bytes 18874368 | tf_op jit(solution)/shard_map/all_gather | solution.py:542
  39.2 55.8 %collective-permute-start.14 = (f32[1536,256]{1,0:T(8,128)S(1)}, f32[1536,256]{1,0:T(8,128)S(1)}, u32[]{:S(2)}, u32[]{:S(2)}) collective-permute-start(f32[1536,256]{1,0:T(8,128)S(1)} %get-tuple-element.30), channel_id=1, source_target_pairs={{0,1},{3,2},{4,5},{7,6},{8,9},{11,10},{12,13},{15,14},{16,17},{19,... | collective-permute-start | bytes 4718600 | tf_op jit(solution)/shard_map/ppermute | solution.py:77
  60.8 67.9 %collective-permute-start.6 = (f32[1536,256]{1,0:T(8,128)S(1)}, f32[1536,256]{1,0:T(8,128)S(1)}, u32[]{:S(2)}, u32[]{:S(2)}) collective-permute-start(f32[1536,256]{1,0:T(8,128)S(1)} %get-tuple-element.25), channel_id=1, source_target_pairs={{0,1},{1,2},{2,3},{4,5},{5,6},{6,7},{8,9},{9,10},{10,11},{12,13},{... | collective-permute-start | bytes 4718600 | tf_op jit(solution)/shard_map/ppermute | solution.py:77
  62.1 71.0 %collective-permute-start.7 = (f32[1536,256]{1,0:T(8,128)S(1)}, f32[1536,256]{1,0:T(8,128)S(1)}, u32[]{:S(2)}, u32[]{:S(2)}) collective-permute-start(f32[1536,256]{1,0:T(8,128)S(1)} %get-tuple-element.25), channel_id=1, source_target_pairs={{1,0},{2,1},{3,2},{5,4},{6,5},{7,6},{9,8},{10,9},{11,10},{13,12},{... | collective-permute-start | bytes 4718600 | tf_op jit(solution)/shard_map/ppermute | solution.py:77
  63.4 98.9 %collective-permute-start.21 = (f32[1536,256]{1,0:T(8,128)S(1)}, f32[1536,256]{1,0:T(8,128)S(1)}, u32[]{:S(2)}, u32[]{:S(2)}) collective-permute-start(f32[1536,256]{1,0:T(8,128)S(1)} %get-tuple-element.29), channel_id=1, source_target_pairs={{0,1},{3,2},{4,5},{7,6},{8,9},{11,10},{12,13},{15,14},{16,17},{19,... | collective-permute-start | bytes 4718600 | tf_op jit(solution)/shard_map/ppermute | solution.py:77
  68.1 128.0 %collective-permute-start.4 = (f32[1536,256]{1,0:T(8,128)S(1)}, f32[1536,256]{1,0:T(8,128)}, u32[]{:S(2)}, u32[]{:S(2)}) collective-permute-start(f32[1536,256]{1,0:T(8,128)S(1)} %get-tuple-element.26), channel_id=1, source_target_pairs={{0,1},{1,2},{2,3},{4,5},{5,6},{6,7},{8,9},{9,10},{10,11},{12,13},{... | collective-permute-start | bytes 4718600 | tf_op jit(solution)/shard_map/ppermute | solution.py:77
  96.1 101.3 %collective-permute-start.5 = (f32[1536,256]{1,0:T(8,128)S(1)}, f32[1536,256]{1,0:T(8,128)}, u32[]{:S(2)}, u32[]{:S(2)}) collective-permute-start(f32[1536,256]{1,0:T(8,128)S(1)} %get-tuple-element.26), channel_id=1, source_target_pairs={{1,0},{2,1},{3,2},{5,4},{6,5},{7,6},{9,8},{10,9},{11,10},{13,12},{... | collective-permute-start | bytes 4718600 | tf_op jit(solution)/shard_map/ppermute | solution.py:77
  128.7 101.1 %collective-permute-start.2 = (f32[1536,256]{1,0:T(8,128)S(1)}, f32[1536,256]{1,0:T(8,128)S(1)}, u32[]{:S(2)}, u32[]{:S(2)}) collective-permute-start(f32[1536,256]{1,0:T(8,128)S(1)} %get-tuple-element.27), channel_id=1, source_target_pairs={{0,1},{1,2},{2,3},{4,5},{5,6},{6,7},{8,9},{9,10},{10,11},{12,13},{... | collective-permute-start | bytes 4718600 | tf_op jit(solution)/shard_map/ppermute | solution.py:77
  133.2 101.1 %collective-permute-start.3 = (f32[1536,256]{1,0:T(8,128)S(1)}, f32[1536,256]{1,0:T(8,128)S(1)}, u32[]{:S(2)}, u32[]{:S(2)}) collective-permute-start(f32[1536,256]{1,0:T(8,128)S(1)} %get-tuple-element.27), channel_id=1, source_target_pairs={{1,0},{2,1},{3,2},{5,4},{6,5},{7,6},{9,8},{10,9},{11,10},{13,12},{... | collective-permute-start | bytes 4718600 | tf_op jit(solution)/shard_map/ppermute | solution.py:77
  163.6 99.9 %collective-permute-start.11 = (f32[1536,256]{1,0:T(8,128)S(1)}, f32[1536,256]{1,0:T(8,128)S(1)}, u32[]{:S(2)}, u32[]{:S(2)}) collective-permute-start(f32[1536,256]{1,0:T(8,128)S(1)} %get-tuple-element.31), channel_id=1, source_target_pairs={{0,1},{3,2},{4,5},{7,6},{8,9},{11,10},{12,13},{15,14},{16,17},{19,... | collective-permute-start | bytes 4718600 | tf_op jit(solution)/shard_map/ppermute | solution.py:77
  196.1 71.0 %collective-permute-start.1 = (f32[1536,256]{1,0:T(8,128)S(1)}, f32[1536,256]{1,0:T(8,128)}, u32[]{:S(2)}, u32[]{:S(2)}) collective-permute-start(f32[1536,256]{1,0:T(8,128)S(1)} %get-tuple-element.28), channel_id=1, source_target_pairs={{1,0},{2,1},{3,2},{5,4},{6,5},{7,6},{9,8},{10,9},{11,10},{13,12},{... | collective-permute-start | bytes 4718600 | tf_op jit(solution)/shard_map/ppermute | solution.py:77
  197.4 99.8 %collective-permute-start = (f32[1536,256]{1,0:T(8,128)S(1)}, f32[1536,256]{1,0:T(8,128)}, u32[]{:S(2)}, u32[]{:S(2)}) collective-permute-start(f32[1536,256]{1,0:T(8,128)S(1)} %get-tuple-element.28), channel_id=1, source_target_pairs={{0,1},{1,2},{2,3},{4,5},{5,6},{6,7},{8,9},{9,10},{10,11},{12,13},{... | collective-permute-start | bytes 4718600 | tf_op jit(solution)/shard_map/ppermute | solution.py:77
  229.8 98.0 %collective-permute-start.8 = (f32[1536,256]{1,0:T(8,128)S(1)}, f32[1536,256]{1,0:T(8,128)S(1)}, u32[]{:S(2)}, u32[]{:S(2)}) collective-permute-start(f32[1536,256]{1,0:T(8,128)S(1)} %get-tuple-element.32), channel_id=1, source_target_pairs={{0,1},{3,2},{4,5},{7,6},{8,9},{11,10},{12,13},{15,14},{16,17},{19,... | collective-permute-start | bytes 4718600 | tf_op jit(solution)/shard_map/ppermute | solution.py:77
  234.3 96.5 %collective-permute-start.22 = (f32[1536,256]{1,0:T(8,128)S(1)}, f32[1536,256]{1,0:T(8,128)}, u32[]{:S(2)}, u32[]{:S(2)}) collective-permute-start(f32[1536,256]{1,0:T(8,128)S(1)} %collective-permute-done.6.refs_2_.refs_3_.rest_0_), channel_id=1, source_target_pairs={{1,2},{2,3},{5,6},{6,7},{9,10},{10,11},{13,14},{14,15},{17,18},{18... | collective-permute-start | bytes 4718600 | tf_op jit(solution)/shard_map/ppermute | solution.py:77
  264.7 67.4 %collective-permute-start.23 = (f32[1536,256]{1,0:T(8,128)S(1)}, f32[1536,256]{1,0:T(8,128)}, u32[]{:S(2)}, u32[]{:S(2)}) collective-permute-start(f32[1536,256]{1,0:T(8,128)S(1)} %collective-permute-done.7.refs_3_.refs_4_.rest_3_), channel_id=1, source_target_pairs={{2,1},{1,0},{6,5},{5,4},{10,9},{9,8},{14,13},{13,12},{18,17},{17,1... | collective-permute-start | bytes 4718600 | tf_op jit(solution)/shard_map/ppermute | solution.py:77
  267.1 66.5 %collective-permute-start.19 = (f32[1536,256]{1,0:T(8,128)}, f32[1536,256]{1,0:T(8,128)}, u32[]{:S(2)}, u32[]{:S(2)}) collective-permute-start(f32[1536,256]{1,0:T(8,128)} %collective-permute-done.4.refs_2_.refs_3_.rest_6_), channel_id=1, source_target_pairs={{1,2},{2,3},{5,6},{6,7},{9,10},{10,11},{13,14},{14,15},{17,18},{18... | collective-permute-start | bytes 4718600 | tf_op jit(solution)/shard_map/ppermute | solution.py:77
  332.1 72.9 %collective-permute-start.10 = (f32[1536,256]{1,0:T(8,128)}, f32[1536,256]{1,0:T(8,128)}, u32[]{:S(2)}, u32[]{:S(2)}) collective-permute-start(f32[1536,256]{1,0:T(8,128)} %collective-permute-done.1.refs_3_.refs_4_.rest_3_), channel_id=1, source_target_pairs={{2,1},{1,0},{6,5},{5,4},{10,9},{9,8},{14,13},{13,12},{18,17},{17,1... | collective-permute-start | bytes 4718600 | tf_op jit(solution)/shard_map/ppermute | solution.py:77
  333.6 132.3 %collective-permute-start.9 = (f32[1536,256]{1,0:T(8,128)}, f32[1536,256]{1,0:T(8,128)}, u32[]{:S(2)}, u32[]{:S(2)}) collective-permute-start(f32[1536,256]{1,0:T(8,128)} %collective-permute-done.refs_2_.refs_3_.rest_0_), channel_id=1, source_target_pairs={{1,2},{2,3},{5,6},{6,7},{9,10},{10,11},{13,14},{14,15},{17,18},{18... | collective-permute-start | bytes 4718600 | tf_op jit(solution)/shard_map/ppermute | solution.py:77
  351.8 202.6 %collective-permute-start.28 = (f32[1536,256]{1,0:T(8,128)}, f32[1536,256]{1,0:T(8,128)}, u32[]{:S(2)}, u32[]{:S(2)}) collective-permute-start(f32[1536,256]{1,0:T(8,128)} %collective-permute-done.22.refs_5_.rest_1_), channel_id=1, source_target_pairs={{2,3},{6,7},{10,11},{14,15},{18,19},{22,23},{26,27},{30,31}} | collective-permute-start | bytes 4718600 | tf_op jit(solution)/shard_map/ppermute | solution.py:77
  353.6 202.0 %collective-permute-start.29 = (f32[1536,256]{1,0:T(8,128)}, f32[1536,256]{1,0:T(8,128)}, u32[]{:S(2)}, u32[]{:S(2)}) collective-permute-start(f32[1536,256]{1,0:T(8,128)} %collective-permute-done.23.refs_6_.rest_4_), channel_id=1, source_target_pairs={{1,0},{5,4},{9,8},{13,12},{17,16},{21,20},{25,24},{29,28}} | collective-permute-start | bytes 4718600 | tf_op jit(solution)/shard_map/ppermute | solution.py:77
  371.3 185.1 %collective-permute-start.30 = (f32[1536,256]{1,0:T(8,128)}, f32[1536,256]{1,0:T(8,128)}, u32[]{:S(2)}, u32[]{:S(2)}) collective-permute-start(f32[1536,256]{1,0:T(8,128)} %collective-permute-done.19.refs_5_.rest_7_), channel_id=1, source_target_pairs={{2,3},{6,7},{10,11},{14,15},{18,19},{22,23},{26,27},{30,31}} | collective-permute-start | bytes 4718600 | tf_op jit(solution)/shard_map/ppermute | solution.py:77
  405.0 152.9 %collective-permute-start.31 = (f32[1536,256]{1,0:T(8,128)}, f32[1536,256]{1,0:T(8,128)}, u32[]{:S(2)}, u32[]{:S(2)}) collective-permute-start(f32[1536,256]{1,0:T(8,128)} %collective-permute-done.20.refs_6_.rest_10_), channel_id=1, source_target_pairs={{1,0},{5,4},{9,8},{13,12},{17,16},{21,20},{25,24},{29,28}} | collective-permute-start | bytes 4718600 | tf_op jit(solution)/shard_map/ppermute | solution.py:77
  465.9 118.8 %collective-permute-start.26 = (f32[1536,256]{1,0:T(8,128)}, f32[1536,256]{1,0:T(8,128)S(1)}, u32[]{:S(2)}, u32[]{:S(2)}) collective-permute-start(f32[1536,256]{1,0:T(8,128)} %collective-permute-done.12.refs_5_.rest_1_), channel_id=1, source_target_pairs={{2,3},{6,7},{10,11},{14,15},{18,19},{22,23},{26,27},{30,31}} | collective-permute-start | bytes 4718600 | tf_op jit(solution)/shard_map/ppermute | solution.py:77
  556.4 70.4 %collective-permute-start.25 = (f32[1536,256]{1,0:T(8,128)}, f32[1536,256]{1,0:T(8,128)S(1)}, u32[]{:S(2)}, u32[]{:S(2)}) collective-permute-start(f32[1536,256]{1,0:T(8,128)} %collective-permute-done.10.refs_6_.rest_4_), channel_id=1, source_target_pairs={{1,0},{5,4},{9,8},{13,12},{17,16},{21,20},{25,24},{29,28}} | collective-permute-start | bytes 4718600 | tf_op jit(solution)/shard_map/ppermute | solution.py:77
  (42 other events, 856.1 us)
Sparse Core Ops, SparseCore 0:
  35.9 106.3 all-gather.1

commit v3 on v2

--- a/solution.py
+++ b/solution.py
@@ -426,73 +426,70 @@
     )(gram, table, eigen_j, eigen_i, ids_j, ids_i, slope_j)
 
 
-def spread_kernel(chips, width, mine, z_ref, land, out_send, out_recv, pair_send, pair_recv):
+def spread_kernel(width, mine, z_ref, land, sends, recvs):
     me = lax.axis_index("harm")
     core = lax.rem(me, 2)
     chip = lax.div(me, 2)
     partner = me + 1 - 2 * core
+    across = [chip + 1 - 2 * lax.rem(chip, 2), chip + 2 - 4 * lax.div(chip, 2)]
+    opposite = 3 - chip
     greet({"harm": partner})
-    for d in range(1, chips):
-        greet({"harm": lax.rem(chip + d, chips) * 2 + core})
-    pl.semaphore_wait(pltpu.get_barrier_semaphore(), chips)
-    outward = []
-    for d in range(1, chips):
-        outward.append(
+    for q in across:
+        greet({"harm": q * 2 + core})
+    pl.semaphore_wait(pltpu.get_barrier_semaphore(), 3)
+
+    def push(source, origin, at, index, device):
+        copy = send(source, land.at[origin, at], sends.at[index], recvs.at[index], {"harm": device})
+        copy.start()
+        return copy
+
+    direct = [push(mine, chip, core, k, across[k] * 2 + core) for k in range(2)]
+    pair = [push(mine, chip, core, 2, partner)]
+    land[chip, core] = mine[...]
+    relay = []
+    for k in range(2):
+        direct[k].wait()
+        origin = across[k]
+        relay.append(
             send(
-                mine,
-                land.at[chip, core],
-                out_send.at[d - 1],
-                out_recv.at[d - 1],
-                {"harm": lax.rem(chip + d, chips) * 2 + core},
+                land.at[origin, core, k],
+                land.at[origin, core, k],
+                sends.at[3 + k],
+                recvs.at[3 + k],
+                {"harm": across[1 - k] * 2 + core},
             )
         )
-        outward[-1].start()
-    paired = [send(mine, land.at[chip, core], pair_send.at[0], pair_recv.at[0], {"harm": partner})]
-    paired[0].start()
-    land[chip, core] = mine[...]
-    for d in range(1, chips):
-        origin = lax.rem(chip + chips - d, chips)
-        outward[d - 1].wait()
-        paired.append(
-            send(
-                land.at[origin, core],
-                land.at[origin, core],
-                pair_send.at[d],
-                pair_recv.at[d],
-                {"harm": partner},
-            )
-        )
-        paired[-1].start()
-    for copy in paired:
+        relay[k].start()
+        pair.append(push(land.at[origin, core], origin, core, 5 + k, partner))
+    for k in range(2):
+        relay[k].wait()
+    pair.append(push(land.at[opposite, core], opposite, core, 7, partner))
+    for copy in pair:
         copy.wait()
     depth = z_ref.shape[1] // 3
-    half = chips // 2
-    for q in range(chips):
+    for q in range(4):
         for side in range(2):
-            piece = 1 - q // half if side == 0 else 2 + q // half
+            piece = 1 - q // 2 if side == 0 else 2 + q // 2
             block = jnp.concatenate([land[q, 0, side], land[q, 1, side]], axis=0).T
             high, low = split(block)
-            at = piece * width + (q % half) * block.shape[1]
             size = block.shape[1]
+            at = piece * width + (q % 2) * size
             z_ref[:, at : at + size] = high
             z_ref[:, depth + at : depth + at + size] = low
             z_ref[:, 2 * depth + at : 2 * depth + at + size] = high
 
 
-def spread(mine, harm_count, mode_count, width):
-    chips = harm_count // 2
+def spread(mine, mode_count, width):
     vmem = pl.BlockSpec(memory_space=pltpu.VMEM)
     return pl.pallas_call(
-        functools.partial(spread_kernel, chips, width),
+        functools.partial(spread_kernel, width),
         in_specs=[vmem],
         out_specs=vmem,
         out_shape=jax.ShapeDtypeStruct((mine.shape[2], 3 * mode_count * width), jnp.bfloat16),
         scratch_shapes=[
-            pltpu.VMEM((chips, 2, *mine.shape), jnp.float32),
-            pltpu.SemaphoreType.DMA((chips - 1,)),
-            pltpu.SemaphoreType.DMA((chips - 1,)),
-            pltpu.SemaphoreType.DMA((chips,)),
-            pltpu.SemaphoreType.DMA((chips,)),
+            pltpu.VMEM((4, 2, *mine.shape), jnp.float32),
+            pltpu.SemaphoreType.DMA((8,)),
+            pltpu.SemaphoreType.DMA((8,)),
         ],
         compiler_params=pltpu.CompilerParams(
             collective_id=2, has_side_effects=True, vmem_limit_bytes=40 * 2**20
@@ -521,7 +518,10 @@
     layer = lax.axis_index("mode")
     height, width = mode_vectors.shape
     lower = layer <= 1
-    own = jnp.split(mode_vectors, chunks, 0)
+    part = height // chunks
+    own = [mode_vectors[:part]]
+    rest, first = lax.optimization_barrier((mode_vectors, own[0]))
+    own = [first] + [rest[c * part : (c + 1) * part] for c in range(1, chunks)]
     slope = jnp.split(cotangent, chunks, 0)
 
     def hop(values, pairs):
@@ -548,7 +548,6 @@
     b3 = hop(b2, [(2, 3)])
     a3 = hop(a2, [(1, 0)])
 
-    part = height // chunks
     near = None
     for c in range(chunks):
         near = gram_chunk(
@@ -558,7 +557,7 @@
     far_parts = None
     for c in range(chunks):
         side = edge[c]
-        if c == 1:
+        if c == 2:
             side, w_slab = lax.optimization_barrier((side, w_slab))
         far_parts = gram_chunk(
             c, part, [cotangent, side], [mode_vectors, b1[c], a1[c], b2[c], a2[c]], (1, 1, 1, 1, 0),
@@ -583,7 +582,7 @@
         gram, w_slab, eigen_j[:, None], eigen_i[None, :], col_ids[:, None], row_ids[None, :],
         slope_j[:, None], harm_count, mode_count,
     )
-    z3 = spread(mine, harm_count, mode_count, width)
+    z3 = spread(mine, mode_count, width)
 
     out = None
     lists = list(zip(b1, b2, b3, a1, a2, a3))
@@ -600,7 +599,8 @@
     harm_count = mesh.shape["harm"]
     mode_count = mesh.shape["mode"]
     placed = (P("harm", "mode"), P("harm", "mode"), P("harm", "mode"), P(), P(), P())
-    form = line if mode_count == 4 else plain
+    lined = mode_count == 4 and harm_count == 8
+    form = line if lined else plain
 
     def local(*operands):
         return form(*operands, harm_count, mode_count)

time: 654 us -> 649 us (level)
    unnamed x66 -> x70, local copies, waits for them, and re-layouts: 28 us -> 30.5 us
  transfers between devices with their start and end apart: 33 -> 33, of which waited for: 13 -> 13; matrix products, arithmetic and copies ran while one was open for 5% -> 5% of each run, Pallas kernels for 24% -> 23%
where the time goes in v3:
time: 649 us; the launch traced here: 647 us
  waiting for transfers between devices  307 us (47%)
  Pallas kernels  168 us (26%)
  starting transfers between devices  81.8 us (13%)
  local copies, waits for them, and re-layouts  67.9 us (10%)
  between operations  14.2 us (2%)
  other arithmetic  8.55 us (1%)
    ppermute x32, waiting for transfers between devices, shift(): return lax.ppermute(value, 'mode', pairs)  307 us
    ppermute x32, starting transfers between devices, shift(): return lax.ppermute(value, 'mode', pairs)  81.8 us
    pallas_call x3, Pallas kernels, final_chunk(): pl.pallas_call(functools.partial(final_kernel, first_row, pieces, len(gro...  58.8 us
    pallas_call x1, Pallas kernels, chain(): pl.pallas_call(functools.partial(chain_kernel, chips), in_specs=[vmem, pl...  47.9 us
    pallas_call x8, Pallas kernels, gram_chunk(): pl.pallas_call(functools.partial(gram_kernel, len(lefts), fresh, plan), g...  38 us
    unnamed x70, local copies, waits for them, and re-layouts  30.5 us
    gather x1, local copies, waits for them, and re-layouts, line_body(): w_slab = jnp.take(w_every, position, axis=0, mode='clip')  27.9 us
    pallas_call x1, Pallas kernels, spread(): pl.pallas_call(functools.partial(spread_kernel, width), in_specs=[vmem],...  23.3 us
  transfers between devices with their start and end apart: 33, of which 13 were waited for; matrix products, arithmetic and copies ran while one was open for 5% of the time, Pallas kernels for 23%

profile of v3, /device:TPU:0, one launch (start us, length us, event | category | flops | bytes accessed | tf_op | source)
XLA Modules:
  0.0 647.2 jit_solution(7044595298710278496)
XLA Ops:
  22.2 10.4 %collective-permute-done.12 = f32[512,256]{1,0:T(8,128)S(1)} collective-permute-done((f32[512,256]{1,0:T(8,128)S(1)}, f32[512,256]{1,0:T(8,128)S(1)}, u32[]{:S(2)}, u32[]{:S(2)}) %collective-permute-start.12) | collective-permute-done | bytes 524320 | tf_op jit(solution)/shard_map/ppermute | solution.py:77
  39.2 21.1 %collective-permute-start.11 = (f32[1536,256]{1,0:T(8,128)S(1)}, f32[1536,256]{1,0:T(8,128)S(1)}, u32[]{:S(2)}, u32[]{:S(2)}) collective-permute-start(f32[1536,256]{1,0:T(8,128)S(1)} %get-tuple-element.31), channel_id=1, source_target_pairs={{0,1},{3,2},{4,5},{7,6},{8,9},{11,10},{12,13},{15,14},{16,17},{19,... | collective-permute-start | bytes 4718600 | tf_op jit(solution)/shard_map/ppermute | solution.py:77
  70.8 24.2 %collective-permute-done.11.refs_1_ = f32[1536,256]{1,0:T(8,128)S(1)} collective-permute-done((f32[1536,256]{1,0:T(8,128)S(1)}, f32[1536,256]{1,0:T(8,128)S(1)}, u32[]{:S(2)}, u32[]{:S(2)}) %collective-permute-start.11) | collective-permute-done | bytes 1572896 | tf_op jit(solution)/shard_map/ppermute | solution.py:77
  97.4 31.2 %collective-permute-done.6.refs_2_.refs_3_.rest_0_ = f32[1536,256]{1,0:T(8,128)S(1)} collective-permute-done((f32[1536,256]{1,0:T(8,128)S(1)}, f32[1536,256]{1,0:T(8,128)S(1)}, u32[]{:S(2)}, u32[]{:S(2)}) %collective-permute-start.6) | collective-permute-done | bytes 1572896 | tf_op jit(solution)/shard_map/ppermute | solution.py:77
  134.6 27.8 %collective-permute-done.21.refs_1_ = f32[1536,256]{1,0:T(8,128)S(1)} collective-permute-done((f32[1536,256]{1,0:T(8,128)S(1)}, f32[1536,256]{1,0:T(8,128)S(1)}, u32[]{:S(2)}, u32[]{:S(2)}) %collective-permute-start.21) | collective-permute-done | bytes 1572896 | tf_op jit(solution)/shard_map/ppermute | solution.py:77
  164.8 31.3 %collective-permute-done.4.refs_2_.refs_3_.rest_6_ = f32[1536,256]{1,0:T(8,128)} collective-permute-done((f32[1536,256]{1,0:T(8,128)S(1)}, f32[1536,256]{1,0:T(8,128)}, u32[]{:S(2)}, u32[]{:S(2)}) %collective-permute-start.4) | collective-permute-done | bytes 1572896 | tf_op jit(solution)/shard_map/ppermute | solution.py:77
  197.4 6.3 collective-permute-start
  203.7 26.1 %collective-permute-done.18.refs_1_ = f32[1536,256]{1,0:T(8,128)S(1)} collective-permute-done((f32[1536,256]{1,0:T(8,128)S(1)}, f32[1536,256]{1,0:T(8,128)S(1)}, u32[]{:S(2)}, u32[]{:S(2)}) %collective-permute-start.18) | collective-permute-done | bytes 1572896 | tf_op jit(solution)/shard_map/ppermute | solution.py:77
  235.5 28.0 %collective-permute-done.2.refs_2_.refs_3_.rest_0_ = f32[1536,256]{1,0:T(8,128)S(1)} collective-permute-done((f32[1536,256]{1,0:T(8,128)S(1)}, f32[1536,256]{1,0:T(8,128)S(1)}, u32[]{:S(2)}, u32[]{:S(2)}) %collective-permute-start.2) | collective-permute-done | bytes 1572896 | tf_op jit(solution)/shard_map/ppermute | solution.py:77
  270.7 26.5 %collective-permute-done.refs_2_.refs_3_.rest_0_ = f32[1536,256]{1,0:T(8,128)} collective-permute-done((f32[1536,256]{1,0:T(8,128)S(1)}, f32[1536,256]{1,0:T(8,128)}, u32[]{:S(2)}, u32[]{:S(2)}) %collective-permute-start) | collective-permute-done | bytes 1572896 | tf_op jit(solution)/shard_map/ppermute | solution.py:77
  298.5 29.3 %collective-permute-done.8.refs_1_ = f32[1536,256]{1,0:T(8,128)S(1)} collective-permute-done((f32[1536,256]{1,0:T(8,128)S(1)}, f32[1536,256]{1,0:T(8,128)S(1)}, u32[]{:S(2)}, u32[]{:S(2)}) %collective-permute-start.8) | collective-permute-done | bytes 1572896 | tf_op jit(solution)/shard_map/ppermute | solution.py:77
  354.9 16.6 %collective-permute-done.17.refs_6_.rest_4_ = f32[1536,256]{1,0:T(8,128)} collective-permute-done((f32[1536,256]{1,0:T(8,128)}, f32[1536,256]{1,0:T(8,128)}, u32[]{:S(2)}, u32[]{:S(2)}) %collective-permute-start.17) | collective-permute-done | bytes 1572896 | tf_op jit(solution)/shard_map/ppermute | solution.py:77
  373.3 31.9 %collective-permute-done.10.refs_6_.rest_4_ = f32[1536,256]{1,0:T(8,128)} collective-permute-done((f32[1536,256]{1,0:T(8,128)S(1)}, f32[1536,256]{1,0:T(8,128)}, u32[]{:S(2)}, u32[]{:S(2)}) %collective-permute-start.10) | collective-permute-done | bytes 1572896 | tf_op jit(solution)/shard_map/ppermute | solution.py:77
  421.2 6.0 gram_chunk.13
  428.2 27.9 %gather_fusion.1 = f32[4096,1024]{1,0:T(8,128)} fusion(f32[4096,1024]{1,0:T(8,128)} %all-gather.2.cloned.1.call-done, s32[4096]{0:T(1024)S(1)} %get-tuple-element.36), kind=kCustom, calls=%fused_computation.1 | custom fusion | bytes 33570816 | tf_op jit(solution)/shard_map/jit(_take)/gather | solution.py:543
  461.5 5.8 gram_chunk.14
  468.1 5.8 gram_chunk.15
  475.5 47.9 %chain.1.mine = f32[2,64,1024]{2,1,0:T(8,128)S(1)} custom-call(f32[512,1024]{1,0:T(8,128)} %pad_maximum_fusion.1.gram, f32[4096,1024]{1,0:T(8,128)} %gather_fusion.1, f32[64,1]{1,0:T(8,128)S(1)} %copy.13.eigen_j, f32[1,1024]{1,0:T(1,128)S(1)} %bitcast.21, s32[64,1]{1,0:T(8,128)S(1)} %iota_add_fusion.ids_j, s32[1,1024]{1,0:T(1,128)S(1)} %bitcast.22, ...), custom_call_target="tpu_custom_call" | custom-call | tf_op jit(solution)/shard_map/chain/pallas_call | solution.py:399
  523.4 23.3 %spread.1.z_ref = bf16[1024,3072]{1,0:T(8,128)(2,1)S(1)} custom-call(f32[2,64,1024]{2,1,0:T(8,128)S(1)} %chain.1.mine), custom_call_target="tpu_custom_call" | custom-call | tf_op jit(solution)/shard_map/spread/pallas_call | solution.py:484
  552.9 26.8 %final_chunk.3.rest_6_ = f32[1024,6144]{1,0:T(8,128)} custom-call(bf16[1024,3072]{1,0:T(8,128)(2,1)} %copy-done.3, f32[6144,256]{1,0:T(8,128)} %own.5, f32[1536,256]{1,0:T(8,128)S(1)} %copy-done.7, f32[1536,256]{1,0:T(8,128)} %collective-permute-done.22.refs_5_.rest_1_, f32[1536,256]{1,0:T(8,128)} %collective-permute-done.28.rest_2_, ...), custom_call_target="tpu_custom_call" | custom-call | flops 19327352832 | bytes 25165824 | tf_op jit(solution)/shard_map/final_chunk/pallas_call | solution.py:234
  579.7 9.0 %collective-permute-done.27.rest_5_ = f32[1536,256]{1,0:T(8,128)S(1)} collective-permute-done((f32[1536,256]{1,0:T(8,128)}, f32[1536,256]{1,0:T(8,128)S(1)}, u32[]{:S(2)}, u32[]{:S(2)}) %collective-permute-start.27) | collective-permute-done | bytes 1572896 | tf_op jit(solution)/shard_map/ppermute | solution.py:77
  591.3 16.0 %final_chunk.4.rest_6_ = f32[1024,6144]{1,0:T(8,128)} custom-call(bf16[1024,3072]{1,0:T(8,128)(2,1)} %copy-done.3, f32[6144,256]{1,0:T(8,128)} %own.5, f32[1536,256]{1,0:T(8,128)S(1)} %collective-permute-done.2.refs_2_.refs_3_.rest_0_, f32[1536,256]{1,0:T(8,128)} %collective-permute-done.16.refs_5_.rest_1_, ...), custom_call_target="tpu_custom_call", output_to_operand_aliasing={{}: (8, {})} | custom-call | flops 9663676416 | bytes 12582912 | tf_op jit(solution)/shard_map/final_chunk/pallas_call | solution.py:234
  607.4 14.4 %collective-permute-done.25.rest_5_ = f32[1536,256]{1,0:T(8,128)S(1)} collective-permute-done((f32[1536,256]{1,0:T(8,128)}, f32[1536,256]{1,0:T(8,128)S(1)}, u32[]{:S(2)}, u32[]{:S(2)}) %collective-permute-start.25) | collective-permute-done | bytes 1572896 | tf_op jit(solution)/shard_map/ppermute | solution.py:77
  624.3 16.0 %final_chunk.5 = f32[1024,6144]{1,0:T(8,128)} custom-call(bf16[1024,3072]{1,0:T(8,128)(2,1)} %copy-done.3, f32[6144,256]{1,0:T(8,128)} %own.5, f32[1536,256]{1,0:T(8,128)} %collective-permute-done.refs_2_.refs_3_.rest_0_, f32[1536,256]{1,0:T(8,128)} %collective-permute-done.9.refs_5_.rest_1_, ...), custom_call_target="tpu_custom_call", output_to_operand_aliasing={{}: (8, {})} | custom-call | flops 9663676416 | bytes 12582912 | tf_op jit(solution)/shard_map/final_chunk/pallas_call | solution.py:234
  (155 shorter events, 123.4 us)
Async XLA Ops:
  6.5 421.7 %all-gather.2.cloned.1.call-start = ((), (), s32[]{:S(2)}) async-start(), calls=%async_computation | async-start | bytes 18874368 | tf_op jit(solution)/shard_map/all_gather | solution.py:542
  60.4 68.2 %collective-permute-start.6 = (f32[1536,256]{1,0:T(8,128)S(1)}, f32[1536,256]{1,0:T(8,128)S(1)}, u32[]{:S(2)}, u32[]{:S(2)}) collective-permute-start(f32[1536,256]{1,0:T(8,128)S(1)} %slice.18), channel_id=1, source_target_pairs={{0,1},{1,2},{2,3},{4,5},{5,6},{6,7},{8,9},{9,10},{10,11},{12,13},{... | collective-permute-start | bytes 4718600 | tf_op jit(solution)/shard_map/ppermute | solution.py:77
  61.8 71.3 %collective-permute-start.7 = (f32[1536,256]{1,0:T(8,128)S(1)}, f32[1536,256]{1,0:T(8,128)S(1)}, u32[]{:S(2)}, u32[]{:S(2)}) collective-permute-start(f32[1536,256]{1,0:T(8,128)S(1)} %slice.18), channel_id=1, source_target_pairs={{1,0},{2,1},{3,2},{5,4},{6,5},{7,6},{9,8},{10,9},{11,10},{13,12},{... | collective-permute-start | bytes 4718600 | tf_op jit(solution)/shard_map/ppermute | solution.py:77
  63.1 99.2 %collective-permute-start.21 = (f32[1536,256]{1,0:T(8,128)S(1)}, f32[1536,256]{1,0:T(8,128)S(1)}, u32[]{:S(2)}, u32[]{:S(2)}) collective-permute-start(f32[1536,256]{1,0:T(8,128)S(1)} %get-tuple-element.29), channel_id=1, source_target_pairs={{0,1},{3,2},{4,5},{7,6},{8,9},{11,10},{12,13},{15,14},{16,17},{19,... | collective-permute-start | bytes 4718600 | tf_op jit(solution)/shard_map/ppermute | solution.py:77
  68.3 127.8 %collective-permute-start.4 = (f32[1536,256]{1,0:T(8,128)S(1)}, f32[1536,256]{1,0:T(8,128)}, u32[]{:S(2)}, u32[]{:S(2)}) collective-permute-start(f32[1536,256]{1,0:T(8,128)S(1)} %get-tuple-element.33), channel_id=1, source_target_pairs={{0,1},{1,2},{2,3},{4,5},{5,6},{6,7},{8,9},{9,10},{10,11},{12,13},{... | collective-permute-start | bytes 4718600 | tf_op jit(solution)/shard_map/ppermute | solution.py:77
  96.1 101.2 %collective-permute-start.5 = (f32[1536,256]{1,0:T(8,128)S(1)}, f32[1536,256]{1,0:T(8,128)}, u32[]{:S(2)}, u32[]{:S(2)}) collective-permute-start(f32[1536,256]{1,0:T(8,128)S(1)} %get-tuple-element.33), channel_id=1, source_target_pairs={{1,0},{2,1},{3,2},{5,4},{6,5},{7,6},{9,8},{10,9},{11,10},{13,12},{... | collective-permute-start | bytes 4718600 | tf_op jit(solution)/shard_map/ppermute | solution.py:77
  128.7 101.1 %collective-permute-start.18 = (f32[1536,256]{1,0:T(8,128)S(1)}, f32[1536,256]{1,0:T(8,128)S(1)}, u32[]{:S(2)}, u32[]{:S(2)}) collective-permute-start(f32[1536,256]{1,0:T(8,128)S(1)} %get-tuple-element.30), channel_id=1, source_target_pairs={{0,1},{3,2},{4,5},{7,6},{8,9},{11,10},{12,13},{15,14},{16,17},{19,... | collective-permute-start | bytes 4718600 | tf_op jit(solution)/shard_map/ppermute | solution.py:77
  133.2 130.3 %collective-permute-start.2 = (f32[1536,256]{1,0:T(8,128)S(1)}, f32[1536,256]{1,0:T(8,128)S(1)}, u32[]{:S(2)}, u32[]{:S(2)}) collective-permute-start(f32[1536,256]{1,0:T(8,128)S(1)} %get-tuple-element.34), channel_id=1, source_target_pairs={{0,1},{1,2},{2,3},{4,5},{5,6},{6,7},{8,9},{9,10},{10,11},{12,13},{... | collective-permute-start | bytes 4718600 | tf_op jit(solution)/shard_map/ppermute | solution.py:77
  163.5 102.9 %collective-permute-start.3 = (f32[1536,256]{1,0:T(8,128)S(1)}, f32[1536,256]{1,0:T(8,128)}, u32[]{:S(2)}, u32[]{:S(2)}) collective-permute-start(f32[1536,256]{1,0:T(8,128)S(1)} %get-tuple-element.34), channel_id=1, source_target_pairs={{1,0},{2,1},{3,2},{5,4},{6,5},{7,6},{9,8},{10,9},{11,10},{13,12},{... | collective-permute-start | bytes 4718600 | tf_op jit(solution)/shard_map/ppermute | solution.py:77
  196.1 72.8 %collective-permute-start.1 = (f32[1536,256]{1,0:T(8,128)S(1)}, f32[1536,256]{1,0:T(8,128)S(1)}, u32[]{:S(2)}, u32[]{:S(2)}) collective-permute-start(f32[1536,256]{1,0:T(8,128)S(1)} %get-tuple-element.35), channel_id=1, source_target_pairs={{1,0},{2,1},{3,2},{5,4},{6,5},{7,6},{9,8},{10,9},{11,10},{13,12},{... | collective-permute-start | bytes 4718600 | tf_op jit(solution)/shard_map/ppermute | solution.py:77
  197.4 99.8 %collective-permute-start = (f32[1536,256]{1,0:T(8,128)S(1)}, f32[1536,256]{1,0:T(8,128)}, u32[]{:S(2)}, u32[]{:S(2)}) collective-permute-start(f32[1536,256]{1,0:T(8,128)S(1)} %get-tuple-element.35), channel_id=1, source_target_pairs={{0,1},{1,2},{2,3},{4,5},{5,6},{6,7},{8,9},{9,10},{10,11},{12,13},{... | collective-permute-start | bytes 4718600 | tf_op jit(solution)/shard_map/ppermute | solution.py:77
  231.0 96.8 %collective-permute-start.8 = (f32[1536,256]{1,0:T(8,128)S(1)}, f32[1536,256]{1,0:T(8,128)S(1)}, u32[]{:S(2)}, u32[]{:S(2)}) collective-permute-start(f32[1536,256]{1,0:T(8,128)S(1)} %get-tuple-element.32), channel_id=1, source_target_pairs={{0,1},{3,2},{4,5},{7,6},{8,9},{11,10},{12,13},{15,14},{16,17},{19,... | collective-permute-start | bytes 4718600 | tf_op jit(solution)/shard_map/ppermute | solution.py:77
  263.5 67.3 %collective-permute-start.22 = (f32[1536,256]{1,0:T(8,128)S(1)}, f32[1536,256]{1,0:T(8,128)}, u32[]{:S(2)}, u32[]{:S(2)}) collective-permute-start(f32[1536,256]{1,0:T(8,128)S(1)} %collective-permute-done.6.refs_2_.refs_3_.rest_0_), channel_id=1, source_target_pairs={{1,2},{2,3},{5,6},{6,7},{9,10},{10,11},{13,14},{14,15},{17,18},{18... | collective-permute-start | bytes 4718600 | tf_op jit(solution)/shard_map/ppermute | solution.py:77
  266.4 65.7 %collective-permute-start.23 = (f32[1536,256]{1,0:T(8,128)S(1)}, f32[1536,256]{1,0:T(8,128)}, u32[]{:S(2)}, u32[]{:S(2)}) collective-permute-start(f32[1536,256]{1,0:T(8,128)S(1)} %collective-permute-done.7.refs_3_.refs_4_.rest_3_), channel_id=1, source_target_pairs={{2,1},{1,0},{6,5},{5,4},{10,9},{9,8},{14,13},{13,12},{18,17},{17,1... | collective-permute-start | bytes 4718600 | tf_op jit(solution)/shard_map/ppermute | solution.py:77
  268.9 64.7 %collective-permute-start.19 = (f32[1536,256]{1,0:T(8,128)}, f32[1536,256]{1,0:T(8,128)}, u32[]{:S(2)}, u32[]{:S(2)}) collective-permute-start(f32[1536,256]{1,0:T(8,128)} %collective-permute-done.4.refs_2_.refs_3_.rest_6_), channel_id=1, source_target_pairs={{1,2},{2,3},{5,6},{6,7},{9,10},{10,11},{13,14},{14,15},{17,18},{18... | collective-permute-start | bytes 4718600 | tf_op jit(solution)/shard_map/ppermute | solution.py:77
  332.1 73.1 %collective-permute-start.10 = (f32[1536,256]{1,0:T(8,128)S(1)}, f32[1536,256]{1,0:T(8,128)}, u32[]{:S(2)}, u32[]{:S(2)}) collective-permute-start(f32[1536,256]{1,0:T(8,128)S(1)} %collective-permute-done.1.refs_3_.refs_4_.rest_3_), channel_id=1, source_target_pairs={{2,1},{1,0},{6,5},{5,4},{10,9},{9,8},{14,13},{13,12},{18,17},{17,1... | collective-permute-start | bytes 4718600 | tf_op jit(solution)/shard_map/ppermute | solution.py:77
  333.6 133.7 %collective-permute-start.9 = (f32[1536,256]{1,0:T(8,128)}, f32[1536,256]{1,0:T(8,128)}, u32[]{:S(2)}, u32[]{:S(2)}) collective-permute-start(f32[1536,256]{1,0:T(8,128)} %collective-permute-done.refs_2_.refs_3_.rest_0_), channel_id=1, source_target_pairs={{1,2},{2,3},{5,6},{6,7},{9,10},{10,11},{13,14},{14,15},{17,18},{18... | collective-permute-start | bytes 4718600 | tf_op jit(solution)/shard_map/ppermute | solution.py:77
  351.8 197.5 %collective-permute-start.30 = (f32[1536,256]{1,0:T(8,128)}, f32[1536,256]{1,0:T(8,128)}, u32[]{:S(2)}, u32[]{:S(2)}) collective-permute-start(f32[1536,256]{1,0:T(8,128)} %collective-permute-done.19.refs_5_.rest_7_), channel_id=1, source_target_pairs={{2,3},{6,7},{10,11},{14,15},{18,19},{22,23},{26,27},{30,31}} | collective-permute-start | bytes 4718600 | tf_op jit(solution)/shard_map/ppermute | solution.py:77
  353.6 197.0 %collective-permute-start.31 = (f32[1536,256]{1,0:T(8,128)}, f32[1536,256]{1,0:T(8,128)}, u32[]{:S(2)}, u32[]{:S(2)}) collective-permute-start(f32[1536,256]{1,0:T(8,128)} %collective-permute-done.20.refs_6_.rest_10_), channel_id=1, source_target_pairs={{1,0},{5,4},{9,8},{13,12},{17,16},{21,20},{25,24},{29,28}} | collective-permute-start | bytes 4718600 | tf_op jit(solution)/shard_map/ppermute | solution.py:77
  371.5 179.8 %collective-permute-start.28 = (f32[1536,256]{1,0:T(8,128)}, f32[1536,256]{1,0:T(8,128)}, u32[]{:S(2)}, u32[]{:S(2)}) collective-permute-start(f32[1536,256]{1,0:T(8,128)} %collective-permute-done.22.refs_5_.rest_1_), channel_id=1, source_target_pairs={{2,3},{6,7},{10,11},{14,15},{18,19},{22,23},{26,27},{30,31}} | collective-permute-start | bytes 4718600 | tf_op jit(solution)/shard_map/ppermute | solution.py:77
  405.2 147.7 %collective-permute-start.29 = (f32[1536,256]{1,0:T(8,128)}, f32[1536,256]{1,0:T(8,128)}, u32[]{:S(2)}, u32[]{:S(2)}) collective-permute-start(f32[1536,256]{1,0:T(8,128)} %collective-permute-done.23.refs_6_.rest_4_), channel_id=1, source_target_pairs={{1,0},{5,4},{9,8},{13,12},{17,16},{21,20},{25,24},{29,28}} | collective-permute-start | bytes 4718600 | tf_op jit(solution)/shard_map/ppermute | solution.py:77
  467.3 112.4 %collective-permute-start.26 = (f32[1536,256]{1,0:T(8,128)}, f32[1536,256]{1,0:T(8,128)S(1)}, u32[]{:S(2)}, u32[]{:S(2)}) collective-permute-start(f32[1536,256]{1,0:T(8,128)} %collective-permute-done.16.refs_5_.rest_1_), channel_id=1, source_target_pairs={{2,3},{6,7},{10,11},{14,15},{18,19},{22,23},{26,27},{30,31}} | collective-permute-start | bytes 4718600 | tf_op jit(solution)/shard_map/ppermute | solution.py:77
  550.6 56.8 %collective-permute-start.24 = (f32[1536,256]{1,0:T(8,128)}, f32[1536,256]{1,0:T(8,128)S(1)}, u32[]{:S(2)}, u32[]{:S(2)}) collective-permute-start(f32[1536,256]{1,0:T(8,128)} %collective-permute-done.9.refs_5_.rest_1_), channel_id=1, source_target_pairs={{2,3},{6,7},{10,11},{14,15},{18,19},{22,23},{26,27},{30,31}} | collective-permute-start | bytes 4718600 | tf_op jit(solution)/shard_map/ppermute | solution.py:77
  551.4 70.4 %collective-permute-start.25 = (f32[1536,256]{1,0:T(8,128)}, f32[1536,256]{1,0:T(8,128)S(1)}, u32[]{:S(2)}, u32[]{:S(2)}) collective-permute-start(f32[1536,256]{1,0:T(8,128)} %collective-permute-done.10.refs_6_.rest_4_), channel_id=1, source_target_pairs={{1,0},{5,4},{9,8},{13,12},{17,16},{21,20},{25,24},{29,28}} | collective-permute-start | bytes 4718600 | tf_op jit(solution)/shard_map/ppermute | solution.py:77
  (44 other events, 822.8 us)
Sparse Core Ops, SparseCore 0:
  35.9 106.3 all-gather.1

commit v4 on v3

--- a/solution.py
+++ b/solution.py
@@ -271,9 +271,68 @@
     pl.semaphore_signal(pltpu.get_barrier_semaphore(), inc=1, device_id=device, device_id_type=MESH)
 
 
+def order_kernel(count, position, *refs):
+    blocks = refs[:count]
+    high_ref, low_ref, buf, stage, sems = refs[count:]
+    step = pl.program_id(0)
+    share = blocks[0].shape[0]
+    rows = stage.shape[0]
+
+    @pl.when(step == 0)
+    def _():
+        copies = [
+            pltpu.make_async_copy(blocks[k], buf.at[pl.ds(k * share, share), :], sems.at[k])
+            for k in range(count)
+        ]
+        for copy in copies:
+            copy.start()
+        for copy in copies:
+            copy.wait()
+
+    def body(index, carry):
+        base = index * 8
+        for k in range(8):
+            stage[pl.ds(base + k, 1), :] = buf[pl.ds(position[step * rows + base + k], 1), :]
+        return carry
+
+    lax.fori_loop(0, rows // 8, body, 0)
+    high, low = split(stage[...])
+    high_ref[0] = high
+    low_ref[0] = low
+
+
+def order(position, blocks):
+    share, modes = blocks[0].shape
+    count = len(blocks)
+    rows = 512
+    steps = count * share // rows
+    shape = jax.ShapeDtypeStruct((steps, rows, modes), jnp.bfloat16)
+    spec = pl.BlockSpec((1, rows, modes), lambda i, p: (i, 0, 0))
+    return pl.pallas_call(
+        functools.partial(order_kernel, count),
+        grid_spec=pltpu.PrefetchScalarGridSpec(
+            num_scalar_prefetch=1,
+            grid=(steps,),
+            in_specs=[pl.BlockSpec(memory_space=pl.ANY)] * count,
+            out_specs=[spec, spec],
+            scratch_shapes=[
+                pltpu.VMEM((count * share, modes), jnp.float32),
+                pltpu.VMEM((rows, modes), jnp.float32),
+                pltpu.SemaphoreType.DMA((count,)),
+            ],
+        ),
+        out_shape=[shape, shape],
+        compiler_params=pltpu.CompilerParams(vmem_limit_bytes=32 * 2**20),
+        cost_estimate=pl.CostEstimate(
+            flops=0, bytes_accessed=8 * count * share * modes, transcendentals=0
+        ),
+        name="order",
+    )(position, *blocks)
+
+
 def chain_kernel(
-    chips, gram, table, eigen_j, eigen_i, ids_j, ids_i, slope_j, mine,
-    met, total, came, w_tiles, w_high, w_low, zt, got, land,
+    chips, gram, high_table, low_table, eigen_j, eigen_i, ids_j, ids_i, slope_j, mine,
+    met, total, came, w_high, w_low, zt, got, land,
     w_sems, met_send, met_recv, came_send, came_recv, z_send, z_recv,
 ):
     me = lax.axis_index("harm")
@@ -283,7 +342,7 @@
     partner = me + 1 - 2 * core
     middle = (layer == 1) | (layer == 2)
     span = met.shape[1]
-    tiles, rows = w_tiles.shape[:2]
+    tiles, rows = w_high.shape[:2]
     peer = 3 - layer
     end = jnp.where(layer == 1, 0, 3)
     keep = jnp.where(layer == 1, 0, 2)
@@ -310,8 +369,8 @@
         for copy in first:
             copy.start()
         loads = [
-            pltpu.make_async_copy(table.at[pl.ds(t * rows, rows), :], w_tiles.at[t], w_sems.at[t])
-            for t in range(tiles)
+            pltpu.make_async_copy(high_table, w_high, w_sems.at[0]),
+            pltpu.make_async_copy(low_table, w_low, w_sems.at[1]),
         ]
         for load in loads:
             load.start()
@@ -333,14 +392,6 @@
             second[-1].start()
         for load in loads:
             load.wait()
-
-        def cut(t, carry):
-            high, low = split(w_tiles[t])
-            w_high[t] = high
-            w_low[t] = low
-            return carry
-
-        lax.fori_loop(0, tiles, cut, 0)
         for copy in second:
             copy.wait()
         value = total[chip]
@@ -388,30 +439,27 @@
         mine[...] = land[...]
 
 
-def chain(gram, table, eigen_j, eigen_i, ids_j, ids_i, slope_j, harm_count, mode_count):
+def chain(gram, high_table, low_table, eigen_j, eigen_i, ids_j, ids_i, slope_j, harm_count, mode_count):
     chips = harm_count // 2
     span = gram.shape[0] // harm_count
     modes = gram.shape[1]
-    rows = table.shape[0] // mode_count
-    cut = 512
-    tiles = table.shape[0] // cut
+    rows = high_table.shape[0] * high_table.shape[1] // mode_count
     vmem = pl.BlockSpec(memory_space=pltpu.VMEM)
     return pl.pallas_call(
         functools.partial(chain_kernel, chips),
-        in_specs=[vmem, pl.BlockSpec(memory_space=pl.ANY)] + [vmem] * 5,
+        in_specs=[vmem] + [pl.BlockSpec(memory_space=pl.ANY)] * 2 + [vmem] * 5,
         out_specs=vmem,
         out_shape=jax.ShapeDtypeStruct((2, span, rows), jnp.float32),
         scratch_shapes=[
             pltpu.VMEM((chips, span, modes), jnp.float32),
             pltpu.VMEM((chips, span, modes), jnp.float32),
             pltpu.VMEM((chips - 1, span, modes), jnp.float32),
-            pltpu.VMEM((tiles, cut, modes), jnp.float32),
-            pltpu.VMEM((tiles, cut, modes), jnp.bfloat16),
-            pltpu.VMEM((tiles, cut, modes), jnp.bfloat16),
+            pltpu.VMEM(high_table.shape, jnp.bfloat16),
+            pltpu.VMEM(low_table.shape, jnp.bfloat16),
             pltpu.VMEM((mode_count, span, rows), jnp.float32),
             pltpu.VMEM((2, span, rows), jnp.float32),
             pltpu.VMEM((2, span, rows), jnp.float32),
-            pltpu.SemaphoreType.DMA((tiles,)),
+            pltpu.SemaphoreType.DMA((2,)),
             pltpu.SemaphoreType.DMA((chips,)),
             pltpu.SemaphoreType.DMA((chips,)),
             pltpu.SemaphoreType.DMA((chips - 1,)),
@@ -423,7 +471,7 @@
             collective_id=1, has_side_effects=True, vmem_limit_bytes=52 * 2**20
         ),
         name="chain",
-    )(gram, table, eigen_j, eigen_i, ids_j, ids_i, slope_j)
+    )(gram, high_table, low_table, eigen_j, eigen_i, ids_j, ids_i, slope_j)
 
 
 def spread_kernel(width, mine, z_ref, land, sends, recvs):
@@ -506,9 +554,9 @@
     hit = (owner[None, :] == ids).astype(jnp.int32)
     running = jnp.cumsum(hit, axis=1)
     rank = jnp.sum(hit * running, axis=0) - 1
-    position = owner * share + rank
+    position = (owner ^ harm_index) * share + rank
     slots = lax.broadcasted_iota(jnp.int32, (share, total), 0)
-    mine = (position - harm_index * share)[None, :] == slots
+    mine = position[None, :] == slots
     offsets = jnp.sum(jnp.where(mine, (slab_rows - harm_index * row_count)[None, :], 0), axis=1)
     return position, offsets
 
@@ -539,8 +587,10 @@
     w_a1 = shift(picked, [(3, 2), (2, 1)])
     w_third = shift(w_b1, [(1, 2)]) + shift(w_a1, [(2, 1)])
     w_all = jnp.concatenate([picked, w_b1, w_a1, w_third], axis=1)
-    w_every = lax.all_gather(w_all, "harm", axis=0, tiled=True)
-    w_slab = jnp.take(w_every, position, axis=0, mode="clip")
+    pairs = lambda flip: [(n, n ^ flip) for n in range(harm_count)]
+    blocks = [w_all] + [lax.ppermute(w_all, "harm", pairs(2 * d)) for d in (1, 2, 3)]
+    blocks = [v for block in blocks for v in (block, lax.ppermute(block, "harm", pairs(1)))]
+    w_high, w_low = order(position, blocks)
 
     b2 = hop(b1, [(1, 2), (2, 3)])
     a2 = hop(a1, [(2, 1), (1, 0)])
@@ -557,8 +607,8 @@
     far_parts = None
     for c in range(chunks):
         side = edge[c]
-        if c == 2:
-            side, w_slab = lax.optimization_barrier((side, w_slab))
+        if c == 1:
+            side, w_high, w_low = lax.optimization_barrier((side, w_high, w_low))
         far_parts = gram_chunk(
             c, part, [cotangent, side], [mode_vectors, b1[c], a1[c], b2[c], a2[c]], (1, 1, 1, 1, 0),
             ((0, 3 * width), (width, 0)), ((width, width), (width, 4 * width)), far_parts,
@@ -579,14 +629,14 @@
     slope_j = lax.dynamic_slice_in_dim(eigen_cotangent, first_col, span)
     col_ids = first_col + jnp.arange(span, dtype=jnp.int32)
     mine = chain(
-        gram, w_slab, eigen_j[:, None], eigen_i[None, :], col_ids[:, None], row_ids[None, :],
+        gram, w_high, w_low, eigen_j[:, None], eigen_i[None, :], col_ids[:, None], row_ids[None, :],
         slope_j[:, None], harm_count, mode_count,
     )
     z3 = spread(mine, mode_count, width)
 
     out = None
     lists = list(zip(b1, b2, b3, a1, a2, a3))
-    for first, count in ((0, 2), (2, 1), (3, 1)):
+    for first, count in ((0, chunks - 1), (chunks - 1, 1)):
         out = final_chunk(first, z3, mode_vectors, lists[first : first + count], out, height)
     return out
 

time: 649 us -> 676 us (1.042)
  Pallas kernels: 168 us -> 203 us
  waiting for transfers between devices: 307 us -> 329 us
  local copies, waits for them, and re-layouts: 67.9 us -> 46.5 us
  between operations: 14.2 us -> 1.13 us
  starting transfers between devices: 81.8 us -> 88.9 us
    pallas_call x1 -> x2, Pallas kernels: 47.9 us -> 93.4 us  [the longest x1 66.2 us: chain(): pl.pallas_call(functools.partial(chain_kernel, chips), in_specs=[vmem] +...]
    gather x1 -> x0, local copies, waits for them, and re-layouts: 27.9 us -> none  [line_body(): w_slab = jnp.take(w_every, position, axis=0, mode='clip')]
    ppermute x0 -> x7, waiting for transfers between devices: none -> 21.1 us  [the longest x3 21.1 us: line_body(): lax.ppermute(w_all, 'harm', pairs(2 * d))]
    pallas_call x3 -> x2, Pallas kernels: 58.8 us -> 53.5 us  [final_chunk(): pl.pallas_call(functools.partial(final_kernel, first_row, pieces, len(gro...]
    unnamed x70 -> x102, local copies, waits for them, and re-layouts: 30.5 us -> 30.9 us
  transfers between devices with their start and end apart: 33 -> 39, of which waited for: 13 -> 13; matrix products, arithmetic and copies ran while one was open for 5% -> 2% of each run, Pallas kernels for 23% -> 28%
where the time goes in v4:
time: 676 us; the launch traced here: 674 us
  waiting for transfers between devices  329 us (49%)
  Pallas kernels  203 us (30%)
  starting transfers between devices  88.9 us (13%)
  local copies, waits for them, and re-layouts  46.5 us (7%)
    ppermute x32, waiting for transfers between devices, shift(): return lax.ppermute(value, 'mode', pairs)  308 us
    ppermute x32, starting transfers between devices, shift(): return lax.ppermute(value, 'mode', pairs)  83.8 us
    pallas_call x1, Pallas kernels, chain(): pl.pallas_call(functools.partial(chain_kernel, chips), in_specs=[vmem] +...  66.2 us
    pallas_call x2, Pallas kernels, final_chunk(): pl.pallas_call(functools.partial(final_kernel, first_row, pieces, len(gro...  53.5 us
    pallas_call x8, Pallas kernels, gram_chunk(): pl.pallas_call(functools.partial(gram_kernel, len(lefts), fresh, plan), g...  32.2 us
    unnamed x102, local copies, waits for them, and re-layouts  30.9 us
    pallas_call x1, Pallas kernels, order(): pl.pallas_call(functools.partial(order_kernel, count), grid_spec=pltpu.Pr...  27.2 us
    pallas_call x1, Pallas kernels, spread(): pl.pallas_call(functools.partial(spread_kernel, width), in_specs=[vmem],...  23.8 us
  transfers between devices with their start and end apart: 39, of which 13 were waited for; matrix products, arithmetic and copies ran while one was open for 2% of the time, Pallas kernels for 28%

profile of v4, /device:TPU:0, one launch (start us, length us, event | category | flops | bytes accessed | tf_op | source)
XLA Modules:
  0.0 674.2 jit_solution(17851374170138551448)
XLA Ops:
  0.0 5.7 fusion.3
  28.5 28.4 %collective-permute-done.15 = f32[512,256]{1,0:T(8,128)S(1)} collective-permute-done((f32[512,256]{1,0:T(8,128)S(1)}, f32[512,256]{1,0:T(8,128)S(1)}, u32[]{:S(2)}, u32[]{:S(2)}) %collective-permute-start.15) | collective-permute-done | bytes 524320 | tf_op jit(solution)/shard_map/ppermute | solution.py:77
  60.9 19.2 %collective-permute-start.28 = (f32[1536,256]{1,0:T(8,128)S(1)}, f32[1536,256]{1,0:T(8,128)S(1)}, u32[]{:S(2)}, u32[]{:S(2)}) collective-permute-start(f32[1536,256]{1,0:T(8,128)S(1)} %copy-done.46), channel_id=1, source_target_pairs={{0,1},{3,2},{4,5},{7,6},{8,9},{11,10},{12,13},{15,14},{16,17},{19,... | collective-permute-start | bytes 4718600 | tf_op jit(solution)/shard_map/ppermute | solution.py:77
  96.4 27.9 %collective-permute-done.28.refs_1_ = f32[1536,256]{1,0:T(8,128)S(1)} collective-permute-done((f32[1536,256]{1,0:T(8,128)S(1)}, f32[1536,256]{1,0:T(8,128)S(1)}, u32[]{:S(2)}, u32[]{:S(2)}) %collective-permute-start.28) | collective-permute-done | bytes 1572896 | tf_op jit(solution)/shard_map/ppermute | solution.py:77
  129.9 28.0 %collective-permute-done.4.refs_2_.refs_3_.rest_6_ = f32[1536,256]{1,0:T(8,128)S(1)} collective-permute-done((f32[1536,256]{1,0:T(8,128)S(1)}, f32[1536,256]{1,0:T(8,128)S(1)}, u32[]{:S(2)}, u32[]{:S(2)}) %collective-permute-start.4) | collective-permute-done | bytes 1572896 | tf_op jit(solution)/shard_map/ppermute | solution.py:77
  159.3 5.1 collective-permute-start
  164.8 26.9 %collective-permute-done.2.refs_2_.refs_3_.rest_12_ = f32[1536,256]{1,0:T(8,128)S(1)} collective-permute-done((f32[1536,256]{1,0:T(8,128)S(1)}, f32[1536,256]{1,0:T(8,128)S(1)}, u32[]{:S(2)}, u32[]{:S(2)}) %collective-permute-start.2) | collective-permute-done | bytes 1572896 | tf_op jit(solution)/shard_map/ppermute | solution.py:77
  197.7 27.7 %collective-permute-done.11.refs_1_ = f32[1536,256]{1,0:T(8,128)S(1)} collective-permute-done((f32[1536,256]{1,0:T(8,128)S(1)}, f32[1536,256]{1,0:T(8,128)S(1)}, u32[]{:S(2)}, u32[]{:S(2)}) %collective-permute-start.11) | collective-permute-done | bytes 1572896 | tf_op jit(solution)/shard_map/ppermute | solution.py:77
  229.5 29.5 %collective-permute-done.refs_2_.refs_3_.rest_0_ = f32[1536,256]{1,0:T(8,128)S(1)} collective-permute-done((f32[1536,256]{1,0:T(8,128)S(1)}, f32[1536,256]{1,0:T(8,128)S(1)}, u32[]{:S(2)}, u32[]{:S(2)}) %collective-permute-start) | collective-permute-done | bytes 1572896 | tf_op jit(solution)/shard_map/ppermute | solution.py:77
  260.4 31.3 %collective-permute-done.8.refs_1_ = f32[1536,256]{1,0:T(8,128)S(1)} collective-permute-done((f32[1536,256]{1,0:T(8,128)S(1)}, f32[1536,256]{1,0:T(8,128)S(1)}, u32[]{:S(2)}, u32[]{:S(2)}) %collective-permute-start.8) | collective-permute-done | bytes 1572896 | tf_op jit(solution)/shard_map/ppermute | solution.py:77
  296.0 21.1 %collective-permute-done.22.refs_4_ = f32[512,1024]{1,0:T(8,128)} collective-permute-done((f32[512,1024]{1,0:T(8,128)S(1)}, f32[512,1024]{1,0:T(8,128)}, u32[]{:S(2)}, u32[]{:S(2)}) %collective-permute-start.22) | collective-permute-done | bytes 2097184 | tf_op jit(solution)/shard_map/ppermute | solution.py:591
  328.1 9.1 %collective-permute-done.30.refs_6_.rest_4_ = f32[1536,256]{1,0:T(8,128)} collective-permute-done((f32[1536,256]{1,0:T(8,128)S(1)}, f32[1536,256]{1,0:T(8,128)}, u32[]{:S(2)}, u32[]{:S(2)}) %collective-permute-start.30) | collective-permute-done | bytes 1572896 | tf_op jit(solution)/shard_map/ppermute | solution.py:77
  338.6 32.3 %collective-permute-done.27.refs_6_.rest_10_ = f32[1536,256]{1,0:T(8,128)} collective-permute-done((f32[1536,256]{1,0:T(8,128)S(1)}, f32[1536,256]{1,0:T(8,128)}, u32[]{:S(2)}, u32[]{:S(2)}) %collective-permute-start.27) | collective-permute-done | bytes 1572896 | tf_op jit(solution)/shard_map/ppermute | solution.py:77
  371.4 33.2 %collective-permute-done.13.refs_6_.rest_16_ = f32[1536,256]{1,0:T(8,128)} collective-permute-done((f32[1536,256]{1,0:T(8,128)S(1)}, f32[1536,256]{1,0:T(8,128)}, u32[]{:S(2)}, u32[]{:S(2)}) %collective-permute-start.13) | collective-permute-done | bytes 1572896 | tf_op jit(solution)/shard_map/ppermute | solution.py:77
  406.5 29.9 %collective-permute-done.10.refs_6_.rest_4_ = f32[1536,256]{1,0:T(8,128)S(1)} collective-permute-done((f32[1536,256]{1,0:T(8,128)S(1)}, f32[1536,256]{1,0:T(8,128)S(1)}, u32[]{:S(2)}, u32[]{:S(2)}) %collective-permute-start.10) | collective-permute-done | bytes 1572896 | tf_op jit(solution)/shard_map/ppermute | solution.py:77
  469.5 5.3 gram_chunk.12
  479.0 27.2 %order.1 = (bf16[8,512,1024]{2,1,0:T(8,128)(2,1)}, bf16[8,512,1024]{2,1,0:T(8,128)(2,1)}) custom-call(s32[4096]{0:T(1024)S(1)} %bitcast_add_fusion.position, f32[512,1024]{1,0:T(8,128)S(1)} %copy-done.4, f32[512,1024]{1,0:T(8,128)S(1)} %copy-done.31, f32[512,1024]{1,0:T(8,128)} %collective-permute-done.20.refs_2_, ...), custom_call_target="tpu_custom_call" | custom-call | bytes 33554432 | tf_op jit(solution)/shard_map/order/pallas_call | solution.py:311
  507.5 5.5 gram_chunk.13
  513.1 5.5 gram_chunk.14
  518.6 5.2 gram_chunk.15
  525.5 66.2 %chain.1.mine = f32[2,64,1024]{2,1,0:T(8,128)S(1)} custom-call(f32[512,1024]{1,0:T(8,128)} %pad_maximum_fusion.1.gram, bf16[8,512,1024]{2,1,0:T(8,128)(2,1)} %get-tuple-element.33.high_table, bf16[8,512,1024]{2,1,0:T(8,128)(2,1)} %get-tuple-element.34.low_table, f32[64,1]{1,0:T(8,128)S(1)} %copy.12.eigen_j, f32[1,1024]{1,0:T(1,128)S(1)} %bitcast.13, ...), custom_call_target="tpu_custom_call" | custom-call | tf_op jit(solution)/shard_map/chain/pallas_call | solution.py:448
  591.8 23.8 %spread.1.z_ref = bf16[1024,3072]{1,0:T(8,128)(2,1)S(1)} custom-call(f32[2,64,1024]{2,1,0:T(8,128)S(1)} %chain.1.mine), custom_call_target="tpu_custom_call" | custom-call | tf_op jit(solution)/shard_map/spread/pallas_call | solution.py:532
  620.5 37.6 %final_chunk.2.rest_6_ = f32[1024,6144]{1,0:T(8,128)} custom-call(bf16[1024,3072]{1,0:T(8,128)(2,1)} %copy-done.2, f32[6144,256]{1,0:T(8,128)} %own.3, f32[1536,256]{1,0:T(8,128)S(1)} %copy-done.7, f32[1536,256]{1,0:T(8,128)} %collective-permute-done.29.refs_5_.rest_1_, f32[1536,256]{1,0:T(8,128)} %collective-permute-done.33.rest_2_, ...), custom_call_target="tpu_custom_call" | custom-call | flops 28991029248 | bytes 37748736 | tf_op jit(solution)/shard_map/final_chunk/pallas_call | solution.py:234
  658.1 15.9 %final_chunk.3 = f32[1024,6144]{1,0:T(8,128)} custom-call(bf16[1024,3072]{1,0:T(8,128)(2,1)} %copy-done.2, f32[6144,256]{1,0:T(8,128)} %own.3, f32[1536,256]{1,0:T(8,128)S(1)} %collective-permute-done.refs_2_.refs_3_.rest_0_, f32[1536,256]{1,0:T(8,128)} %collective-permute-done.9.refs_5_.rest_1_, ...), custom_call_target="tpu_custom_call", output_to_operand_aliasing={{}: (8, {})} | custom-call | flops 9663676416 | bytes 12582912 | tf_op jit(solution)/shard_map/final_chunk/pallas_call | solution.py:234
  (195 shorter events, 125.6 us)
Async XLA Ops:
  5.7 78.6 %collective-permute-start.14 = (f32[1536,256]{1,0:T(8,128)}, f32[1536,256]{1,0:T(8,128)S(1)}, u32[]{:S(2)}, u32[]{:S(2)}) collective-permute-start(f32[1536,256]{1,0:T(8,128)} %get-tuple-element.36), channel_id=1, source_target_pairs={{0,1},{3,2},{4,5},{7,6},{8,9},{11,10},{12,13},{15,14},{16,17},{19,... | collective-permute-start | bytes 4718600 | tf_op jit(solution)/shard_map/ppermute | solution.py:77
  22.9 67.7 %collective-permute-start.6 = (f32[1536,256]{1,0:T(8,128)S(1)}, f32[1536,256]{1,0:T(8,128)S(1)}, u32[]{:S(2)}, u32[]{:S(2)}) collective-permute-start(f32[1536,256]{1,0:T(8,128)S(1)} %slice.18), channel_id=1, source_target_pairs={{0,1},{1,2},{2,3},{4,5},{5,6},{6,7},{8,9},{9,10},{10,11},{12,13},{... | collective-permute-start | bytes 4718600 | tf_op jit(solution)/shard_map/ppermute | solution.py:77
  27.2 67.9 %collective-permute-start.7 = (f32[1536,256]{1,0:T(8,128)S(1)}, f32[1536,256]{1,0:T(8,128)S(1)}, u32[]{:S(2)}, u32[]{:S(2)}) collective-permute-start(f32[1536,256]{1,0:T(8,128)S(1)} %slice.18), channel_id=1, source_target_pairs={{1,0},{2,1},{3,2},{5,4},{6,5},{7,6},{9,8},{10,9},{11,10},{13,12},{... | collective-permute-start | bytes 4718600 | tf_op jit(solution)/shard_map/ppermute | solution.py:77
  80.2 77.8 %collective-permute-start.4 = (f32[1536,256]{1,0:T(8,128)S(1)}, f32[1536,256]{1,0:T(8,128)S(1)}, u32[]{:S(2)}, u32[]{:S(2)}) collective-permute-start(f32[1536,256]{1,0:T(8,128)S(1)} %get-tuple-element.39), channel_id=1, source_target_pairs={{0,1},{1,2},{2,3},{4,5},{5,6},{6,7},{8,9},{9,10},{10,11},{12,13},{... | collective-permute-start | bytes 4718600 | tf_op jit(solution)/shard_map/ppermute | solution.py:77
  85.4 73.8 %collective-permute-start.5 = (f32[1536,256]{1,0:T(8,128)S(1)}, f32[1536,256]{1,0:T(8,128)S(1)}, u32[]{:S(2)}, u32[]{:S(2)}) collective-permute-start(f32[1536,256]{1,0:T(8,128)S(1)} %get-tuple-element.39), channel_id=1, source_target_pairs={{1,0},{2,1},{3,2},{5,4},{6,5},{7,6},{9,8},{10,9},{11,10},{13,12},{... | collective-permute-start | bytes 4718600 | tf_op jit(solution)/shard_map/ppermute | solution.py:77
  90.6 101.1 %collective-permute-start.2 = (f32[1536,256]{1,0:T(8,128)S(1)}, f32[1536,256]{1,0:T(8,128)S(1)}, u32[]{:S(2)}, u32[]{:S(2)}) collective-permute-start(f32[1536,256]{1,0:T(8,128)S(1)} %get-tuple-element.40), channel_id=1, source_target_pairs={{0,1},{1,2},{2,3},{4,5},{5,6},{6,7},{8,9},{9,10},{10,11},{12,13},{... | collective-permute-start | bytes 4718600 | tf_op jit(solution)/shard_map/ppermute | solution.py:77
  95.1 98.1 %collective-permute-start.3 = (f32[1536,256]{1,0:T(8,128)S(1)}, f32[1536,256]{1,0:T(8,128)S(1)}, u32[]{:S(2)}, u32[]{:S(2)}) collective-permute-start(f32[1536,256]{1,0:T(8,128)S(1)} %get-tuple-element.40), channel_id=1, source_target_pairs={{1,0},{2,1},{3,2},{5,4},{6,5},{7,6},{9,8},{10,9},{11,10},{13,12},{... | collective-permute-start | bytes 4718600 | tf_op jit(solution)/shard_map/ppermute | solution.py:77
  125.5 99.9 %collective-permute-start.11 = (f32[1536,256]{1,0:T(8,128)S(1)}, f32[1536,256]{1,0:T(8,128)S(1)}, u32[]{:S(2)}, u32[]{:S(2)}) collective-permute-start(f32[1536,256]{1,0:T(8,128)S(1)} %copy-done.45), channel_id=1, source_target_pairs={{0,1},{3,2},{4,5},{7,6},{8,9},{11,10},{12,13},{15,14},{16,17},{19,... | collective-permute-start | bytes 4718600 | tf_op jit(solution)/shard_map/ppermute | solution.py:77
  158.0 70.1 %collective-permute-start.1 = (f32[1536,256]{1,0:T(8,128)S(1)}, f32[1536,256]{1,0:T(8,128)S(1)}, u32[]{:S(2)}, u32[]{:S(2)}) collective-permute-start(f32[1536,256]{1,0:T(8,128)S(1)} %get-tuple-element.41), channel_id=1, source_target_pairs={{1,0},{2,1},{3,2},{5,4},{6,5},{7,6},{9,8},{10,9},{11,10},{13,12},{... | collective-permute-start | bytes 4718600 | tf_op jit(solution)/shard_map/ppermute | solution.py:77
  159.3 99.8 %collective-permute-start = (f32[1536,256]{1,0:T(8,128)S(1)}, f32[1536,256]{1,0:T(8,128)S(1)}, u32[]{:S(2)}, u32[]{:S(2)}) collective-permute-start(f32[1536,256]{1,0:T(8,128)S(1)} %get-tuple-element.41), channel_id=1, source_target_pairs={{0,1},{1,2},{2,3},{4,5},{5,6},{6,7},{8,9},{9,10},{10,11},{12,13},{... | collective-permute-start | bytes 4718600 | tf_op jit(solution)/shard_map/ppermute | solution.py:77
  191.7 103.0 %collective-permute-start.20 = (f32[512,1024]{1,0:T(8,128)S(1)}, f32[512,1024]{1,0:T(8,128)}, u32[]{:S(2)}, u32[]{:S(2)}) collective-permute-start(f32[512,1024]{1,0:T(8,128)S(1)} %pad_maximum_fusion.refs_0_), channel_id=1, source_target_pairs={{0,8},{4,12},{8,0},{12,4},{16,24},{20,28},{24,16},{28,20},{1,9},{5... | collective-permute-start | bytes 6291464 | tf_op jit(solution)/shard_map/ppermute | solution.py:591
  193.2 98.5 %collective-permute-start.8 = (f32[1536,256]{1,0:T(8,128)S(1)}, f32[1536,256]{1,0:T(8,128)S(1)}, u32[]{:S(2)}, u32[]{:S(2)}) collective-permute-start(f32[1536,256]{1,0:T(8,128)S(1)} %copy-done.44), channel_id=1, source_target_pairs={{0,1},{3,2},{4,5},{7,6},{8,9},{11,10},{12,13},{15,14},{16,17},{19,... | collective-permute-start | bytes 4718600 | tf_op jit(solution)/shard_map/ppermute | solution.py:77
  226.6 90.4 %collective-permute-start.22 = (f32[512,1024]{1,0:T(8,128)S(1)}, f32[512,1024]{1,0:T(8,128)}, u32[]{:S(2)}, u32[]{:S(2)}) collective-permute-start(f32[512,1024]{1,0:T(8,128)S(1)} %pad_maximum_fusion.refs_0_), channel_id=1, source_target_pairs={{0,16},{4,20},{8,24},{12,28},{16,0},{20,4},{24,8},{28,12},{1,17},{... | collective-permute-start | bytes 6291464 | tf_op jit(solution)/shard_map/ppermute | solution.py:591
  228.1 90.7 %collective-permute-start.24 = (f32[512,1024]{1,0:T(8,128)S(1)}, f32[512,1024]{1,0:T(8,128)}, u32[]{:S(2)}, u32[]{:S(2)}) collective-permute-start(f32[512,1024]{1,0:T(8,128)S(1)} %pad_maximum_fusion.refs_0_), channel_id=1, source_target_pairs={{0,24},{4,28},{8,16},{12,20},{16,8},{20,12},{24,0},{28,4},{1,25},{... | collective-permute-start | bytes 6291464 | tf_op jit(solution)/shard_map/ppermute | solution.py:591
  325.7 78.9 %collective-permute-start.13 = (f32[1536,256]{1,0:T(8,128)S(1)}, f32[1536,256]{1,0:T(8,128)}, u32[]{:S(2)}, u32[]{:S(2)}) collective-permute-start(f32[1536,256]{1,0:T(8,128)S(1)} %collective-permute-done.3.refs_3_.refs_4_.rest_15_), channel_id=1, source_target_pairs={{2,1},{1,0},{6,5},{5,4},{10,9},{9,8},{14,13},{13,12},{18,17},{17,1... | collective-permute-start | bytes 4718600 | tf_op jit(solution)/shard_map/ppermute | solution.py:77
  337.2 99.1 %collective-permute-start.10 = (f32[1536,256]{1,0:T(8,128)S(1)}, f32[1536,256]{1,0:T(8,128)S(1)}, u32[]{:S(2)}, u32[]{:S(2)}) collective-permute-start(f32[1536,256]{1,0:T(8,128)S(1)} %collective-permute-done.1.refs_3_.refs_4_.rest_3_), channel_id=1, source_target_pairs={{2,1},{1,0},{6,5},{5,4},{10,9},{9,8},{14,13},{13,12},{18,17},{17,1... | collective-permute-start | bytes 4718600 | tf_op jit(solution)/shard_map/ppermute | solution.py:77
  338.5 118.7 %collective-permute-start.21 = (f32[512,1024]{1,0:T(8,128)}, f32[512,1024]{1,0:T(8,128)}, u32[]{:S(2)}, u32[]{:S(2)}) collective-permute-start(f32[512,1024]{1,0:T(8,128)} %collective-permute-done.20.refs_2_), channel_id=1, source_target_pairs={{0,4},{4,0},{8,12},{12,8},{16,20},{20,16},{24,28},{28,24},{1,5},{5... | collective-permute-start | bytes 6291464 | tf_op jit(solution)/shard_map/ppermute | solution.py:592
  370.9 87.6 %collective-permute-start.23 = (f32[512,1024]{1,0:T(8,128)}, f32[512,1024]{1,0:T(8,128)}, u32[]{:S(2)}, u32[]{:S(2)}) collective-permute-start(f32[512,1024]{1,0:T(8,128)} %collective-permute-done.22.refs_4_), channel_id=1, source_target_pairs={{0,4},{4,0},{8,12},{12,8},{16,20},{20,16},{24,28},{28,24},{1,5},{5... | collective-permute-start | bytes 6291464 | tf_op jit(solution)/shard_map/ppermute | solution.py:592
  370.9 89.4 %collective-permute-start.25 = (f32[512,1024]{1,0:T(8,128)}, f32[512,1024]{1,0:T(8,128)}, u32[]{:S(2)}, u32[]{:S(2)}) collective-permute-start(f32[512,1024]{1,0:T(8,128)} %collective-permute-done.24.refs_6_), channel_id=1, source_target_pairs={{0,4},{4,0},{8,12},{12,8},{16,20},{20,16},{24,28},{28,24},{1,5},{5... | collective-permute-start | bytes 6291464 | tf_op jit(solution)/shard_map/ppermute | solution.py:592
  454.1 164.0 %collective-permute-start.36 = (f32[1536,256]{1,0:T(8,128)}, f32[1536,256]{1,0:T(8,128)}, u32[]{:S(2)}, u32[]{:S(2)}) collective-permute-start(f32[1536,256]{1,0:T(8,128)} %collective-permute-done.27.refs_6_.rest_10_), channel_id=1, source_target_pairs={{1,0},{5,4},{9,8},{13,12},{17,16},{21,20},{25,24},{29,28}} | collective-permute-start | bytes 4718600 | tf_op jit(solution)/shard_map/ppermute | solution.py:77
  455.4 163.5 %collective-permute-start.37 = (f32[1536,256]{1,0:T(8,128)}, f32[1536,256]{1,0:T(8,128)}, u32[]{:S(2)}, u32[]{:S(2)}) collective-permute-start(f32[1536,256]{1,0:T(8,128)} %collective-permute-done.12.refs_5_.rest_13_), channel_id=1, source_target_pairs={{2,3},{6,7},{10,11},{14,15},{18,19},{22,23},{26,27},{30,31}} | collective-permute-start | bytes 4718600 | tf_op jit(solution)/shard_map/ppermute | solution.py:77
  457.2 163.2 %collective-permute-start.38 = (f32[1536,256]{1,0:T(8,128)}, f32[1536,256]{1,0:T(8,128)}, u32[]{:S(2)}, u32[]{:S(2)}) collective-permute-start(f32[1536,256]{1,0:T(8,128)} %collective-permute-done.13.refs_6_.rest_16_), channel_id=1, source_target_pairs={{1,0},{5,4},{9,8},{13,12},{17,16},{21,20},{25,24},{29,28}} | collective-permute-start | bytes 4718600 | tf_op jit(solution)/shard_map/ppermute | solution.py:77
  458.5 161.9 %collective-permute-start.33 = (f32[1536,256]{1,0:T(8,128)}, f32[1536,256]{1,0:T(8,128)}, u32[]{:S(2)}, u32[]{:S(2)}) collective-permute-start(f32[1536,256]{1,0:T(8,128)} %collective-permute-done.29.refs_5_.rest_1_), channel_id=1, source_target_pairs={{2,3},{6,7},{10,11},{14,15},{18,19},{22,23},{26,27},{30,31}} | collective-permute-start | bytes 4718600 | tf_op jit(solution)/shard_map/ppermute | solution.py:77
  460.3 160.1 %collective-permute-start.34 = (f32[1536,256]{1,0:T(8,128)}, f32[1536,256]{1,0:T(8,128)}, u32[]{:S(2)}, u32[]{:S(2)}) collective-permute-start(f32[1536,256]{1,0:T(8,128)} %collective-permute-done.30.refs_6_.rest_4_), channel_id=1, source_target_pairs={{1,0},{5,4},{9,8},{13,12},{17,16},{21,20},{25,24},{29,28}} | collective-permute-start | bytes 4718600 | tf_op jit(solution)/shard_map/ppermute | solution.py:77
  (66 other events, 2034.3 us)

commit v5 on v4

--- a/solution.py
+++ b/solution.py
@@ -11,6 +11,7 @@
 regular = 0.01
 chunks = 4
 tile = 512
+final_tile = 768
 
 
 def product(left, right, left_dim, right_dim):
@@ -83,9 +84,9 @@
     return high, low
 
 
-def final_kernel(first_row, pieces, parts, z_ref, own, *rest):
+def final_kernel(first_row, pieces, parts, z_hbm, own, *rest):
     lists = [rest[6 * c : 6 * c + 6] for c in range(parts)]
-    out_ref, x_buf, x3, sems = rest[-4:]
+    out_ref, x_buf, x3, z_ref, z_sem, sems = rest[-6:]
     step = pl.program_id(0)
     steps = pl.num_programs(0)
     each = steps // parts
@@ -117,6 +118,7 @@
     @pl.when(step == 0)
     def _():
         fetch(step, 0, (0,))
+        pltpu.make_async_copy(z_hbm, z_ref, z_sem).start()
 
     @pl.when(step + 1 < steps)
     def _():
@@ -133,6 +135,11 @@
     x3[:, :depth] = high
     x3[:, depth : 2 * depth] = high
     x3[:, 2 * depth :] = low
+
+    @pl.when(step == 0)
+    def _():
+        pltpu.make_async_copy(z_hbm, z_ref, z_sem).wait()
+
     out_ref[...] = lax.dot_general(
         z_ref[...], x3[...], (((1,), (1,)), ((), ())), preferred_element_type=jnp.float32
     )
@@ -220,33 +227,34 @@
     pieces = z3.shape[1] // (3 * width)
     lists = [v for group in groups for v in group]
     first_row = index * lists[0].shape[0]
-    steps = len(groups) * (lists[0].shape[0] // tile)
+    steps = len(groups) * (lists[0].shape[0] // final_tile)
     anywhere = pl.BlockSpec(memory_space=pl.ANY)
     operands = [z3, own, *lists]
-    specs = [pl.BlockSpec(z3.shape, lambda i: (0, 0), pipeline_mode=pl.Buffered(1))]
-    specs += [anywhere] * (1 + len(lists))
+    specs = [anywhere] * len(operands)
     aliases = {}
     if previous is not None:
         aliases = {len(operands): 0}
         operands.append(previous)
         specs.append(anywhere)
-    first_block = first_row // tile
+    first_block = first_row // final_tile
     return pl.pallas_call(
         functools.partial(final_kernel, first_row, pieces, len(groups)),
         grid=(steps,),
         in_specs=specs,
-        out_specs=pl.BlockSpec((rows, tile), lambda i: (0, first_block + i)),
+        out_specs=pl.BlockSpec((rows, final_tile), lambda i: (0, first_block + i)),
         out_shape=jax.ShapeDtypeStruct((rows, columns), jnp.float32),
         scratch_shapes=[
-            pltpu.VMEM((2, tile, pieces * width), jnp.float32),
-            pltpu.VMEM((tile, 3 * pieces * width), jnp.bfloat16),
+            pltpu.VMEM((2, final_tile, pieces * width), jnp.float32),
+            pltpu.VMEM((final_tile, 3 * pieces * width), jnp.bfloat16),
+            pltpu.VMEM(z3.shape, z3.dtype),
+            pltpu.SemaphoreType.DMA(()),
             pltpu.SemaphoreType.DMA((2, pieces)),
         ],
         input_output_aliases=aliases,
         compiler_params=pltpu.CompilerParams(vmem_limit_bytes=40 * 2**20),
         cost_estimate=pl.CostEstimate(
-            flops=2 * rows * z3.shape[1] * steps * tile,
-            bytes_accessed=4 * steps * tile * (rows + pieces * width),
+            flops=2 * rows * z3.shape[1] * steps * final_tile,
+            bytes_accessed=4 * steps * final_tile * (rows + pieces * width),
             transcendentals=0,
         ),
         name="final_chunk",

time: 676 us -> 677 us (level)
  no operation moved by 1% of the time
where the time goes in v5:
time: 677 us; the launch traced here: 675 us
  waiting for transfers between devices  329 us (49%)
  Pallas kernels  204 us (30%)
  starting transfers between devices  88.9 us (13%)
  local copies, waits for them, and re-layouts  46.5 us (7%)
    ppermute x32, waiting for transfers between devices, shift(): return lax.ppermute(value, 'mode', pairs)  308 us
    ppermute x32, starting transfers between devices, shift(): return lax.ppermute(value, 'mode', pairs)  83.8 us
    pallas_call x1, Pallas kernels, chain(): pl.pallas_call(functools.partial(chain_kernel, chips), in_specs=[vmem] +...  66.2 us
    pallas_call x2, Pallas kernels, final_chunk(): pl.pallas_call(functools.partial(final_kernel, first_row, pieces, len(gro...  54.6 us
    pallas_call x8, Pallas kernels, gram_chunk(): pl.pallas_call(functools.partial(gram_kernel, len(lefts), fresh, plan), g...  32.2 us
    unnamed x102, local copies, waits for them, and re-layouts  30.9 us
    pallas_call x1, Pallas kernels, order(): pl.pallas_call(functools.partial(order_kernel, count), grid_spec=pltpu.Pr...  27.2 us
    pallas_call x1, Pallas kernels, spread(): pl.pallas_call(functools.partial(spread_kernel, width), in_specs=[vmem],...  23.8 us
  transfers between devices with their start and end apart: 39, of which 13 were waited for; matrix products, arithmetic and copies ran while one was open for 2% of the time, Pallas kernels for 28%

profile of v5, /device:TPU:0, one launch (start us, length us, event | category | flops | bytes accessed | tf_op | source)
XLA Modules:
  0.0 675.3 jit_solution(4467056883610993427)
XLA Ops:
  0.0 5.7 fusion.3
  28.5 28.4 %collective-permute-done.15 = f32[512,256]{1,0:T(8,128)S(1)} collective-permute-done((f32[512,256]{1,0:T(8,128)S(1)}, f32[512,256]{1,0:T(8,128)S(1)}, u32[]{:S(2)}, u32[]{:S(2)}) %collective-permute-start.15) | collective-permute-done | bytes 524320 | tf_op jit(solution)/shard_map/ppermute | solution.py:78
  60.9 19.2 %collective-permute-start.28 = (f32[1536,256]{1,0:T(8,128)S(1)}, f32[1536,256]{1,0:T(8,128)S(1)}, u32[]{:S(2)}, u32[]{:S(2)}) collective-permute-start(f32[1536,256]{1,0:T(8,128)S(1)} %copy-done.46), channel_id=1, source_target_pairs={{0,1},{3,2},{4,5},{7,6},{8,9},{11,10},{12,13},{15,14},{16,17},{19,... | collective-permute-start | bytes 4718600 | tf_op jit(solution)/shard_map/ppermute | solution.py:78
  96.4 27.9 %collective-permute-done.28.refs_1_ = f32[1536,256]{1,0:T(8,128)S(1)} collective-permute-done((f32[1536,256]{1,0:T(8,128)S(1)}, f32[1536,256]{1,0:T(8,128)S(1)}, u32[]{:S(2)}, u32[]{:S(2)}) %collective-permute-start.28) | collective-permute-done | bytes 1572896 | tf_op jit(solution)/shard_map/ppermute | solution.py:78
  129.9 28.0 %collective-permute-done.4.refs_2_.refs_3_.rest_6_ = f32[1536,256]{1,0:T(8,128)S(1)} collective-permute-done((f32[1536,256]{1,0:T(8,128)S(1)}, f32[1536,256]{1,0:T(8,128)S(1)}, u32[]{:S(2)}, u32[]{:S(2)}) %collective-permute-start.4) | collective-permute-done | bytes 1572896 | tf_op jit(solution)/shard_map/ppermute | solution.py:78
  159.3 5.1 collective-permute-start
  164.8 26.9 %collective-permute-done.2.refs_2_.refs_3_.rest_12_ = f32[1536,256]{1,0:T(8,128)S(1)} collective-permute-done((f32[1536,256]{1,0:T(8,128)S(1)}, f32[1536,256]{1,0:T(8,128)S(1)}, u32[]{:S(2)}, u32[]{:S(2)}) %collective-permute-start.2) | collective-permute-done | bytes 1572896 | tf_op jit(solution)/shard_map/ppermute | solution.py:78
  197.7 27.7 %collective-permute-done.11.refs_1_ = f32[1536,256]{1,0:T(8,128)S(1)} collective-permute-done((f32[1536,256]{1,0:T(8,128)S(1)}, f32[1536,256]{1,0:T(8,128)S(1)}, u32[]{:S(2)}, u32[]{:S(2)}) %collective-permute-start.11) | collective-permute-done | bytes 1572896 | tf_op jit(solution)/shard_map/ppermute | solution.py:78
  229.5 29.5 %collective-permute-done.refs_2_.refs_3_.rest_0_ = f32[1536,256]{1,0:T(8,128)S(1)} collective-permute-done((f32[1536,256]{1,0:T(8,128)S(1)}, f32[1536,256]{1,0:T(8,128)S(1)}, u32[]{:S(2)}, u32[]{:S(2)}) %collective-permute-start) | collective-permute-done | bytes 1572896 | tf_op jit(solution)/shard_map/ppermute | solution.py:78
  260.4 31.3 %collective-permute-done.8.refs_1_ = f32[1536,256]{1,0:T(8,128)S(1)} collective-permute-done((f32[1536,256]{1,0:T(8,128)S(1)}, f32[1536,256]{1,0:T(8,128)S(1)}, u32[]{:S(2)}, u32[]{:S(2)}) %collective-permute-start.8) | collective-permute-done | bytes 1572896 | tf_op jit(solution)/shard_map/ppermute | solution.py:78
  296.0 21.1 %collective-permute-done.22.refs_4_ = f32[512,1024]{1,0:T(8,128)} collective-permute-done((f32[512,1024]{1,0:T(8,128)S(1)}, f32[512,1024]{1,0:T(8,128)}, u32[]{:S(2)}, u32[]{:S(2)}) %collective-permute-start.22) | collective-permute-done | bytes 2097184 | tf_op jit(solution)/shard_map/ppermute | solution.py:599
  328.1 9.1 %collective-permute-done.30.refs_6_.rest_4_ = f32[1536,256]{1,0:T(8,128)} collective-permute-done((f32[1536,256]{1,0:T(8,128)S(1)}, f32[1536,256]{1,0:T(8,128)}, u32[]{:S(2)}, u32[]{:S(2)}) %collective-permute-start.30) | collective-permute-done | bytes 1572896 | tf_op jit(solution)/shard_map/ppermute | solution.py:78
  338.6 32.3 %collective-permute-done.27.refs_6_.rest_10_ = f32[1536,256]{1,0:T(8,128)} collective-permute-done((f32[1536,256]{1,0:T(8,128)S(1)}, f32[1536,256]{1,0:T(8,128)}, u32[]{:S(2)}, u32[]{:S(2)}) %collective-permute-start.27) | collective-permute-done | bytes 1572896 | tf_op jit(solution)/shard_map/ppermute | solution.py:78
  371.4 33.2 %collective-permute-done.13.refs_6_.rest_16_ = f32[1536,256]{1,0:T(8,128)} collective-permute-done((f32[1536,256]{1,0:T(8,128)S(1)}, f32[1536,256]{1,0:T(8,128)}, u32[]{:S(2)}, u32[]{:S(2)}) %collective-permute-start.13) | collective-permute-done | bytes 1572896 | tf_op jit(solution)/shard_map/ppermute | solution.py:78
  406.5 29.9 %collective-permute-done.10.refs_6_.rest_4_ = f32[1536,256]{1,0:T(8,128)S(1)} collective-permute-done((f32[1536,256]{1,0:T(8,128)S(1)}, f32[1536,256]{1,0:T(8,128)S(1)}, u32[]{:S(2)}, u32[]{:S(2)}) %collective-permute-start.10) | collective-permute-done | bytes 1572896 | tf_op jit(solution)/shard_map/ppermute | solution.py:78
  469.5 5.3 gram_chunk.12
  479.0 27.2 %order.1 = (bf16[8,512,1024]{2,1,0:T(8,128)(2,1)}, bf16[8,512,1024]{2,1,0:T(8,128)(2,1)}) custom-call(s32[4096]{0:T(1024)S(1)} %bitcast_add_fusion.position, f32[512,1024]{1,0:T(8,128)S(1)} %copy-done.4, f32[512,1024]{1,0:T(8,128)S(1)} %copy-done.31, f32[512,1024]{1,0:T(8,128)} %collective-permute-done.20.refs_2_, ...), custom_call_target="tpu_custom_call" | custom-call | bytes 33554432 | tf_op jit(solution)/shard_map/order/pallas_call | solution.py:319
  507.5 5.5 gram_chunk.13
  513.1 5.5 gram_chunk.14
  518.6 5.2 gram_chunk.15
  525.5 66.2 %chain.1.mine = f32[2,64,1024]{2,1,0:T(8,128)S(1)} custom-call(f32[512,1024]{1,0:T(8,128)} %pad_maximum_fusion.1.gram, bf16[8,512,1024]{2,1,0:T(8,128)(2,1)} %get-tuple-element.33.high_table, bf16[8,512,1024]{2,1,0:T(8,128)(2,1)} %get-tuple-element.34.low_table, f32[64,1]{1,0:T(8,128)S(1)} %copy.12.eigen_j, f32[1,1024]{1,0:T(1,128)S(1)} %bitcast.13, ...), custom_call_target="tpu_custom_call" | custom-call | tf_op jit(solution)/shard_map/chain/pallas_call | solution.py:456
  591.8 23.8 %spread.1.z_hbm = bf16[1024,3072]{1,0:T(8,128)(2,1)S(1)} custom-call(f32[2,64,1024]{2,1,0:T(8,128)S(1)} %chain.1.mine), custom_call_target="tpu_custom_call" | custom-call | tf_op jit(solution)/shard_map/spread/pallas_call | solution.py:540
  620.5 38.9 %final_chunk.2.rest_6_ = f32[1024,6144]{1,0:T(8,128)} custom-call(bf16[1024,3072]{1,0:T(8,128)(2,1)} %copy-done.2, f32[6144,256]{1,0:T(8,128)} %own.3, f32[1536,256]{1,0:T(8,128)S(1)} %copy-done.7, f32[1536,256]{1,0:T(8,128)} %collective-permute-done.29.refs_5_.rest_1_, f32[1536,256]{1,0:T(8,128)} %collective-permute-done.33.rest_2_, ...), custom_call_target="tpu_custom_call" | custom-call | flops 28991029248 | bytes 37748736 | tf_op jit(solution)/shard_map/final_chunk/pallas_call | solution.py:240
  659.5 15.7 %final_chunk.3 = f32[1024,6144]{1,0:T(8,128)} custom-call(bf16[1024,3072]{1,0:T(8,128)(2,1)} %copy-done.2, f32[6144,256]{1,0:T(8,128)} %own.3, f32[1536,256]{1,0:T(8,128)S(1)} %collective-permute-done.refs_2_.refs_3_.rest_0_, f32[1536,256]{1,0:T(8,128)} %collective-permute-done.9.refs_5_.rest_1_, ...), custom_call_target="tpu_custom_call", output_to_operand_aliasing={{}: (8, {})} | custom-call | flops 9663676416 | bytes 12582912 | tf_op jit(solution)/shard_map/final_chunk/pallas_call | solution.py:240
  (195 shorter events, 125.6 us)
Async XLA Ops:
  5.7 78.6 %collective-permute-start.14 = (f32[1536,256]{1,0:T(8,128)}, f32[1536,256]{1,0:T(8,128)S(1)}, u32[]{:S(2)}, u32[]{:S(2)}) collective-permute-start(f32[1536,256]{1,0:T(8,128)} %get-tuple-element.36), channel_id=1, source_target_pairs={{0,1},{3,2},{4,5},{7,6},{8,9},{11,10},{12,13},{15,14},{16,17},{19,... | collective-permute-start | bytes 4718600 | tf_op jit(solution)/shard_map/ppermute | solution.py:78
  22.9 67.7 %collective-permute-start.6 = (f32[1536,256]{1,0:T(8,128)S(1)}, f32[1536,256]{1,0:T(8,128)S(1)}, u32[]{:S(2)}, u32[]{:S(2)}) collective-permute-start(f32[1536,256]{1,0:T(8,128)S(1)} %slice.18), channel_id=1, source_target_pairs={{0,1},{1,2},{2,3},{4,5},{5,6},{6,7},{8,9},{9,10},{10,11},{12,13},{... | collective-permute-start | bytes 4718600 | tf_op jit(solution)/shard_map/ppermute | solution.py:78
  27.2 67.9 %collective-permute-start.7 = (f32[1536,256]{1,0:T(8,128)S(1)}, f32[1536,256]{1,0:T(8,128)S(1)}, u32[]{:S(2)}, u32[]{:S(2)}) collective-permute-start(f32[1536,256]{1,0:T(8,128)S(1)} %slice.18), channel_id=1, source_target_pairs={{1,0},{2,1},{3,2},{5,4},{6,5},{7,6},{9,8},{10,9},{11,10},{13,12},{... | collective-permute-start | bytes 4718600 | tf_op jit(solution)/shard_map/ppermute | solution.py:78
  80.2 77.8 %collective-permute-start.4 = (f32[1536,256]{1,0:T(8,128)S(1)}, f32[1536,256]{1,0:T(8,128)S(1)}, u32[]{:S(2)}, u32[]{:S(2)}) collective-permute-start(f32[1536,256]{1,0:T(8,128)S(1)} %get-tuple-element.39), channel_id=1, source_target_pairs={{0,1},{1,2},{2,3},{4,5},{5,6},{6,7},{8,9},{9,10},{10,11},{12,13},{... | collective-permute-start | bytes 4718600 | tf_op jit(solution)/shard_map/ppermute | solution.py:78
  85.4 73.8 %collective-permute-start.5 = (f32[1536,256]{1,0:T(8,128)S(1)}, f32[1536,256]{1,0:T(8,128)S(1)}, u32[]{:S(2)}, u32[]{:S(2)}) collective-permute-start(f32[1536,256]{1,0:T(8,128)S(1)} %get-tuple-element.39), channel_id=1, source_target_pairs={{1,0},{2,1},{3,2},{5,4},{6,5},{7,6},{9,8},{10,9},{11,10},{13,12},{... | collective-permute-start | bytes 4718600 | tf_op jit(solution)/shard_map/ppermute | solution.py:78
  90.6 101.1 %collective-permute-start.2 = (f32[1536,256]{1,0:T(8,128)S(1)}, f32[1536,256]{1,0:T(8,128)S(1)}, u32[]{:S(2)}, u32[]{:S(2)}) collective-permute-start(f32[1536,256]{1,0:T(8,128)S(1)} %get-tuple-element.40), channel_id=1, source_target_pairs={{0,1},{1,2},{2,3},{4,5},{5,6},{6,7},{8,9},{9,10},{10,11},{12,13},{... | collective-permute-start | bytes 4718600 | tf_op jit(solution)/shard_map/ppermute | solution.py:78
  95.1 98.1 %collective-permute-start.3 = (f32[1536,256]{1,0:T(8,128)S(1)}, f32[1536,256]{1,0:T(8,128)S(1)}, u32[]{:S(2)}, u32[]{:S(2)}) collective-permute-start(f32[1536,256]{1,0:T(8,128)S(1)} %get-tuple-element.40), channel_id=1, source_target_pairs={{1,0},{2,1},{3,2},{5,4},{6,5},{7,6},{9,8},{10,9},{11,10},{13,12},{... | collective-permute-start | bytes 4718600 | tf_op jit(solution)/shard_map/ppermute | solution.py:78
  125.5 99.9 %collective-permute-start.11 = (f32[1536,256]{1,0:T(8,128)S(1)}, f32[1536,256]{1,0:T(8,128)S(1)}, u32[]{:S(2)}, u32[]{:S(2)}) collective-permute-start(f32[1536,256]{1,0:T(8,128)S(1)} %copy-done.45), channel_id=1, source_target_pairs={{0,1},{3,2},{4,5},{7,6},{8,9},{11,10},{12,13},{15,14},{16,17},{19,... | collective-permute-start | bytes 4718600 | tf_op jit(solution)/shard_map/ppermute | solution.py:78
  158.0 70.1 %collective-permute-start.1 = (f32[1536,256]{1,0:T(8,128)S(1)}, f32[1536,256]{1,0:T(8,128)S(1)}, u32[]{:S(2)}, u32[]{:S(2)}) collective-permute-start(f32[1536,256]{1,0:T(8,128)S(1)} %get-tuple-element.41), channel_id=1, source_target_pairs={{1,0},{2,1},{3,2},{5,4},{6,5},{7,6},{9,8},{10,9},{11,10},{13,12},{... | collective-permute-start | bytes 4718600 | tf_op jit(solution)/shard_map/ppermute | solution.py:78
  159.3 99.8 %collective-permute-start = (f32[1536,256]{1,0:T(8,128)S(1)}, f32[1536,256]{1,0:T(8,128)S(1)}, u32[]{:S(2)}, u32[]{:S(2)}) collective-permute-start(f32[1536,256]{1,0:T(8,128)S(1)} %get-tuple-element.41), channel_id=1, source_target_pairs={{0,1},{1,2},{2,3},{4,5},{5,6},{6,7},{8,9},{9,10},{10,11},{12,13},{... | collective-permute-start | bytes 4718600 | tf_op jit(solution)/shard_map/ppermute | solution.py:78
  191.7 103.0 %collective-permute-start.20 = (f32[512,1024]{1,0:T(8,128)S(1)}, f32[512,1024]{1,0:T(8,128)}, u32[]{:S(2)}, u32[]{:S(2)}) collective-permute-start(f32[512,1024]{1,0:T(8,128)S(1)} %pad_maximum_fusion.refs_0_), channel_id=1, source_target_pairs={{0,8},{4,12},{8,0},{12,4},{16,24},{20,28},{24,16},{28,20},{1,9},{5... | collective-permute-start | bytes 6291464 | tf_op jit(solution)/shard_map/ppermute | solution.py:599
  193.2 98.5 %collective-permute-start.8 = (f32[1536,256]{1,0:T(8,128)S(1)}, f32[1536,256]{1,0:T(8,128)S(1)}, u32[]{:S(2)}, u32[]{:S(2)}) collective-permute-start(f32[1536,256]{1,0:T(8,128)S(1)} %copy-done.44), channel_id=1, source_target_pairs={{0,1},{3,2},{4,5},{7,6},{8,9},{11,10},{12,13},{15,14},{16,17},{19,... | collective-permute-start | bytes 4718600 | tf_op jit(solution)/shard_map/ppermute | solution.py:78
  226.6 90.4 %collective-permute-start.22 = (f32[512,1024]{1,0:T(8,128)S(1)}, f32[512,1024]{1,0:T(8,128)}, u32[]{:S(2)}, u32[]{:S(2)}) collective-permute-start(f32[512,1024]{1,0:T(8,128)S(1)} %pad_maximum_fusion.refs_0_), channel_id=1, source_target_pairs={{0,16},{4,20},{8,24},{12,28},{16,0},{20,4},{24,8},{28,12},{1,17},{... | collective-permute-start | bytes 6291464 | tf_op jit(solution)/shard_map/ppermute | solution.py:599
  228.1 90.7 %collective-permute-start.24 = (f32[512,1024]{1,0:T(8,128)S(1)}, f32[512,1024]{1,0:T(8,128)}, u32[]{:S(2)}, u32[]{:S(2)}) collective-permute-start(f32[512,1024]{1,0:T(8,128)S(1)} %pad_maximum_fusion.refs_0_), channel_id=1, source_target_pairs={{0,24},{4,28},{8,16},{12,20},{16,8},{20,12},{24,0},{28,4},{1,25},{... | collective-permute-start | bytes 6291464 | tf_op jit(solution)/shard_map/ppermute | solution.py:599
  325.7 78.9 %collective-permute-start.13 = (f32[1536,256]{1,0:T(8,128)S(1)}, f32[1536,256]{1,0:T(8,128)}, u32[]{:S(2)}, u32[]{:S(2)}) collective-permute-start(f32[1536,256]{1,0:T(8,128)S(1)} %collective-permute-done.3.refs_3_.refs_4_.rest_15_), channel_id=1, source_target_pairs={{2,1},{1,0},{6,5},{5,4},{10,9},{9,8},{14,13},{13,12},{18,17},{17,1... | collective-permute-start | bytes 4718600 | tf_op jit(solution)/shard_map/ppermute | solution.py:78
  337.2 99.1 %collective-permute-start.10 = (f32[1536,256]{1,0:T(8,128)S(1)}, f32[1536,256]{1,0:T(8,128)S(1)}, u32[]{:S(2)}, u32[]{:S(2)}) collective-permute-start(f32[1536,256]{1,0:T(8,128)S(1)} %collective-permute-done.1.refs_3_.refs_4_.rest_3_), channel_id=1, source_target_pairs={{2,1},{1,0},{6,5},{5,4},{10,9},{9,8},{14,13},{13,12},{18,17},{17,1... | collective-permute-start | bytes 4718600 | tf_op jit(solution)/shard_map/ppermute | solution.py:78
  338.5 118.7 %collective-permute-start.21 = (f32[512,1024]{1,0:T(8,128)}, f32[512,1024]{1,0:T(8,128)}, u32[]{:S(2)}, u32[]{:S(2)}) collective-permute-start(f32[512,1024]{1,0:T(8,128)} %collective-permute-done.20.refs_2_), channel_id=1, source_target_pairs={{0,4},{4,0},{8,12},{12,8},{16,20},{20,16},{24,28},{28,24},{1,5},{5... | collective-permute-start | bytes 6291464 | tf_op jit(solution)/shard_map/ppermute | solution.py:600
  370.9 87.6 %collective-permute-start.23 = (f32[512,1024]{1,0:T(8,128)}, f32[512,1024]{1,0:T(8,128)}, u32[]{:S(2)}, u32[]{:S(2)}) collective-permute-start(f32[512,1024]{1,0:T(8,128)} %collective-permute-done.22.refs_4_), channel_id=1, source_target_pairs={{0,4},{4,0},{8,12},{12,8},{16,20},{20,16},{24,28},{28,24},{1,5},{5... | collective-permute-start | bytes 6291464 | tf_op jit(solution)/shard_map/ppermute | solution.py:600
  370.9 89.4 %collective-permute-start.25 = (f32[512,1024]{1,0:T(8,128)}, f32[512,1024]{1,0:T(8,128)}, u32[]{:S(2)}, u32[]{:S(2)}) collective-permute-start(f32[512,1024]{1,0:T(8,128)} %collective-permute-done.24.refs_6_), channel_id=1, source_target_pairs={{0,4},{4,0},{8,12},{12,8},{16,20},{20,16},{24,28},{28,24},{1,5},{5... | collective-permute-start | bytes 6291464 | tf_op jit(solution)/shard_map/ppermute | solution.py:600
  454.1 164.0 %collective-permute-start.36 = (f32[1536,256]{1,0:T(8,128)}, f32[1536,256]{1,0:T(8,128)}, u32[]{:S(2)}, u32[]{:S(2)}) collective-permute-start(f32[1536,256]{1,0:T(8,128)} %collective-permute-done.27.refs_6_.rest_10_), channel_id=1, source_target_pairs={{1,0},{5,4},{9,8},{13,12},{17,16},{21,20},{25,24},{29,28}} | collective-permute-start | bytes 4718600 | tf_op jit(solution)/shard_map/ppermute | solution.py:78
  455.4 163.5 %collective-permute-start.37 = (f32[1536,256]{1,0:T(8,128)}, f32[1536,256]{1,0:T(8,128)}, u32[]{:S(2)}, u32[]{:S(2)}) collective-permute-start(f32[1536,256]{1,0:T(8,128)} %collective-permute-done.12.refs_5_.rest_13_), channel_id=1, source_target_pairs={{2,3},{6,7},{10,11},{14,15},{18,19},{22,23},{26,27},{30,31}} | collective-permute-start | bytes 4718600 | tf_op jit(solution)/shard_map/ppermute | solution.py:78
  457.2 163.2 %collective-permute-start.38 = (f32[1536,256]{1,0:T(8,128)}, f32[1536,256]{1,0:T(8,128)}, u32[]{:S(2)}, u32[]{:S(2)}) collective-permute-start(f32[1536,256]{1,0:T(8,128)} %collective-permute-done.13.refs_6_.rest_16_), channel_id=1, source_target_pairs={{1,0},{5,4},{9,8},{13,12},{17,16},{21,20},{25,24},{29,28}} | collective-permute-start | bytes 4718600 | tf_op jit(solution)/shard_map/ppermute | solution.py:78
  458.5 161.9 %collective-permute-start.33 = (f32[1536,256]{1,0:T(8,128)}, f32[1536,256]{1,0:T(8,128)}, u32[]{:S(2)}, u32[]{:S(2)}) collective-permute-start(f32[1536,256]{1,0:T(8,128)} %collective-permute-done.29.refs_5_.rest_1_), channel_id=1, source_target_pairs={{2,3},{6,7},{10,11},{14,15},{18,19},{22,23},{26,27},{30,31}} | collective-permute-start | bytes 4718600 | tf_op jit(solution)/shard_map/ppermute | solution.py:78
  460.3 160.1 %collective-permute-start.34 = (f32[1536,256]{1,0:T(8,128)}, f32[1536,256]{1,0:T(8,128)}, u32[]{:S(2)}, u32[]{:S(2)}) collective-permute-start(f32[1536,256]{1,0:T(8,128)} %collective-permute-done.30.refs_6_.rest_4_), channel_id=1, source_target_pairs={{1,0},{5,4},{9,8},{13,12},{17,16},{21,20},{25,24},{29,28}} | collective-permute-start | bytes 4718600 | tf_op jit(solution)/shard_map/ppermute | solution.py:78
  (66 other events, 2037.0 us)
